TPU v7x, 512 devices: a whole 4x8x8 slice. The times are simulated.
512 devices in a mesh: ctx: 64 (over z, y_hi, core), head: 8 (over x, y_lo).
Axes of the slice: x: 4, y: 8 (y_hi: 4, y_lo: 2; y = y_hi * 2 + y_lo), z: 8, core: 2. Of those that a mesh axis runs over, the one named last changes fastest.
Arguments:
- prompt_latent: bfloat16 [6144, 576], P('ctx'), may hold values from -8 to 8
- prefill_query: bfloat16 [4096, 64, 192], P('ctx', 'head'), may hold values from -12 to 12
- span_start: int32 [1], replicated, may hold values from 0 to 2048
- w_uk: bfloat16 [64, 128, 512], P('head'), may hold values from -0.5 to 0.5
- w_uv: bfloat16 [64, 512, 128], P('head'), may hold values from -0.25 to 0.25
- decode_latent: bfloat16 [256, 256, 576], P(None, 'ctx'), may hold values from -8 to 8
- owner_slot: int32 [256], replicated, may hold values from 0 to 255, each once
- lengths: int32 [256], P('ctx'), may hold values from 1 to 256
- hidden_new: bfloat16 [4, 256, 7168], P(None, 'ctx', 'head'), may hold values from -6 to 6
- decode_query: bfloat16 [4, 256, 64, 192], P(None, 'ctx', 'head'), may hold values from -12 to 12
- w_down: bfloat16 [7168, 576], P('head'), may hold values from -0.0625 to 0.0625
- kv_gain: float32 [512], replicated, may hold values from 0.5 to 1.5
Outputs:
- prefill_out: bfloat16 [4096, 64, 128], P('ctx', 'head')
- decode_out: bfloat16 [4, 256, 64, 128], P(None, 'ctx', 'head')
Inputs may be any that keep to these rules, and one draw needn't show every extreme that they name: span_start + 4096 <= 6144. `owner_slot`: each slot once.
All inputs are finite; a program needn't handle non-finite values.
Results may differ from a plain program's by a relative error of at most 0.014.
Values may be sent and summed in bfloat16 or wider, within the bound.
No kernel may reach another device: no remote copies, remote signals or barrier semaphores. Data moves between devices by JAX's collectives and lax.ppermute only.
A program may use at most 128 MiB of HBM per device.

v0:
```python
import functools

import jax
import jax.numpy as jnp
from jax import lax
from jax.experimental import pallas as pl
from jax.experimental.pallas import tpu as pltpu
from jax.sharding import Mesh
from jax.sharding import PartitionSpec as P


KV_RANK = 512
ROPE = 64
NOPE = 128
LOG2E = 1.4426950408889634
SCALE = (NOPE + ROPE) ** (-0.5)
CTX = ("z", "yh", "c")
HEAD = ("x", "yl")


def split3(v):
    hi = v.astype(jnp.bfloat16)
    rest = v - hi.astype(jnp.float32)
    mid = rest.astype(jnp.bfloat16)
    low = (rest - mid.astype(jnp.float32)).astype(jnp.bfloat16)
    return hi, mid, low


def flash_kernel(offsets, start, *refs):
    count = len(offsets)
    queries, outs = dict(zip(offsets, refs[:count])), dict(zip(offsets, refs[count + 4 :]))
    k1_ref, k2_ref, wuk_ref, wuv_ref = refs[count : count + 4]
    z, yh, c = lax.axis_index("z"), lax.axis_index("yh"), lax.axis_index("c")
    k1 = k1_ref[...].reshape(768, 576)
    k2 = k2_ref[...].reshape(768, 576)
    j = lax.broadcasted_iota(jnp.int32, (1, 768), 1)
    blk = (j * 683) >> 16
    kpos = blk * 768 + (j - blk * 96) + yh * 192
    where1, where2 = kpos + c * 96, kpos + (1 - c) * 96
    scale = SCALE * LOG2E

    def score(k):
        rows = []
        for h in range(8):
            pair = queries[k][h, 64:, :]
            rope = jnp.concatenate([pair[:, :64], pair[:, 64:]], axis=0)
            a = jnp.dot(queries[k][h, :64, :], wuk_ref[h], preferred_element_type=jnp.float32)
            rows.append(jnp.concatenate([a.astype(jnp.bfloat16), rope], axis=1))
        full = jnp.concatenate(rows, axis=0)
        s1 = lax.dot_general(full, k1, NT, preferred_element_type=jnp.float32)
        s2 = lax.dot_general(full, k2, NT, preferred_element_type=jnp.float32)
        return s1, s2

    def weigh(k, s):
        source = (yh + (4 - k)) & 3
        first = start[0] + ((z * 4 + source) * 2 + c) * 64
        qpos = first + (lax.broadcasted_iota(jnp.int32, (512, 1), 0) & 63)
        s1 = jnp.where(where1 <= qpos, s[0], -1e30)
        s2 = jnp.where(where2 <= qpos, s[1], -1e30)
        top = jnp.maximum(jnp.max(s1, axis=1, keepdims=True), jnp.max(s2, axis=1, keepdims=True))
        p1 = jnp.exp2((s1 - top) * scale)
        p2 = jnp.exp2((s2 - top) * scale)
        total = jnp.sum(p1, axis=1, keepdims=True) + jnp.sum(p2, axis=1, keepdims=True)
        lse = top * scale + jnp.log2(total)
        return p1.astype(jnp.bfloat16), p2.astype(jnp.bfloat16), total, lse

    def mix(k, p1, p2, total, lse):
        acc = jnp.dot(p1, k1[:, :KV_RANK], preferred_element_type=jnp.float32)
        acc = acc + jnp.dot(p2, k2[:, :KV_RANK], preferred_element_type=jnp.float32)
        mixed = (acc / total).astype(jnp.bfloat16)
        for h in range(8):
            at = h * 64
            o = jnp.dot(mixed[at : at + 64], wuv_ref[h], preferred_element_type=jnp.float32)
            outs[k][at : at + 64, :] = o.astype(jnp.bfloat16)
        flat = jnp.transpose(jnp.broadcast_to(lse, (512, 128)))[0:1, :]
        lines = jnp.concatenate([flat[:, i * 128 : (i + 1) * 128] for i in range(4)], axis=0)
        hi, mid, low = split3(lines)
        outs[k][512:, :] = jnp.concatenate([hi, mid, low, jnp.zeros_like(hi)], axis=0)

    s = score(offsets[0])
    for n, k in enumerate(offsets):
        following = score(offsets[n + 1]) if n + 1 < count else None
        mix(k, *weigh(k, s))
        s = following


def merge_kernel(a_ref, b_ref, c_ref, d_ref, out_ref):
    parts = [a_ref, b_ref, c_ref, d_ref]
    weights = []
    for ref in parts:
        tail = ref[512:, :].astype(jnp.float32)
        weights.append(tail[0:4] + tail[4:8] + tail[8:12])
    top = jnp.maximum(jnp.maximum(weights[0], weights[1]), jnp.maximum(weights[2], weights[3]))
    weights = [jnp.exp2(w - top) for w in weights]
    inv = 1.0 / (weights[0] + weights[1] + weights[2] + weights[3])
    weights = [w * inv for w in weights]
    merged = []
    for i in range(4):
        total = jnp.zeros((128, 128), jnp.float32)
        for w, ref in zip(weights, parts):
            col = jnp.transpose(jnp.broadcast_to(w[i : i + 1, :], (128, 128)))
            total = total + col * ref[i * 128 : (i + 1) * 128, :].astype(jnp.float32)
        merged.append(total.astype(jnp.bfloat16))
    by_head = jnp.concatenate(merged, axis=0)
    row = lax.broadcasted_iota(jnp.int32, (512, 512), 0)
    col = lax.broadcasted_iota(jnp.int32, (512, 512), 1)
    pick = jnp.where(((row & 7) * 64 + (row >> 3)) == col, 1.0, 0.0).astype(jnp.bfloat16)
    out_ref[...] = jnp.dot(pick, by_head, preferred_element_type=jnp.float32).astype(jnp.bfloat16)


def small(kernel, outs, ins, scalars=0, scratch=(), limit=10, flops=1 << 27):
    vm = pl.BlockSpec(memory_space=pltpu.VMEM)
    sm = pl.BlockSpec(memory_space=pltpu.SMEM)
    return pl.pallas_call(
        kernel,
        out_shape=outs,
        in_specs=[sm] * scalars + [vm] * (len(ins) - scalars),
        out_specs=jax.tree.map(lambda _: vm, outs),
        scratch_shapes=scratch,
        compiler_params=pltpu.CompilerParams(vmem_limit_bytes=limit << 20),
        cost_estimate=pl.CostEstimate(flops=flops, bytes_accessed=1 << 20, transcendentals=1 << 12),
    )(*ins)


def merge(parts):
    return small(merge_kernel, jax.ShapeDtypeStruct((512, 128), jnp.bfloat16), parts)


NT = (((1,), (1,)), ((), ()))


def head_rows(count):
    return lax.broadcasted_iota(jnp.int32, (count, 1), 0) & 7


def prep_kernel(q_ref, wuk_ref, hid_ref, wd_ref, *refs):
    outs, rows = refs[:4], refs[4]
    q = q_ref[...].reshape(128, NOPE + ROPE)
    nope = q[:, :NOPE].astype(jnp.float32)
    head = head_rows(128)
    acc = jnp.zeros((128, KV_RANK), jnp.float32)
    for h in range(8):
        mine = jnp.where(head == h, nope, 0.0).astype(jnp.bfloat16)
        acc = acc + jnp.dot(mine, wuk_ref[h], preferred_element_type=jnp.float32)
    rows[:128, :KV_RANK] = acc
    rows[:128, KV_RANK:] = q[:, NOPE:].astype(jnp.float32)
    hidden = jnp.concatenate([hid_ref[t].astype(jnp.float32) for t in range(4)], axis=0)
    raw = lax.dot_general(
        hidden.astype(jnp.bfloat16), wd_ref[...], NT, preferred_element_type=jnp.float32
    ).astype(jnp.bfloat16)
    o = lax.broadcasted_iota(jnp.int32, (32, 16), 0)
    n = lax.broadcasted_iota(jnp.int32, (32, 16), 1)
    pick = jnp.where(((o & 7) * 4 + (o >> 3) == n) & ((o & 7) < 4), 1.0, 0.0)
    rows[128:, :] = jnp.dot(pick.astype(jnp.bfloat16), raw, preferred_element_type=jnp.float32)
    for k in range(4):
        r = (lax.axis_index("x") + k) & 3
        for s in range(4):
            at = pl.multiple_of((s * 4 + r) * 8, 8)
            outs[k][s * 8 : s * 8 + 8, :] = rows[pl.ds(at, 8), :].astype(jnp.bfloat16)
        at = pl.multiple_of(128 + r * 8, 8)
        outs[k][32:40, :] = rows[pl.ds(at, 8), :].astype(jnp.bfloat16)


def pack_kernel(owner_ref, x_ref, out_ref):
    row = lax.broadcasted_iota(jnp.int32, (512, 256), 0)
    hit = owner_ref[...] == ((row >> 3) * 4 + lax.axis_index("x"))
    acc = jnp.zeros((512, KV_RANK + ROPE), jnp.float32)
    for j in range(4):
        pick = jnp.where(hit & ((row & 7) == j), 1.0, 0.0).astype(jnp.bfloat16)
        acc = acc + lax.dot_general(pick, x_ref[j], NT, preferred_element_type=jnp.float32)
    out_ref[...] = acc.astype(jnp.bfloat16)


def spread_kernel(x_ref, out_ref):
    for i in range(8):
        out_ref[i] = x_ref[...]


def attend_kernel(lengths, p0, p1, p2, p3, raw_a, raw_b, cache_ref, gain_ref, out_ref):
    raw = raw_a[...] + raw_b[...]
    front = raw[:, :KV_RANK]
    factor = lax.rsqrt(jnp.mean(front * front, axis=1, keepdims=True) + 1e-06)
    fresh = jnp.concatenate([front * factor * gain_ref[...], raw[:, KV_RANK:]], axis=1)
    fresh = fresh.astype(jnp.bfloat16)
    q = jnp.concatenate([p[:32, :] for p in (p0, p1, p2, p3)], axis=0)
    cache = cache_ref[...]
    s1 = lax.dot_general(q, cache, NT, preferred_element_type=jnp.float32)
    s2 = lax.dot_general(q, fresh, NT, preferred_element_type=jnp.float32)
    j = lax.broadcasted_iota(jnp.int32, (128, 512), 1)
    held = ((j & 7) < 4) & ((j >> 3) * 4 + (j & 7) < lengths[lax.axis_index("x")])
    s1 = jnp.where(held, s1, -1e30)
    step = (lax.broadcasted_iota(jnp.int32, (128, 8), 0) >> 3) & 3
    s2 = jnp.where(lax.broadcasted_iota(jnp.int32, (128, 8), 1) <= step, s2, -1e30)
    top = jnp.maximum(jnp.max(s1, axis=1, keepdims=True), jnp.max(s2, axis=1, keepdims=True))
    c = SCALE * LOG2E
    p_c = jnp.exp2((s1 - top) * c)
    p_n = jnp.exp2((s2 - top) * c)
    total = jnp.sum(p_c, axis=1, keepdims=True) + jnp.sum(p_n, axis=1, keepdims=True)
    acc = jnp.dot(p_c.astype(jnp.bfloat16), cache[:, :KV_RANK], preferred_element_type=jnp.float32)
    acc = acc + jnp.dot(
        p_n.astype(jnp.bfloat16), fresh[:, :KV_RANK], preferred_element_type=jnp.float32
    )
    mixed = (acc / total).astype(jnp.bfloat16)
    for k in range(4):
        out_ref[(lax.axis_index("x") + (4 - k)) & 3] = mixed[k * 32 : (k + 1) * 32]


def finish_kernel(m_ref, wuv_ref, out_ref):
    m = m_ref[...].reshape(128, KV_RANK).astype(jnp.float32)
    head = head_rows(128)
    acc = jnp.zeros((128, 128), jnp.float32)
    for h in range(8):
        mine = jnp.where(head == h, m, 0.0).astype(jnp.bfloat16)
        acc = acc + jnp.dot(mine, wuv_ref[h], preferred_element_type=jnp.float32)
    for r in range(4):
        for s in range(4):
            at = (r * 4 + s) * 8
            out_ref[s, r] = acc[at : at + 8].astype(jnp.bfloat16)


def shift(v, axis, k, n):
    return lax.ppermute(v, axis, [(i, (i + k) % n) for i in range(n)])


def layer(
    prompt_latent,
    prefill_query,
    span_start,
    w_uk,
    w_uv,
    decode_latent,
    owner_slot,
    lengths,
    hidden_new,
    decode_query,
    w_down,
    kv_gain,
):
    heads_here = w_uk.shape[0]
    queries = prefill_query.shape[0]
    width = prompt_latent.shape[1]
    bf = jnp.bfloat16
    fence = lax.optimization_barrier
    spread = small(spread_kernel, jax.ShapeDtypeStruct((8, 96, width), bf), [prompt_latent])
    keys = lax.all_to_all(spread, "z", 0, 0, tiled=True)

    by_head = jnp.transpose(prefill_query, (1, 0, 2))
    rope = by_head[:, :, NOPE:]
    packed = jnp.concatenate(
        [by_head[:, :, :NOPE], jnp.concatenate([rope[:, :32], rope[:, 32:]], axis=2)], axis=1
    )
    visiting = [packed] + [None] * 3
    for k in (2, 1, 3):
        visiting[k] = shift(packed, "yh", k, 4)
    tile = jax.ShapeDtypeStruct((40, width), bf)
    sent = small(
        prep_kernel,
        [tile] * 4,
        [decode_query, w_uk, hidden_new, w_down.T],
        0,
        [pltpu.VMEM((160, width), jnp.float32)],
    )
    got = [sent[0]] + [None] * 3
    for k in (2, 1, 3):
        got[k] = shift(sent[k], "x", k, 4)
    raw_here = got[0][32:].astype(jnp.float32)
    for k in (1, 2, 3):
        raw_here = raw_here + got[k][32:].astype(jnp.float32)
    rows = small(
        pack_kernel,
        jax.ShapeDtypeStruct((512, width), bf),
        [owner_slot.reshape(1, 256), jnp.transpose(decode_latent, (1, 2, 0))],
    ).reshape(64, 8, width)

    keys, raw_here, rows, *rest = fence((keys, raw_here, rows, *visiting[1:]))
    visiting = [packed] + rest
    raw_there = shift(raw_here, "yl", 1, 2)
    other_keys = shift(keys, "c", 1, 2)
    cache = lax.all_to_all(rows, CTX, 0, 0, tiled=True)

    def flash(offsets, chunks):
        return small(
            functools.partial(flash_kernel, offsets),
            [jax.ShapeDtypeStruct((512 + 16, 128), bf)] * len(offsets),
            [span_start, *chunks, keys, other_keys, w_uk, w_uv],
            1,
            limit=24,
            flops=len(offsets) * 2 * 512 * 1536 * 1100,
        )

    far = (2, 1, 3)
    sending = flash(far, [visiting[k] for k in far])
    cache, *sending = fence((cache, *sending))
    parts = [None] * 4
    for k, piece in zip(far, sending):
        parts[k] = shift(piece, "yh", 4 - k, 4)

    mixed = small(
        attend_kernel,
        jax.ShapeDtypeStruct((4, 32, KV_RANK), bf),
        [
            lengths,
            *got,
            raw_here,
            raw_there,
            cache.reshape(512, width),
            kv_gain.reshape(1, KV_RANK),
        ],
        1,
        limit=16,
    )
    own, mixed = fence((packed, mixed))
    mixed = lax.all_to_all(mixed, "x", 0, 0, tiled=True)
    parts[0] = flash((0,), [own])[0]
    mixed, parts[0] = fence((mixed, parts[0]))
    decode_out = small(finish_kernel, jax.ShapeDtypeStruct((4, 4, 8, 128), bf), [mixed, w_uv])
    prefill_out = merge(parts).reshape(queries, heads_here, 128)
    return (prefill_out, decode_out)


def solution(mesh):
    fine = Mesh(mesh.devices.reshape(8, 4, 2, 4, 2), ("z", "yh", "c", "x", "yl"))
    in_specs = (
        P(CTX, None),
        P(CTX, HEAD, None),
        P(),
        P(HEAD, None, None),
        P(HEAD, None, None),
        P(None, CTX, None),
        P(),
        P(CTX),
        P(None, CTX, HEAD),
        P(None, CTX, HEAD, None),
        P(HEAD, None),
        P(),
    )
    out_specs = (P(CTX, HEAD, None), P(None, CTX, HEAD, None))
    return jax.shard_map(layer, mesh=fine, in_specs=in_specs, out_specs=out_specs, check_vma=False)
```

profile of v0, /device:TPU:10, one launch (start us, length us, event | category | flops | bytes accessed | tf_op | source)
XLA Modules:
  0.0 119.4 jit_solution(17547829102393808546)
XLA Ops:
  0.6 0.9 copy-done.4
  1.5 1.0 shard_map.132
  2.6 10.4 %all-to-all-start = ((bf16[8,96,576]{2,1,0:T(8,128)(2,1)}), bf16[8,96,576]{2,1,0:T(8,128)(2,1)}, u32[]{:S(2)}, u32[]{:S(2)}) async-start(bf16[8,96,576]{2,1,0:T(8,128)(2,1)} %shard_map.132), calls=%async_computation | async-start | bytes 1966080 | tf_op jit(solution)/shard_map/all_to_all | solution.py:245
  13.0 0.8 shard_map.131
  13.9 3.5 %collective-permute-start = (bf16[40,576]{1,0:T(8,128)(2,1)S(1)}, bf16[40,576]{1,0:T(8,128)(2,1)S(1)}, u32[]{:S(2)}, u32[]{:S(2)}) collective-permute-start(bf16[40,576]{1,0:T(8,128)(2,1)S(1)} %get-tuple-element.24), channel_id=1, source_target_pairs={{0,2},{2,4},{4,6},{6,0},{1,3},{3,5},{5,7},{7,1},{8,10},{10,12},{12... | collective-permute-start | bytes 138248 | tf_op jit(solution)/shard_map/ppermute | solution.py:222
  17.4 3.0 %collective-permute-start.1 = (bf16[40,576]{1,0:T(8,128)(2,1)S(1)}, bf16[40,576]{1,0:T(8,128)(2,1)S(1)}, u32[]{:S(2)}, u32[]{:S(2)}) collective-permute-start(bf16[40,576]{1,0:T(8,128)(2,1)S(1)} %get-tuple-element.25), channel_id=1, source_target_pairs={{0,4},{2,6},{4,0},{6,2},{1,5},{3,7},{5,1},{7,3},{8,12},{10,14},{12... | collective-permute-start | bytes 138248 | tf_op jit(solution)/shard_map/ppermute | solution.py:222
  20.5 4.1 %collective-permute-start.2 = (bf16[40,576]{1,0:T(8,128)(2,1)S(1)}, bf16[40,576]{1,0:T(8,128)(2,1)S(1)}, u32[]{:S(2)}, u32[]{:S(2)}) collective-permute-start(bf16[40,576]{1,0:T(8,128)(2,1)S(1)} %get-tuple-element.26), channel_id=1, source_target_pairs={{0,6},{2,0},{4,2},{6,4},{1,7},{3,1},{5,3},{7,5},{8,14},{10,8},{12,... | collective-permute-start | bytes 138248 | tf_op jit(solution)/shard_map/ppermute | solution.py:222
  24.8 5.3 %collective-permute-start.5 = (bf16[8,96,128]{2,1,0:T(8,128)(2,1)S(1)}, bf16[8,96,128]{2,1,0:T(8,128)(2,1)S(1)}, u32[]{:S(2)}, u32[]{:S(2)}) collective-permute-start(bf16[8,96,128]{2,1,0:T(8,128)(2,1)S(1)} %maximum_maximum_fusion.refs_0_), channel_id=1, source_target_pairs={{0,48},{16,0},{32,16},{48,32},{1,49},{17,1},{33,17},{49,33},{2,50}... | collective-permute-start | bytes 589832 | tf_op jit(solution)/shard_map/ppermute | solution.py:222
  30.0 4.7 %collective-permute-start.4 = (bf16[8,96,128]{2,1,0:T(8,128)(2,1)S(1)}, bf16[8,96,128]{2,1,0:T(8,128)(2,1)S(1)}, u32[]{:S(2)}, u32[]{:S(2)}) collective-permute-start(bf16[8,96,128]{2,1,0:T(8,128)(2,1)S(1)} %maximum_maximum_fusion.refs_0_), channel_id=1, source_target_pairs={{0,32},{16,48},{32,0},{48,16},{1,33},{17,49},{33,1},{49,17},{2,34}... | collective-permute-start | bytes 589832 | tf_op jit(solution)/shard_map/ppermute | solution.py:222
  34.8 1.8 %shard_map.133 = bf16[512,576]{1,0:T(8,128)(2,1)} custom-call(s32[1,256]{1,0:T(1,128)S(1)} %bitcast.14, bf16[4,576,256]{2,1,0:T(8,128)(2,1)S(1)} %bitcast.11), custom_call_target="tpu_custom_call" | custom-call | flops 134217728 | bytes 1048576 | tf_op jit(solution)/shard_map/pallas_call | solution.py:114
  36.6 3.6 %collective-permute-start.3 = (bf16[8,96,128]{2,1,0:T(8,128)(2,1)S(1)}, bf16[8,96,128]{2,1,0:T(8,128)(2,1)S(1)}, u32[]{:S(2)}, u32[]{:S(2)}) collective-permute-start(bf16[8,96,128]{2,1,0:T(8,128)(2,1)S(1)} %maximum_maximum_fusion.refs_0_), channel_id=1, source_target_pairs={{0,16},{16,32},{32,48},{48,0},{1,17},{17,33},{33,49},{49,1},{2,18}... | collective-permute-start | bytes 589832 | tf_op jit(solution)/shard_map/ppermute | solution.py:222
  40.3 8.7 %collective-permute-done.4.refs_0_ = bf16[8,96,128]{2,1,0:T(8,128)(2,1)S(1)} collective-permute-done((bf16[8,96,128]{2,1,0:T(8,128)(2,1)S(1)}, bf16[8,96,128]{2,1,0:T(8,128)(2,1)S(1)}, u32[]{:S(2)}, u32[]{:S(2)}) %collective-permute-start.4) | collective-permute-done | bytes 196640 | tf_op jit(solution)/shard_map/ppermute | solution.py:222
  49.0 0.7 copy-done.10
  49.7 2.6 %collective-permute-done.3.refs_1_ = bf16[8,96,128]{2,1,0:T(8,128)(2,1)S(1)} collective-permute-done((bf16[8,96,128]{2,1,0:T(8,128)(2,1)S(1)}, bf16[8,96,128]{2,1,0:T(8,128)(2,1)S(1)}, u32[]{:S(2)}, u32[]{:S(2)}) %collective-permute-start.3) | collective-permute-done | bytes 196640 | tf_op jit(solution)/shard_map/ppermute | solution.py:222
  52.2 0.7 copy-done.12
  52.9 1.9 %collective-permute-start.7 = (bf16[8,96,576]{2,1,0:T(8,128)(2,1)}, bf16[8,96,576]{2,1,0:T(8,128)(2,1)}, u32[]{:S(2)}, u32[]{:S(2)}) collective-permute-start(bf16[8,96,576]{2,1,0:T(8,128)(2,1)} %all-to-all-done.refs_3_.refs_1_), channel_id=1, source_target_pairs={{0,8},{8,0},{1,9},{9,1},{2,10},{10,2},{3,11},{11,3},{4,12},{12,4},... | collective-permute-start | bytes 2654216 | tf_op jit(solution)/shard_map/ppermute | solution.py:222
  54.8 11.6 %all-to-all-start.1 = ((bf16[64,8,576]{2,1,0:T(8,128)(2,1)}), bf16[64,8,576]{2,1,0:T(8,128)(2,1)S(1)}, u32[]{:S(2)}, u32[]{:S(2)}) async-start(bf16[64,8,576]{2,1,0:T(8,128)(2,1)} %bitcast.4), calls=%async_computation.1 | async-start | bytes 1310720 | tf_op jit(solution)/shard_map/all_to_all | solution.py:279
  67.1 2.9 %collective-permute-start.6 = (f32[8,576]{1,0:T(8,128)S(1)}, f32[8,576]{1,0:T(8,128)S(1)}, u32[]{:S(2)}, u32[]{:S(2)}) collective-permute-start(f32[8,576]{1,0:T(8,128)S(1)} %convert_add_fusion.raw_a), channel_id=1, source_target_pairs={{0,1},{1,0},{2,3},{3,2},{4,5},{5,4},{6,7},{7,6},{8,9},{9,8},{10,11... | collective-permute-start | bytes 55304 | tf_op jit(solution)/shard_map/ppermute | solution.py:222
  70.1 0.9 copy-done.11
  71.0 0.9 copy-done.13
  71.9 9.6 %shard_map.134 = (bf16[528,128]{1,0:T(8,128)(2,1)S(1)}, bf16[528,128]{1,0:T(8,128)(2,1)S(1)}, bf16[528,128]{1,0:T(8,128)(2,1)S(1)}) custom-call(s32[1]{0:T(128)S(6)} %copy.17.start, bf16[8,96,128]{2,1,0:T(8,128)(2,1)S(1)} %copy-done.11, bf16[8,96,128]{2,1,0:T(8,128)(2,1)S(1)} %copy-done.13, bf16[8,96,128]{2,1,0:T(8,128)(2,1)S(1)} %collective-permute-done.5.refs_2_, ...), custom_call_target="tpu_custom_call" | custom-call | flops 5190451200 | bytes 1048576 | tf_op jit(solution)/shard_map/pallas_call | solution.py:114
  82.9 7.2 %all-to-all-done.1 = bf16[64,8,576]{2,1,0:T(8,128)(2,1)S(1)} async-done(((bf16[64,8,576]{2,1,0:T(8,128)(2,1)}), bf16[64,8,576]{2,1,0:T(8,128)(2,1)S(1)}, u32[]{:S(2)}, u32[]{:S(2)}) %all-to-all-start.1) | async-done | bytes 589856 | tf_op jit(solution)/shard_map/all_to_all | solution.py:279
  90.1 2.1 %shard_map.135 = bf16[4,32,512]{2,1,0:T(8,128)(2,1)} custom-call(s32[4]{0:T(128)S(1)} %copy-done.9, bf16[40,576]{1,0:T(8,128)(2,1)S(1)} %get-tuple-element.23.p0, bf16[40,576]{1,0:T(8,128)(2,1)S(1)} %collective-permute-done.p1, bf16[40,576]{1,0:T(8,128)(2,1)S(1)} %collective-permute-done.1.p2, bf16[40,576]{1,0:T(8,128)(2,1)S(1)} %collective-permute-done.2.p3, ...), custom_call_target="tpu_custom_call" | custom-call | flops 134217728 | bytes 1048576 | tf_op jit(solution)/shard_map/pallas_call | solution.py:114
  92.1 4.7 %all-to-all-start.2 = ((bf16[4,32,512]{2,1,0:T(8,128)(2,1)}), bf16[4,32,512]{2,1,0:T(8,128)(2,1)S(1)}, u32[]{:S(2)}, u32[]{:S(2)}) async-start(bf16[4,32,512]{2,1,0:T(8,128)(2,1)} %shard_map.135), calls=%async_computation.2 | async-start | bytes 262144 | tf_op jit(solution)/shard_map/all_to_all | solution.py:313
  96.9 1.9 %collective-permute-start.8 = (bf16[528,128]{1,0:T(8,128)(2,1)}, bf16[528,128]{1,0:T(8,128)(2,1)S(1)}, u32[]{:S(2)}, u32[]{:S(2)}) collective-permute-start(bf16[528,128]{1,0:T(8,128)(2,1)} %copy-done.16), channel_id=1, source_target_pairs={{0,48},{16,0},{32,16},{48,32},{1,49},{17,1},{33,17},{49,33},{2,50}... | collective-permute-start | bytes 405512 | tf_op jit(solution)/shard_map/ppermute | solution.py:222
  98.8 6.0 %collective-permute-start.9 = (bf16[528,128]{1,0:T(8,128)(2,1)S(1)}, bf16[528,128]{1,0:T(8,128)(2,1)S(1)}, u32[]{:S(2)}, u32[]{:S(2)}) collective-permute-start(bf16[528,128]{1,0:T(8,128)(2,1)S(1)} %copy-done.15), channel_id=1, source_target_pairs={{0,32},{16,48},{32,0},{48,16},{1,33},{17,49},{33,1},{49,17},{2,34}... | collective-permute-start | bytes 405512 | tf_op jit(solution)/shard_map/ppermute | solution.py:222
  104.8 3.1 %collective-permute-start.10 = (bf16[528,128]{1,0:T(8,128)(2,1)S(1)}, bf16[528,128]{1,0:T(8,128)(2,1)S(1)}, u32[]{:S(2)}, u32[]{:S(2)}) collective-permute-start(bf16[528,128]{1,0:T(8,128)(2,1)S(1)} %get-tuple-element.42), channel_id=1, source_target_pairs={{0,16},{16,32},{32,48},{48,0},{1,17},{17,33},{33,49},{49,1},{2,18}... | collective-permute-start | bytes 405512 | tf_op jit(solution)/shard_map/ppermute | solution.py:222
  107.9 4.5 %shard_map.136.a_ref = bf16[528,128]{1,0:T(8,128)(2,1)S(1)} custom-call(s32[1]{0:T(128)S(6)} %copy.17.start, bf16[8,96,128]{2,1,0:T(8,128)(2,1)S(1)} %maximum_maximum_fusion.refs_0_, bf16[8,96,576]{2,1,0:T(8,128)(2,1)} %all-to-all-done.refs_3_.refs_1_, bf16[8,96,576]{2,1,0:T(8,128)(2,1)} %collective-permute-done.7.refs_4_.refs_2_, ...), custom_call_target="tpu_custom_call" | custom-call | flops 1730150400 | bytes 1048576 | tf_op jit(solution)/shard_map/pallas_call | solution.py:114
  112.5 1.0 shard_map.138
  113.6 1.7 %collective-permute-done.9.c_ref = bf16[528,128]{1,0:T(8,128)(2,1)S(1)} collective-permute-done((bf16[528,128]{1,0:T(8,128)(2,1)S(1)}, bf16[528,128]{1,0:T(8,128)(2,1)S(1)}, u32[]{:S(2)}, u32[]{:S(2)}) %collective-permute-start.9) | collective-permute-done | bytes 135200 | tf_op jit(solution)/shard_map/ppermute | solution.py:222
  115.3 2.9 %collective-permute-done.10.d_ref = bf16[528,128]{1,0:T(8,128)(2,1)S(1)} collective-permute-done((bf16[528,128]{1,0:T(8,128)(2,1)S(1)}, bf16[528,128]{1,0:T(8,128)(2,1)S(1)}, u32[]{:S(2)}, u32[]{:S(2)}) %collective-permute-start.10) | collective-permute-done | bytes 135200 | tf_op jit(solution)/shard_map/ppermute | solution.py:222
  118.1 1.3 %shard_map.137 = bf16[512,128]{1,0:T(8,128)(2,1)} custom-call(bf16[528,128]{1,0:T(8,128)(2,1)S(1)} %shard_map.136.a_ref, bf16[528,128]{1,0:T(8,128)(2,1)S(1)} %collective-permute-done.8.b_ref, bf16[528,128]{1,0:T(8,128)(2,1)S(1)} %collective-permute-done.9.c_ref, bf16[528,128]{1,0:T(8,128)(2,1)S(1)} %collective-permute-done.10.d_ref), custom_call_target="tpu_custom_call" | custom-call | flops 134217728 | bytes 1048576 | tf_op jit(solution)/shard_map/pallas_call | solution.py:114
  (45 shorter events, 1.6 us)
Async XLA Ops:
  0.6 0.9 copy-start.4
  1.5 11.5 %copy-start.3 = (bf16[896,576]{0,1:T(8,128)(2,1)S(1)}, bf16[896,576]{0,1:T(8,128)(2,1)}, u32[]{:S(2)}) copy-start(bf16[896,576]{0,1:T(8,128)(2,1)} %param.22) | copy-start | bytes 3096580
  2.5 10.5 %copy-start.2 = (bf16[8,128,512]{2,1,0:T(8,128)(2,1)S(1)}, bf16[8,128,512]{2,1,0:T(8,128)(2,1)}, u32[]{:S(2)}) copy-start(bf16[8,128,512]{2,1,0:T(8,128)(2,1)} %refs_3_.1) | copy-start | bytes 3145732
  2.5 10.5 %copy-start.5 = (bf16[4,4,8,192]{3,2,1,0:T(8,128)(2,1)S(1)}, bf16[4,4,8,192]{3,2,1,0:T(8,128)(2,1)}, u32[]{:S(2)}) copy-start(bf16[4,4,8,192]{3,2,1,0:T(8,128)(2,1)} %q_ref.1) | copy-start | bytes 147460
  2.5 10.5 %copy-start.6 = (bf16[4,4,896]{2,1,0:T(4,128)(2,1)S(1)}, bf16[4,4,896]{2,1,0:T(4,128)(2,1)}, u32[]{:S(2)}) copy-start(bf16[4,4,896]{2,1,0:T(4,128)(2,1)} %hid_ref.1) | copy-start | bytes 86020
  2.6 50.4 %all-to-all-start = ((bf16[8,96,576]{2,1,0:T(8,128)(2,1)}), bf16[8,96,576]{2,1,0:T(8,128)(2,1)}, u32[]{:S(2)}, u32[]{:S(2)}) async-start(bf16[8,96,576]{2,1,0:T(8,128)(2,1)} %shard_map.132), calls=%async_computation | async-start | bytes 1966080 | tf_op jit(solution)/shard_map/all_to_all | solution.py:245
  13.0 11.5 %copy-start.17 = (bf16[64,8,192]{2,1,0:T(8,128)(2,1)S(1)}, bf16[64,8,192]{2,1,0:T(8,128)(2,1)}, u32[]{:S(2)}) copy-start(bf16[64,8,192]{2,1,0:T(8,128)(2,1)} %param.13) | copy-start | bytes 589828
  13.9 20.9 %copy-start = (bf16[256,4,576]{0,2,1:T(8,128)(2,1)S(1)}, bf16[256,4,576]{0,2,1:T(8,128)(2,1)}, u32[]{:S(2)}) copy-start(bf16[256,4,576]{0,2,1:T(8,128)(2,1)} %param.17) | copy-start | bytes 3538948
  13.9 20.9 %copy-start.8 = (s32[256]{0:T(256)S(1)}, s32[256]{0:T(256)}, u32[]{:S(2)}) copy-start(s32[256]{0:T(256)} %param.18) | copy-start | bytes 3076
  13.9 22.7 %collective-permute-start = (bf16[40,576]{1,0:T(8,128)(2,1)S(1)}, bf16[40,576]{1,0:T(8,128)(2,1)S(1)}, u32[]{:S(2)}, u32[]{:S(2)}) collective-permute-start(bf16[40,576]{1,0:T(8,128)(2,1)S(1)} %get-tuple-element.24), channel_id=1, source_target_pairs={{0,2},{2,4},{4,6},{6,0},{1,3},{3,5},{5,7},{7,1},{8,10},{10,12},{12... | collective-permute-start | bytes 138248 | tf_op jit(solution)/shard_map/ppermute | solution.py:222
  17.4 22.8 %collective-permute-start.1 = (bf16[40,576]{1,0:T(8,128)(2,1)S(1)}, bf16[40,576]{1,0:T(8,128)(2,1)S(1)}, u32[]{:S(2)}, u32[]{:S(2)}) collective-permute-start(bf16[40,576]{1,0:T(8,128)(2,1)S(1)} %get-tuple-element.25), channel_id=1, source_target_pairs={{0,4},{2,6},{4,0},{6,2},{1,5},{3,7},{5,1},{7,3},{8,12},{10,14},{12... | collective-permute-start | bytes 138248 | tf_op jit(solution)/shard_map/ppermute | solution.py:222
  20.5 19.8 %collective-permute-start.2 = (bf16[40,576]{1,0:T(8,128)(2,1)S(1)}, bf16[40,576]{1,0:T(8,128)(2,1)S(1)}, u32[]{:S(2)}, u32[]{:S(2)}) collective-permute-start(bf16[40,576]{1,0:T(8,128)(2,1)S(1)} %get-tuple-element.26), channel_id=1, source_target_pairs={{0,6},{2,0},{4,2},{6,4},{1,7},{3,1},{5,3},{7,5},{8,14},{10,8},{12,... | collective-permute-start | bytes 138248 | tf_op jit(solution)/shard_map/ppermute | solution.py:222
  24.8 15.5 %collective-permute-start.5 = (bf16[8,96,128]{2,1,0:T(8,128)(2,1)S(1)}, bf16[8,96,128]{2,1,0:T(8,128)(2,1)S(1)}, u32[]{:S(2)}, u32[]{:S(2)}) collective-permute-start(bf16[8,96,128]{2,1,0:T(8,128)(2,1)S(1)} %maximum_maximum_fusion.refs_0_), channel_id=1, source_target_pairs={{0,48},{16,0},{32,16},{48,32},{1,49},{17,1},{33,17},{49,33},{2,50}... | collective-permute-start | bytes 589832 | tf_op jit(solution)/shard_map/ppermute | solution.py:222
  30.0 19.0 %collective-permute-start.4 = (bf16[8,96,128]{2,1,0:T(8,128)(2,1)S(1)}, bf16[8,96,128]{2,1,0:T(8,128)(2,1)S(1)}, u32[]{:S(2)}, u32[]{:S(2)}) collective-permute-start(bf16[8,96,128]{2,1,0:T(8,128)(2,1)S(1)} %maximum_maximum_fusion.refs_0_), channel_id=1, source_target_pairs={{0,32},{16,48},{32,0},{48,16},{1,33},{17,49},{33,1},{49,17},{2,34}... | collective-permute-start | bytes 589832 | tf_op jit(solution)/shard_map/ppermute | solution.py:222
  34.8 35.3 %copy-start.1 = (bf16[8,512,128]{2,1,0:T(8,128)(2,1)S(1)}, bf16[8,512,128]{2,1,0:T(8,128)(2,1)}, u32[]{:S(2)}) copy-start(bf16[8,512,128]{2,1,0:T(8,128)(2,1)} %wuv_ref.1) | copy-start | bytes 3145732
  36.6 15.6 %collective-permute-start.3 = (bf16[8,96,128]{2,1,0:T(8,128)(2,1)S(1)}, bf16[8,96,128]{2,1,0:T(8,128)(2,1)S(1)}, u32[]{:S(2)}, u32[]{:S(2)}) collective-permute-start(bf16[8,96,128]{2,1,0:T(8,128)(2,1)S(1)} %maximum_maximum_fusion.refs_0_), channel_id=1, source_target_pairs={{0,16},{16,32},{32,48},{48,0},{1,17},{17,33},{33,49},{49,1},{2,18}... | collective-permute-start | bytes 589832 | tf_op jit(solution)/shard_map/ppermute | solution.py:222
  49.0 0.7 copy-start.10
  52.2 0.7 copy-start.12
  52.9 17.1 %collective-permute-start.7 = (bf16[8,96,576]{2,1,0:T(8,128)(2,1)}, bf16[8,96,576]{2,1,0:T(8,128)(2,1)}, u32[]{:S(2)}, u32[]{:S(2)}) collective-permute-start(bf16[8,96,576]{2,1,0:T(8,128)(2,1)} %all-to-all-done.refs_3_.refs_1_), channel_id=1, source_target_pairs={{0,8},{8,0},{1,9},{9,1},{2,10},{10,2},{3,11},{11,3},{4,12},{12,4},... | collective-permute-start | bytes 2654216 | tf_op jit(solution)/shard_map/ppermute | solution.py:222
  54.8 35.2 %all-to-all-start.1 = ((bf16[64,8,576]{2,1,0:T(8,128)(2,1)}), bf16[64,8,576]{2,1,0:T(8,128)(2,1)S(1)}, u32[]{:S(2)}, u32[]{:S(2)}) async-start(bf16[64,8,576]{2,1,0:T(8,128)(2,1)} %bitcast.4), calls=%async_computation.1 | async-start | bytes 1310720 | tf_op jit(solution)/shard_map/all_to_all | solution.py:279
  67.1 23.0 %copy-start.7 = (f32[512]{0:T(512)S(1)}, f32[512]{0:T(512)}, u32[]{:S(2)}) copy-start(f32[512]{0:T(512)} %param.23) | copy-start | bytes 6148
  67.1 23.0 %copy-start.9 = (s32[4]{0:T(128)S(1)}, s32[4]{0:T(128)}, u32[]{:S(2)}) copy-start(s32[4]{0:T(128)} %lengths.1) | copy-start | bytes 52
  67.1 22.9 %collective-permute-start.6 = (f32[8,576]{1,0:T(8,128)S(1)}, f32[8,576]{1,0:T(8,128)S(1)}, u32[]{:S(2)}, u32[]{:S(2)}) collective-permute-start(f32[8,576]{1,0:T(8,128)S(1)} %convert_add_fusion.raw_a), channel_id=1, source_target_pairs={{0,1},{1,0},{2,3},{3,2},{4,5},{5,4},{6,7},{7,6},{8,9},{9,8},{10,11... | collective-permute-start | bytes 55304 | tf_op jit(solution)/shard_map/ppermute | solution.py:222
  70.1 0.9 copy-start.11
  71.0 0.9 copy-start.13
  81.6 0.7 copy-start.14
  82.2 0.7 copy-start.16
  90.1 8.7 %copy-start.15 = (bf16[528,128]{1,0:T(8,128)(2,1)S(1)}, bf16[528,128]{1,0:T(8,128)(2,1)}, u32[]{:S(2)}) copy-start(bf16[528,128]{1,0:T(8,128)(2,1)} %copy-done.14) | copy-start | bytes 405508
  92.1 20.4 %all-to-all-start.2 = ((bf16[4,32,512]{2,1,0:T(8,128)(2,1)}), bf16[4,32,512]{2,1,0:T(8,128)(2,1)S(1)}, u32[]{:S(2)}, u32[]{:S(2)}) async-start(bf16[4,32,512]{2,1,0:T(8,128)(2,1)} %shard_map.135), calls=%async_computation.2 | async-start | bytes 262144 | tf_op jit(solution)/shard_map/all_to_all | solution.py:313
  96.9 16.7 %collective-permute-start.8 = (bf16[528,128]{1,0:T(8,128)(2,1)}, bf16[528,128]{1,0:T(8,128)(2,1)S(1)}, u32[]{:S(2)}, u32[]{:S(2)}) collective-permute-start(bf16[528,128]{1,0:T(8,128)(2,1)} %copy-done.16), channel_id=1, source_target_pairs={{0,48},{16,0},{32,16},{48,32},{1,49},{17,1},{33,17},{49,33},{2,50}... | collective-permute-start | bytes 405512 | tf_op jit(solution)/shard_map/ppermute | solution.py:222
  98.8 16.5 %collective-permute-start.9 = (bf16[528,128]{1,0:T(8,128)(2,1)S(1)}, bf16[528,128]{1,0:T(8,128)(2,1)S(1)}, u32[]{:S(2)}, u32[]{:S(2)}) collective-permute-start(bf16[528,128]{1,0:T(8,128)(2,1)S(1)} %copy-done.15), channel_id=1, source_target_pairs={{0,32},{16,48},{32,0},{48,16},{1,33},{17,49},{33,1},{49,17},{2,34}... | collective-permute-start | bytes 405512 | tf_op jit(solution)/shard_map/ppermute | solution.py:222
  104.8 13.3 %collective-permute-start.10 = (bf16[528,128]{1,0:T(8,128)(2,1)S(1)}, bf16[528,128]{1,0:T(8,128)(2,1)S(1)}, u32[]{:S(2)}, u32[]{:S(2)}) collective-permute-start(bf16[528,128]{1,0:T(8,128)(2,1)S(1)} %get-tuple-element.42), channel_id=1, source_target_pairs={{0,16},{16,32},{32,48},{48,0},{1,17},{17,33},{33,49},{49,1},{2,18}... | collective-permute-start | bytes 405512 | tf_op jit(solution)/shard_map/ppermute | solution.py:222
where the time goes:
time: 120 us; the launch traced here: 119 us
  starting transfers between devices  66.8 us (56%)
  waiting for transfers between devices  23.1 us (19%)
  Pallas kernels  22.2 us (18%)
  local copies, waits for them, and re-layouts  5.56 us (5%)
  between operations  1.62 us (1%)
    ppermute x11, starting transfers between devices, shift(): return lax.ppermute(v, axis, [(i, (i + k) % n) for i in range(n)])  40.1 us
    pallas_call x8, Pallas kernels, small(): pl.pallas_call(kernel, out_shape=outs, in_specs=[sm] * scalars + [vm] * (...  22.2 us
    ppermute x11, waiting for transfers between devices, shift(): return lax.ppermute(v, axis, [(i, (i + k) % n) for i in range(n)])  15.9 us
    all_to_all x1, starting transfers between devices, layer(): cache = lax.all_to_all(rows, CTX, 0, 0, tiled=True)  11.6 us
    all_to_all x1, starting transfers between devices, layer(): keys = lax.all_to_all(spread, 'z', 0, 0, tiled=True)  10.4 us
    all_to_all x1, waiting for transfers between devices, layer(): cache = lax.all_to_all(rows, CTX, 0, 0, tiled=True)  7.18 us
    unnamed x37, local copies, waits for them, and re-layouts  5.5 us
    all_to_all x1, starting transfers between devices, layer(): mixed = lax.all_to_all(mixed, 'x', 0, 0, tiled=True)  4.72 us
  transfers between devices with their start and end apart: 14, of which 5 were waited for; matrix products, arithmetic and copies ran while one was open for 0% of the time, Pallas kernels for 15%

commit v1 on v0

--- a/solution.py
+++ b/solution.py
@@ -28,9 +28,17 @@
 
 def flash_kernel(offsets, start, *refs):
     count = len(offsets)
-    queries, outs = dict(zip(offsets, refs[:count])), dict(zip(offsets, refs[count + 4 :]))
-    k1_ref, k2_ref, wuk_ref, wuv_ref = refs[count : count + 4]
+    moved, (wuk_ref, wuv_ref), targets = refs[: count + 2], refs[count + 2 : count + 4], refs[count + 4 : 2 * count + 4]
+    held, out_held, sems = refs[2 * count + 4 : 3 * count + 6], refs[3 * count + 6 : -1], refs[-1]
+    loads = [pltpu.make_async_copy(m, h, sems.at[i]) for i, (m, h) in enumerate(zip(moved, held))]
+    for load in loads:
+        load.start()
+    queries, outs = dict(zip(offsets, held[:count])), dict(zip(offsets, out_held))
+    k1_ref, k2_ref = held[count:]
+    stores = []
     z, yh, c = lax.axis_index("z"), lax.axis_index("yh"), lax.axis_index("c")
+    for load in loads:
+        load.wait()
     k1 = k1_ref[...].reshape(768, 576)
     k2 = k2_ref[...].reshape(768, 576)
     j = lax.broadcasted_iota(jnp.int32, (1, 768), 1)
@@ -67,7 +75,7 @@
     def mix(k, p1, p2, total, lse):
         acc = jnp.dot(p1, k1[:, :KV_RANK], preferred_element_type=jnp.float32)
         acc = acc + jnp.dot(p2, k2[:, :KV_RANK], preferred_element_type=jnp.float32)
-        mixed = (acc / total).astype(jnp.bfloat16)
+        mixed = (acc * (1.0 / total)).astype(jnp.bfloat16)
         for h in range(8):
             at = h * 64
             o = jnp.dot(mixed[at : at + 64], wuv_ref[h], preferred_element_type=jnp.float32)
@@ -81,7 +89,12 @@
     for n, k in enumerate(offsets):
         following = score(offsets[n + 1]) if n + 1 < count else None
         mix(k, *weigh(k, s))
+        store = pltpu.make_async_copy(outs[k], targets[n], sems.at[count + 2 + n])
+        store.start()
+        stores.append(store)
         s = following
+    for store in stores:
+        store.wait()
 
 
 def merge_kernel(a_ref, b_ref, c_ref, d_ref, out_ref):
@@ -171,9 +184,15 @@
     out_ref[...] = acc.astype(jnp.bfloat16)
 
 
-def spread_kernel(x_ref, out_ref):
-    for i in range(8):
-        out_ref[i] = x_ref[...]
+def spread_kernel(x_ref, out_ref, held, sems):
+    take = pltpu.make_async_copy(x_ref, held, sems.at[8])
+    take.start()
+    take.wait()
+    moves = [pltpu.make_async_copy(held, out_ref.at[i], sems.at[i]) for i in range(8)]
+    for move in moves:
+        move.start()
+    for move in moves:
+        move.wait()
 
 
 def attend_kernel(lengths, p0, p1, p2, p3, raw_a, raw_b, cache_ref, gain_ref, out_ref):
@@ -241,7 +260,17 @@
     width = prompt_latent.shape[1]
     bf = jnp.bfloat16
     fence = lax.optimization_barrier
-    spread = small(spread_kernel, jax.ShapeDtypeStruct((8, 96, width), bf), [prompt_latent])
+    hbm = pl.BlockSpec(memory_space=pltpu.HBM)
+    spread = pl.pallas_call(
+        spread_kernel,
+        out_shape=jax.ShapeDtypeStruct((8, 96, width), bf),
+        in_specs=[hbm],
+        out_specs=hbm,
+        scratch_shapes=[pltpu.VMEM((96, width), bf), pltpu.SemaphoreType.DMA((9,))],
+        compiler_params=pltpu.CompilerParams(vmem_limit_bytes=4 << 20),
+        cost_estimate=pl.CostEstimate(flops=1 << 10, bytes_accessed=1 << 20, transcendentals=0),
+        name="spread",
+    )(prompt_latent)
     keys = lax.all_to_all(spread, "z", 0, 0, tiled=True)
 
     by_head = jnp.transpose(prefill_query, (1, 0, 2))
@@ -272,25 +301,33 @@
         [owner_slot.reshape(1, 256), jnp.transpose(decode_latent, (1, 2, 0))],
     ).reshape(64, 8, width)
 
-    keys, raw_here, rows, *rest = fence((keys, raw_here, rows, *visiting[1:]))
-    visiting = [packed] + rest
+    keys, raw_here, rows = fence((keys, raw_here, rows))
     raw_there = shift(raw_here, "yl", 1, 2)
     other_keys = shift(keys, "c", 1, 2)
     cache = lax.all_to_all(rows, CTX, 0, 0, tiled=True)
 
     def flash(offsets, chunks):
-        return small(
+        count = len(offsets)
+        chunk, key = pltpu.VMEM((8, 96, 128), bf), pltpu.VMEM((8, 96, width), bf)
+        vmem = pl.BlockSpec(memory_space=pltpu.VMEM)
+        return pl.pallas_call(
             functools.partial(flash_kernel, offsets),
-            [jax.ShapeDtypeStruct((512 + 16, 128), bf)] * len(offsets),
-            [span_start, *chunks, keys, other_keys, w_uk, w_uv],
-            1,
-            limit=24,
-            flops=len(offsets) * 2 * 512 * 1536 * 1100,
-        )
+            out_shape=[jax.ShapeDtypeStruct((512 + 16, 128), bf)] * count,
+            in_specs=[pl.BlockSpec(memory_space=pltpu.SMEM)] + [hbm] * (count + 2) + [vmem] * 2,
+            out_specs=[hbm] * count,
+            scratch_shapes=[chunk] * count
+            + [key] * 2
+            + [pltpu.VMEM((512 + 16, 128), bf)] * count
+            + [pltpu.SemaphoreType.DMA((2 * count + 2,))],
+            compiler_params=pltpu.CompilerParams(vmem_limit_bytes=28 << 20),
+            cost_estimate=pl.CostEstimate(
+                flops=count * 2 * 512 * 1536 * 1100, bytes_accessed=4 << 20, transcendentals=1 << 20
+            ),
+            name="flash",
+        )(span_start, *chunks, keys, other_keys, w_uk, w_uv)
 
     far = (2, 1, 3)
     sending = flash(far, [visiting[k] for k in far])
-    cache, *sending = fence((cache, *sending))
     parts = [None] * 4
     for k, piece in zip(far, sending):
         parts[k] = shift(piece, "yh", 4 - k, 4)
@@ -307,7 +344,7 @@
             kv_gain.reshape(1, KV_RANK),
         ],
         1,
-        limit=16,
+        limit=10,
     )
     own, mixed = fence((packed, mixed))
     mixed = lax.all_to_all(mixed, "x", 0, 0, tiled=True)

time: 120 us -> 127 us (1.058)
  the two profiles are of different devices: /device:TPU:10 before, /device:TPU:1 now
where the time goes in v1:
time: 127 us; the launch traced here: 125 us
  starting transfers between devices  64.3 us (51%)
  waiting for transfers between devices  31 us (24%)
  Pallas kernels  24.3 us (19%)
  local copies, waits for them, and re-layouts  3.79 us (3%)
  between operations  1.59 us (1%)
    ppermute x11, starting transfers between devices, shift(): return lax.ppermute(v, axis, [(i, (i + k) % n) for i in range(n)])  41.5 us
    ppermute x11, waiting for transfers between devices, shift(): return lax.ppermute(v, axis, [(i, (i + k) % n) for i in range(n)])  17.4 us
    pallas_call x2, Pallas kernels, flash(): pl.pallas_call(functools.partial(flash_kernel, offsets), out_shape=[jax.S...  16.1 us
    all_to_all x1, waiting for transfers between devices, layer(): keys = lax.all_to_all(spread, 'z', 0, 0, tiled=True)  13.6 us
    all_to_all x1, starting transfers between devices, layer(): keys = lax.all_to_all(spread, 'z', 0, 0, tiled=True)  11 us
    all_to_all x1, starting transfers between devices, layer(): cache = lax.all_to_all(rows, CTX, 0, 0, tiled=True)  7.78 us
    pallas_call x5, Pallas kernels, small(): pl.pallas_call(kernel, out_shape=outs, in_specs=[sm] * scalars + [vm] * (...  7.05 us
    all_to_all x1, starting transfers between devices, layer(): mixed = lax.all_to_all(mixed, 'x', 0, 0, tiled=True)  4.01 us
  transfers between devices with their start and end apart: 14, of which 4 were waited for; matrix products, arithmetic and copies ran while one was open for 0% of the time, Pallas kernels for 17%

profile of v1, /device:TPU:1, one launch (start us, length us, event | category | flops | bytes accessed | tf_op | source)
XLA Modules:
  0.0 125.1 jit_solution(719557679888798727)
XLA Ops:
  0.6 0.9 copy-done.4
  1.5 1.2 spread.1
  2.7 11.0 %all-to-all-start = ((bf16[8,96,576]{2,1,0:T(8,128)(2,1)}), bf16[8,96,576]{2,1,0:T(8,128)(2,1)}, u32[]{:S(2)}, u32[]{:S(2)}) async-start(bf16[8,96,576]{2,1,0:T(8,128)(2,1)} %spread.1), calls=%async_computation | async-start | bytes 1966080 | tf_op jit(solution)/shard_map/all_to_all | solution.py:274
  13.8 0.8 shard_map.131
  14.6 3.1 %collective-permute-start = (bf16[40,576]{1,0:T(8,128)(2,1)S(1)}, bf16[40,576]{1,0:T(8,128)(2,1)S(1)}, u32[]{:S(2)}, u32[]{:S(2)}) collective-permute-start(bf16[40,576]{1,0:T(8,128)(2,1)S(1)} %get-tuple-element.17), channel_id=1, source_target_pairs={{0,2},{2,4},{4,6},{6,0},{1,3},{3,5},{5,7},{7,1},{8,10},{10,12},{12... | collective-permute-start | bytes 138248 | tf_op jit(solution)/shard_map/ppermute | solution.py:241
  17.7 4.4 %collective-permute-start.1 = (bf16[40,576]{1,0:T(8,128)(2,1)S(1)}, bf16[40,576]{1,0:T(8,128)(2,1)S(1)}, u32[]{:S(2)}, u32[]{:S(2)}) collective-permute-start(bf16[40,576]{1,0:T(8,128)(2,1)S(1)} %get-tuple-element.18), channel_id=1, source_target_pairs={{0,4},{2,6},{4,0},{6,2},{1,5},{3,7},{5,1},{7,3},{8,12},{10,14},{12... | collective-permute-start | bytes 138248 | tf_op jit(solution)/shard_map/ppermute | solution.py:241
  22.1 3.1 %collective-permute-start.2 = (bf16[40,576]{1,0:T(8,128)(2,1)S(1)}, bf16[40,576]{1,0:T(8,128)(2,1)S(1)}, u32[]{:S(2)}, u32[]{:S(2)}) collective-permute-start(bf16[40,576]{1,0:T(8,128)(2,1)S(1)} %get-tuple-element.19), channel_id=1, source_target_pairs={{0,6},{2,0},{4,2},{6,4},{1,7},{3,1},{5,3},{7,5},{8,14},{10,8},{12,... | collective-permute-start | bytes 138248 | tf_op jit(solution)/shard_map/ppermute | solution.py:241
  25.2 1.8 %shard_map.132 = bf16[512,576]{1,0:T(8,128)(2,1)} custom-call(s32[1,256]{1,0:T(1,128)S(1)} %bitcast.14, bf16[4,576,256]{2,1,0:T(8,128)(2,1)S(1)} %bitcast.11), custom_call_target="tpu_custom_call" | custom-call | flops 134217728 | bytes 1048576 | tf_op jit(solution)/shard_map/pallas_call | solution.py:127
  27.1 0.3 collective-permute-done.2.p3
  27.4 0.6 copy-done.5
  28.0 13.6 %all-to-all-done.refs_1_.refs_3_ = bf16[8,96,576]{2,1,0:T(8,128)(2,1)} async-done(((bf16[8,96,576]{2,1,0:T(8,128)(2,1)}), bf16[8,96,576]{2,1,0:T(8,128)(2,1)}, u32[]{:S(2)}, u32[]{:S(2)}) %all-to-all-start) | async-done | bytes 884768 | tf_op jit(solution)/shard_map/all_to_all | solution.py:274
  41.6 2.5 %collective-permute-start.4 = (bf16[8,96,576]{2,1,0:T(8,128)(2,1)}, bf16[8,96,576]{2,1,0:T(8,128)(2,1)}, u32[]{:S(2)}, u32[]{:S(2)}) collective-permute-start(bf16[8,96,576]{2,1,0:T(8,128)(2,1)} %all-to-all-done.refs_1_.refs_3_), channel_id=1, source_target_pairs={{0,8},{8,0},{1,9},{9,1},{2,10},{10,2},{3,11},{11,3},{4,12},{12,4},... | collective-permute-start | bytes 2654216 | tf_op jit(solution)/shard_map/ppermute | solution.py:241
  44.2 7.8 %all-to-all-start.1 = ((bf16[64,8,576]{2,1,0:T(8,128)(2,1)}), bf16[64,8,576]{2,1,0:T(8,128)(2,1)S(1)}, u32[]{:S(2)}, u32[]{:S(2)}) async-start(bf16[64,8,576]{2,1,0:T(8,128)(2,1)} %bitcast.4), calls=%async_computation.1 | async-start | bytes 1310720 | tf_op jit(solution)/shard_map/all_to_all | solution.py:307
  52.1 0.1 maximum_maximum_fusion.refs_0_
  52.2 7.2 %collective-permute-start.5 = (bf16[8,96,128]{2,1,0:T(8,128)(2,1)S(1)}, bf16[8,96,128]{2,1,0:T(8,128)(2,1)S(1)}, u32[]{:S(2)}, u32[]{:S(2)}) collective-permute-start(bf16[8,96,128]{2,1,0:T(8,128)(2,1)S(1)} %maximum_maximum_fusion.refs_0_), channel_id=1, source_target_pairs={{0,32},{16,48},{32,0},{48,16},{1,33},{17,49},{33,1},{49,17},{2,34}... | collective-permute-start | bytes 589832 | tf_op jit(solution)/shard_map/ppermute | solution.py:241
  59.4 2.2 %collective-permute-start.6 = (bf16[8,96,128]{2,1,0:T(8,128)(2,1)S(1)}, bf16[8,96,128]{2,1,0:T(8,128)(2,1)S(1)}, u32[]{:S(2)}, u32[]{:S(2)}) collective-permute-start(bf16[8,96,128]{2,1,0:T(8,128)(2,1)S(1)} %maximum_maximum_fusion.refs_0_), channel_id=1, source_target_pairs={{0,16},{16,32},{32,48},{48,0},{1,17},{17,33},{33,49},{49,1},{2,18}... | collective-permute-start | bytes 589832 | tf_op jit(solution)/shard_map/ppermute | solution.py:241
  61.6 5.2 %collective-permute-start.7 = (bf16[8,96,128]{2,1,0:T(8,128)(2,1)S(1)}, bf16[8,96,128]{2,1,0:T(8,128)(2,1)S(1)}, u32[]{:S(2)}, u32[]{:S(2)}) collective-permute-start(bf16[8,96,128]{2,1,0:T(8,128)(2,1)S(1)} %maximum_maximum_fusion.refs_0_), channel_id=1, source_target_pairs={{0,48},{16,0},{32,16},{48,32},{1,49},{17,1},{33,17},{49,33},{2,50}... | collective-permute-start | bytes 589832 | tf_op jit(solution)/shard_map/ppermute | solution.py:241
  67.4 2.3 %collective-permute-start.3 = (f32[8,576]{1,0:T(8,128)S(1)}, f32[8,576]{1,0:T(8,128)S(1)}, u32[]{:S(2)}, u32[]{:S(2)}) collective-permute-start(f32[8,576]{1,0:T(8,128)S(1)} %convert_add_fusion.raw_a), channel_id=1, source_target_pairs={{0,1},{1,0},{2,3},{3,2},{4,5},{5,4},{6,7},{7,6},{8,9},{9,8},{10,11... | collective-permute-start | bytes 55304 | tf_op jit(solution)/shard_map/ppermute | solution.py:241
  69.7 11.4 %collective-permute-done.5.refs_0_ = bf16[8,96,128]{2,1,0:T(8,128)(2,1)S(1)} collective-permute-done((bf16[8,96,128]{2,1,0:T(8,128)(2,1)S(1)}, bf16[8,96,128]{2,1,0:T(8,128)(2,1)S(1)}, u32[]{:S(2)}, u32[]{:S(2)}) %collective-permute-start.5) | collective-permute-done | bytes 196640 | tf_op jit(solution)/shard_map/ppermute | solution.py:241
  81.2 5.6 %collective-permute-done.6.refs_1_ = bf16[8,96,128]{2,1,0:T(8,128)(2,1)S(1)} collective-permute-done((bf16[8,96,128]{2,1,0:T(8,128)(2,1)S(1)}, bf16[8,96,128]{2,1,0:T(8,128)(2,1)S(1)}, u32[]{:S(2)}, u32[]{:S(2)}) %collective-permute-start.6) | collective-permute-done | bytes 196640 | tf_op jit(solution)/shard_map/ppermute | solution.py:241
  86.8 11.1 %flash.3 = (bf16[528,128]{1,0:T(8,128)(2,1)}, bf16[528,128]{1,0:T(8,128)(2,1)}, bf16[528,128]{1,0:T(8,128)(2,1)}) custom-call(s32[1]{0:T(128)S(6)} %copy.17.start, bf16[8,96,128]{2,1,0:T(8,128)(2,1)S(1)} %collective-permute-done.5.refs_0_, bf16[8,96,128]{2,1,0:T(8,128)(2,1)S(1)} %collective-permute-done.6.refs_1_, ...), custom_call_target="tpu_custom_call" | custom-call | flops 5190451200 | bytes 4194304 | tf_op jit(solution)/shard_map/flash/pallas_call | solution.py:313
  97.9 4.1 %collective-permute-start.10 = (bf16[528,128]{1,0:T(8,128)(2,1)}, bf16[528,128]{1,0:T(8,128)(2,1)S(1)}, u32[]{:S(2)}, u32[]{:S(2)}) collective-permute-start(bf16[528,128]{1,0:T(8,128)(2,1)} %get-tuple-element.28), channel_id=1, source_target_pairs={{0,16},{16,32},{32,48},{48,0},{1,17},{17,33},{33,49},{49,1},{2,18}... | collective-permute-start | bytes 405512 | tf_op jit(solution)/shard_map/ppermute | solution.py:241
  102.0 3.3 %collective-permute-start.8 = (bf16[528,128]{1,0:T(8,128)(2,1)}, bf16[528,128]{1,0:T(8,128)(2,1)S(1)}, u32[]{:S(2)}, u32[]{:S(2)}) collective-permute-start(bf16[528,128]{1,0:T(8,128)(2,1)} %get-tuple-element.26), channel_id=1, source_target_pairs={{0,48},{16,0},{32,16},{48,32},{1,49},{17,1},{33,17},{49,33},{2,50}... | collective-permute-start | bytes 405512 | tf_op jit(solution)/shard_map/ppermute | solution.py:241
  105.3 4.2 %collective-permute-start.9 = (bf16[528,128]{1,0:T(8,128)(2,1)}, bf16[528,128]{1,0:T(8,128)(2,1)S(1)}, u32[]{:S(2)}, u32[]{:S(2)}) collective-permute-start(bf16[528,128]{1,0:T(8,128)(2,1)} %get-tuple-element.27), channel_id=1, source_target_pairs={{0,32},{16,48},{32,0},{48,16},{1,33},{17,49},{33,1},{49,17},{2,34}... | collective-permute-start | bytes 405512 | tf_op jit(solution)/shard_map/ppermute | solution.py:241
  109.5 0.8 copy-done.6
  110.3 0.7 copy-done.9
  111.0 0.7 copy-done.11
  111.7 2.1 %shard_map.133 = bf16[4,32,512]{2,1,0:T(8,128)(2,1)} custom-call(s32[4]{0:T(128)S(1)} %copy-done.11, bf16[40,576]{1,0:T(8,128)(2,1)S(1)} %get-tuple-element.16.p0, bf16[40,576]{1,0:T(8,128)(2,1)S(1)} %collective-permute-done.p1, bf16[40,576]{1,0:T(8,128)(2,1)S(1)} %collective-permute-done.1.p2, bf16[40,576]{1,0:T(8,128)(2,1)S(1)} %copy-done.6, ...), custom_call_target="tpu_custom_call" | custom-call | flops 134217728 | bytes 1048576 | tf_op jit(solution)/shard_map/pallas_call | solution.py:127
  113.7 4.0 %all-to-all-start.2 = ((bf16[4,32,512]{2,1,0:T(8,128)(2,1)}), bf16[4,32,512]{2,1,0:T(8,128)(2,1)S(1)}, u32[]{:S(2)}, u32[]{:S(2)}) async-start(bf16[4,32,512]{2,1,0:T(8,128)(2,1)} %shard_map.133), calls=%async_computation.2 | async-start | bytes 262144 | tf_op jit(solution)/shard_map/all_to_all | solution.py:350
  117.7 5.0 %flash.2.a_ref = bf16[528,128]{1,0:T(8,128)(2,1)S(1)} custom-call(s32[1]{0:T(128)S(6)} %copy.17.start, bf16[8,96,128]{2,1,0:T(8,128)(2,1)S(1)} %maximum_maximum_fusion.refs_0_, bf16[8,96,576]{2,1,0:T(8,128)(2,1)} %all-to-all-done.refs_1_.refs_3_, bf16[8,96,576]{2,1,0:T(8,128)(2,1)} %collective-permute-done.4.refs_2_.refs_4_, ...), custom_call_target="tpu_custom_call" | custom-call | flops 1730150400 | bytes 4194304 | tf_op jit(solution)/shard_map/flash/pallas_call | solution.py:313
  122.7 1.0 shard_map.135
  123.8 1.3 %shard_map.134 = bf16[512,128]{1,0:T(8,128)(2,1)} custom-call(bf16[528,128]{1,0:T(8,128)(2,1)S(1)} %flash.2.a_ref, bf16[528,128]{1,0:T(8,128)(2,1)S(1)} %collective-permute-done.8.b_ref, bf16[528,128]{1,0:T(8,128)(2,1)S(1)} %collective-permute-done.9.c_ref, bf16[528,128]{1,0:T(8,128)(2,1)S(1)} %collective-permute-done.10.d_ref), custom_call_target="tpu_custom_call" | custom-call | flops 134217728 | bytes 1048576 | tf_op jit(solution)/shard_map/pallas_call | solution.py:127
  (35 shorter events, 0.2 us)
Async XLA Ops:
  0.6 0.9 copy-start.4
  1.5 12.2 %copy-start.3 = (bf16[896,576]{0,1:T(8,128)(2,1)S(1)}, bf16[896,576]{0,1:T(8,128)(2,1)}, u32[]{:S(2)}) copy-start(bf16[896,576]{0,1:T(8,128)(2,1)} %param.22) | copy-start | bytes 3096580
  2.7 11.1 %copy-start.2 = (bf16[8,128,512]{2,1,0:T(8,128)(2,1)S(1)}, bf16[8,128,512]{2,1,0:T(8,128)(2,1)}, u32[]{:S(2)}) copy-start(bf16[8,128,512]{2,1,0:T(8,128)(2,1)} %refs_5_.1) | copy-start | bytes 3145732
  2.7 11.1 %copy-start.7 = (bf16[4,4,8,192]{3,2,1,0:T(8,128)(2,1)S(1)}, bf16[4,4,8,192]{3,2,1,0:T(8,128)(2,1)}, u32[]{:S(2)}) copy-start(bf16[4,4,8,192]{3,2,1,0:T(8,128)(2,1)} %q_ref.1) | copy-start | bytes 147460
  2.7 11.1 %copy-start.8 = (bf16[4,4,896]{2,1,0:T(4,128)(2,1)S(1)}, bf16[4,4,896]{2,1,0:T(4,128)(2,1)}, u32[]{:S(2)}) copy-start(bf16[4,4,896]{2,1,0:T(4,128)(2,1)} %hid_ref.1) | copy-start | bytes 86020
  2.7 38.9 %all-to-all-start = ((bf16[8,96,576]{2,1,0:T(8,128)(2,1)}), bf16[8,96,576]{2,1,0:T(8,128)(2,1)}, u32[]{:S(2)}, u32[]{:S(2)}) async-start(bf16[8,96,576]{2,1,0:T(8,128)(2,1)} %spread.1), calls=%async_computation | async-start | bytes 1966080 | tf_op jit(solution)/shard_map/all_to_all | solution.py:274
  13.7 11.5 %copy-start = (bf16[256,4,576]{0,2,1:T(8,128)(2,1)S(1)}, bf16[256,4,576]{0,2,1:T(8,128)(2,1)}, u32[]{:S(2)}) copy-start(bf16[256,4,576]{0,2,1:T(8,128)(2,1)} %param.17) | copy-start | bytes 3538948
  13.7 11.5 %copy-start.10 = (s32[256]{0:T(256)S(1)}, s32[256]{0:T(256)}, u32[]{:S(2)}) copy-start(s32[256]{0:T(256)} %param.18) | copy-start | bytes 3076
  14.6 12.5 %collective-permute-start = (bf16[40,576]{1,0:T(8,128)(2,1)S(1)}, bf16[40,576]{1,0:T(8,128)(2,1)S(1)}, u32[]{:S(2)}, u32[]{:S(2)}) collective-permute-start(bf16[40,576]{1,0:T(8,128)(2,1)S(1)} %get-tuple-element.17), channel_id=1, source_target_pairs={{0,2},{2,4},{4,6},{6,0},{1,3},{3,5},{5,7},{7,1},{8,10},{10,12},{12... | collective-permute-start | bytes 138248 | tf_op jit(solution)/shard_map/ppermute | solution.py:241
  17.7 9.3 %collective-permute-start.1 = (bf16[40,576]{1,0:T(8,128)(2,1)S(1)}, bf16[40,576]{1,0:T(8,128)(2,1)S(1)}, u32[]{:S(2)}, u32[]{:S(2)}) collective-permute-start(bf16[40,576]{1,0:T(8,128)(2,1)S(1)} %get-tuple-element.18), channel_id=1, source_target_pairs={{0,4},{2,6},{4,0},{6,2},{1,5},{3,7},{5,1},{7,3},{8,12},{10,14},{12... | collective-permute-start | bytes 138248 | tf_op jit(solution)/shard_map/ppermute | solution.py:241
  22.1 5.3 %collective-permute-start.2 = (bf16[40,576]{1,0:T(8,128)(2,1)S(1)}, bf16[40,576]{1,0:T(8,128)(2,1)S(1)}, u32[]{:S(2)}, u32[]{:S(2)}) collective-permute-start(bf16[40,576]{1,0:T(8,128)(2,1)S(1)} %get-tuple-element.19), channel_id=1, source_target_pairs={{0,6},{2,0},{4,2},{6,4},{1,7},{3,1},{5,3},{7,5},{8,14},{10,8},{12,... | collective-permute-start | bytes 138248 | tf_op jit(solution)/shard_map/ppermute | solution.py:241
  25.2 26.7 %copy-start.12 = (bf16[64,8,192]{2,1,0:T(8,128)(2,1)S(1)}, bf16[64,8,192]{2,1,0:T(8,128)(2,1)}, u32[]{:S(2)}) copy-start(bf16[64,8,192]{2,1,0:T(8,128)(2,1)} %param.13) | copy-start | bytes 589828
  27.4 0.6 copy-start.5
  41.6 45.2 %copy-start.1 = (bf16[8,512,128]{2,1,0:T(8,128)(2,1)S(1)}, bf16[8,512,128]{2,1,0:T(8,128)(2,1)}, u32[]{:S(2)}) copy-start(bf16[8,512,128]{2,1,0:T(8,128)(2,1)} %wuv_ref.1) | copy-start | bytes 3145732
  41.6 45.1 %collective-permute-start.4 = (bf16[8,96,576]{2,1,0:T(8,128)(2,1)}, bf16[8,96,576]{2,1,0:T(8,128)(2,1)}, u32[]{:S(2)}, u32[]{:S(2)}) collective-permute-start(bf16[8,96,576]{2,1,0:T(8,128)(2,1)} %all-to-all-done.refs_1_.refs_3_), channel_id=1, source_target_pairs={{0,8},{8,0},{1,9},{9,1},{2,10},{10,2},{3,11},{11,3},{4,12},{12,4},... | collective-permute-start | bytes 2654216 | tf_op jit(solution)/shard_map/ppermute | solution.py:241
  44.2 65.3 %all-to-all-start.1 = ((bf16[64,8,576]{2,1,0:T(8,128)(2,1)}), bf16[64,8,576]{2,1,0:T(8,128)(2,1)S(1)}, u32[]{:S(2)}, u32[]{:S(2)}) async-start(bf16[64,8,576]{2,1,0:T(8,128)(2,1)} %bitcast.4), calls=%async_computation.1 | async-start | bytes 1310720 | tf_op jit(solution)/shard_map/all_to_all | solution.py:307
  52.2 29.0 %collective-permute-start.5 = (bf16[8,96,128]{2,1,0:T(8,128)(2,1)S(1)}, bf16[8,96,128]{2,1,0:T(8,128)(2,1)S(1)}, u32[]{:S(2)}, u32[]{:S(2)}) collective-permute-start(bf16[8,96,128]{2,1,0:T(8,128)(2,1)S(1)} %maximum_maximum_fusion.refs_0_), channel_id=1, source_target_pairs={{0,32},{16,48},{32,0},{48,16},{1,33},{17,49},{33,1},{49,17},{2,34}... | collective-permute-start | bytes 589832 | tf_op jit(solution)/shard_map/ppermute | solution.py:241
  59.4 27.4 %collective-permute-start.6 = (bf16[8,96,128]{2,1,0:T(8,128)(2,1)S(1)}, bf16[8,96,128]{2,1,0:T(8,128)(2,1)S(1)}, u32[]{:S(2)}, u32[]{:S(2)}) collective-permute-start(bf16[8,96,128]{2,1,0:T(8,128)(2,1)S(1)} %maximum_maximum_fusion.refs_0_), channel_id=1, source_target_pairs={{0,16},{16,32},{32,48},{48,0},{1,17},{17,33},{33,49},{49,1},{2,18}... | collective-permute-start | bytes 589832 | tf_op jit(solution)/shard_map/ppermute | solution.py:241
  61.6 25.2 %collective-permute-start.7 = (bf16[8,96,128]{2,1,0:T(8,128)(2,1)S(1)}, bf16[8,96,128]{2,1,0:T(8,128)(2,1)S(1)}, u32[]{:S(2)}, u32[]{:S(2)}) collective-permute-start(bf16[8,96,128]{2,1,0:T(8,128)(2,1)S(1)} %maximum_maximum_fusion.refs_0_), channel_id=1, source_target_pairs={{0,48},{16,0},{32,16},{48,32},{1,49},{17,1},{33,17},{49,33},{2,50}... | collective-permute-start | bytes 589832 | tf_op jit(solution)/shard_map/ppermute | solution.py:241
  67.4 42.1 %collective-permute-start.3 = (f32[8,576]{1,0:T(8,128)S(1)}, f32[8,576]{1,0:T(8,128)S(1)}, u32[]{:S(2)}, u32[]{:S(2)}) collective-permute-start(f32[8,576]{1,0:T(8,128)S(1)} %convert_add_fusion.raw_a), channel_id=1, source_target_pairs={{0,1},{1,0},{2,3},{3,2},{4,5},{5,4},{6,7},{7,6},{8,9},{9,8},{10,11... | collective-permute-start | bytes 55304 | tf_op jit(solution)/shard_map/ppermute | solution.py:241
  97.9 25.8 %collective-permute-start.10 = (bf16[528,128]{1,0:T(8,128)(2,1)}, bf16[528,128]{1,0:T(8,128)(2,1)S(1)}, u32[]{:S(2)}, u32[]{:S(2)}) collective-permute-start(bf16[528,128]{1,0:T(8,128)(2,1)} %get-tuple-element.28), channel_id=1, source_target_pairs={{0,16},{16,32},{32,48},{48,0},{1,17},{17,33},{33,49},{49,1},{2,18}... | collective-permute-start | bytes 405512 | tf_op jit(solution)/shard_map/ppermute | solution.py:241
  102.0 21.7 %collective-permute-start.8 = (bf16[528,128]{1,0:T(8,128)(2,1)}, bf16[528,128]{1,0:T(8,128)(2,1)S(1)}, u32[]{:S(2)}, u32[]{:S(2)}) collective-permute-start(bf16[528,128]{1,0:T(8,128)(2,1)} %get-tuple-element.26), channel_id=1, source_target_pairs={{0,48},{16,0},{32,16},{48,32},{1,49},{17,1},{33,17},{49,33},{2,50}... | collective-permute-start | bytes 405512 | tf_op jit(solution)/shard_map/ppermute | solution.py:241
  105.3 18.4 %collective-permute-start.9 = (bf16[528,128]{1,0:T(8,128)(2,1)}, bf16[528,128]{1,0:T(8,128)(2,1)S(1)}, u32[]{:S(2)}, u32[]{:S(2)}) collective-permute-start(bf16[528,128]{1,0:T(8,128)(2,1)} %get-tuple-element.27), channel_id=1, source_target_pairs={{0,32},{16,48},{32,0},{48,16},{1,33},{17,49},{33,1},{49,17},{2,34}... | collective-permute-start | bytes 405512 | tf_op jit(solution)/shard_map/ppermute | solution.py:241
  109.5 0.8 copy-start.6
  110.3 0.7 copy-start.9
  111.0 0.7 copy-start.11
  113.7 9.0 %all-to-all-start.2 = ((bf16[4,32,512]{2,1,0:T(8,128)(2,1)}), bf16[4,32,512]{2,1,0:T(8,128)(2,1)S(1)}, u32[]{:S(2)}, u32[]{:S(2)}) async-start(bf16[4,32,512]{2,1,0:T(8,128)(2,1)} %shard_map.133), calls=%async_computation.2 | async-start | bytes 262144 | tf_op jit(solution)/shard_map/all_to_all | solution.py:350

commit v2 on v1

--- a/solution.py
+++ b/solution.py
@@ -31,16 +31,21 @@
     moved, (wuk_ref, wuv_ref), targets = refs[: count + 2], refs[count + 2 : count + 4], refs[count + 4 : 2 * count + 4]
     held, out_held, sems = refs[2 * count + 4 : 3 * count + 6], refs[3 * count + 6 : -1], refs[-1]
     loads = [pltpu.make_async_copy(m, h, sems.at[i]) for i, (m, h) in enumerate(zip(moved, held))]
-    for load in loads:
+    for load in (loads[0], *loads[count:], *loads[1:count]):
         load.start()
     queries, outs = dict(zip(offsets, held[:count])), dict(zip(offsets, out_held))
     k1_ref, k2_ref = held[count:]
     stores = []
     z, yh, c = lax.axis_index("z"), lax.axis_index("yh"), lax.axis_index("c")
-    for load in loads:
-        load.wait()
-    k1 = k1_ref[...].reshape(768, 576)
-    k2 = k2_ref[...].reshape(768, 576)
+    waits = dict(zip((*offsets, "k1", "k2"), loads))
+    ready = {}
+
+    def key_rows(name, ref):
+        if name not in ready:
+            waits[name].wait()
+            ready[name] = ref[...].reshape(768, 576)
+        return ready[name]
+
     j = lax.broadcasted_iota(jnp.int32, (1, 768), 1)
     blk = (j * 683) >> 16
     kpos = blk * 768 + (j - blk * 96) + yh * 192
@@ -49,14 +54,15 @@
 
     def score(k):
         rows = []
+        waits[k].wait()
         for h in range(8):
             pair = queries[k][h, 64:, :]
             rope = jnp.concatenate([pair[:, :64], pair[:, 64:]], axis=0)
             a = jnp.dot(queries[k][h, :64, :], wuk_ref[h], preferred_element_type=jnp.float32)
             rows.append(jnp.concatenate([a.astype(jnp.bfloat16), rope], axis=1))
         full = jnp.concatenate(rows, axis=0)
-        s1 = lax.dot_general(full, k1, NT, preferred_element_type=jnp.float32)
-        s2 = lax.dot_general(full, k2, NT, preferred_element_type=jnp.float32)
+        s1 = lax.dot_general(full, key_rows("k1", k1_ref), NT, preferred_element_type=jnp.float32)
+        s2 = lax.dot_general(full, key_rows("k2", k2_ref), NT, preferred_element_type=jnp.float32)
         return s1, s2
 
     def weigh(k, s):
@@ -73,8 +79,8 @@
         return p1.astype(jnp.bfloat16), p2.astype(jnp.bfloat16), total, lse
 
     def mix(k, p1, p2, total, lse):
-        acc = jnp.dot(p1, k1[:, :KV_RANK], preferred_element_type=jnp.float32)
-        acc = acc + jnp.dot(p2, k2[:, :KV_RANK], preferred_element_type=jnp.float32)
+        acc = jnp.dot(p1, ready["k1"][:, :KV_RANK], preferred_element_type=jnp.float32)
+        acc = acc + jnp.dot(p2, ready["k2"][:, :KV_RANK], preferred_element_type=jnp.float32)
         mixed = (acc * (1.0 / total)).astype(jnp.bfloat16)
         for h in range(8):
             at = h * 64
@@ -147,7 +153,8 @@
 
 
 def prep_kernel(q_ref, wuk_ref, hid_ref, wd_ref, *refs):
-    outs, rows = refs[:4], refs[4]
+    near, next_, far, rows = refs
+    outs = (near, next_, far.at[:40], far.at[40:])
     q = q_ref[...].reshape(128, NOPE + ROPE)
     nope = q[:, :NOPE].astype(jnp.float32)
     head = head_rows(128)
@@ -166,7 +173,7 @@
     pick = jnp.where(((o & 7) * 4 + (o >> 3) == n) & ((o & 7) < 4), 1.0, 0.0)
     rows[128:, :] = jnp.dot(pick.astype(jnp.bfloat16), raw, preferred_element_type=jnp.float32)
     for k in range(4):
-        r = (lax.axis_index("x") + k) & 3
+        r = lax.axis_index("x") ^ k
         for s in range(4):
             at = pl.multiple_of((s * 4 + r) * 8, 8)
             outs[k][s * 8 : s * 8 + 8, :] = rows[pl.ds(at, 8), :].astype(jnp.bfloat16)
@@ -184,24 +191,21 @@
     out_ref[...] = acc.astype(jnp.bfloat16)
 
 
-def spread_kernel(x_ref, out_ref, held, sems):
-    take = pltpu.make_async_copy(x_ref, held, sems.at[8])
-    take.start()
-    take.wait()
-    moves = [pltpu.make_async_copy(held, out_ref.at[i], sems.at[i]) for i in range(8)]
+def spread_kernel(x_ref, out_ref, sems):
+    moves = [pltpu.make_async_copy(x_ref, out_ref.at[i], sems.at[i]) for i in range(8)]
     for move in moves:
         move.start()
     for move in moves:
         move.wait()
 
 
-def attend_kernel(lengths, p0, p1, p2, p3, raw_a, raw_b, cache_ref, gain_ref, out_ref):
+def attend_kernel(lengths, p0, p13, p2, raw_a, raw_b, cache_ref, gain_ref, out_ref):
     raw = raw_a[...] + raw_b[...]
     front = raw[:, :KV_RANK]
     factor = lax.rsqrt(jnp.mean(front * front, axis=1, keepdims=True) + 1e-06)
     fresh = jnp.concatenate([front * factor * gain_ref[...], raw[:, KV_RANK:]], axis=1)
     fresh = fresh.astype(jnp.bfloat16)
-    q = jnp.concatenate([p[:32, :] for p in (p0, p1, p2, p3)], axis=0)
+    q = jnp.concatenate([p0[:32], p13[:32], p2[:32], p13[40:72]], axis=0)
     cache = cache_ref[...]
     s1 = lax.dot_general(q, cache, NT, preferred_element_type=jnp.float32)
     s2 = lax.dot_general(q, fresh, NT, preferred_element_type=jnp.float32)
@@ -221,7 +225,7 @@
     )
     mixed = (acc / total).astype(jnp.bfloat16)
     for k in range(4):
-        out_ref[(lax.axis_index("x") + (4 - k)) & 3] = mixed[k * 32 : (k + 1) * 32]
+        out_ref[lax.axis_index("x") ^ k] = mixed[k * 32 : (k + 1) * 32]
 
 
 def finish_kernel(m_ref, wuv_ref, out_ref):
@@ -239,6 +243,10 @@
 
 def shift(v, axis, k, n):
     return lax.ppermute(v, axis, [(i, (i + k) % n) for i in range(n)])
+
+
+def trade(v, axis, k, n):
+    return lax.ppermute(v, axis, [(i, i ^ k) for i in range(n)])
 
 
 def layer(
@@ -264,9 +272,9 @@
     spread = pl.pallas_call(
         spread_kernel,
         out_shape=jax.ShapeDtypeStruct((8, 96, width), bf),
-        in_specs=[hbm],
+        in_specs=[pl.BlockSpec(memory_space=pltpu.VMEM)],
         out_specs=hbm,
-        scratch_shapes=[pltpu.VMEM((96, width), bf), pltpu.SemaphoreType.DMA((9,))],
+        scratch_shapes=[pltpu.SemaphoreType.DMA((8,))],
         compiler_params=pltpu.CompilerParams(vmem_limit_bytes=4 << 20),
         cost_estimate=pl.CostEstimate(flops=1 << 10, bytes_accessed=1 << 20, transcendentals=0),
         name="spread",
@@ -282,27 +290,27 @@
     for k in (2, 1, 3):
         visiting[k] = shift(packed, "yh", k, 4)
     tile = jax.ShapeDtypeStruct((40, width), bf)
-    sent = small(
+    near, following, far_two = small(
         prep_kernel,
-        [tile] * 4,
+        [tile, tile, jax.ShapeDtypeStruct((80, width), bf)],
         [decode_query, w_uk, hidden_new, w_down.T],
         0,
         [pltpu.VMEM((160, width), jnp.float32)],
     )
-    got = [sent[0]] + [None] * 3
-    for k in (2, 1, 3):
-        got[k] = shift(sent[k], "x", k, 4)
-    raw_here = got[0][32:].astype(jnp.float32)
-    for k in (1, 2, 3):
-        raw_here = raw_here + got[k][32:].astype(jnp.float32)
+    from_two = trade(far_two, "x", 2, 4)
+    relay = jnp.concatenate([following, from_two[40:]], axis=0)
+    from_one = trade(relay, "x", 1, 4)
+    got = (near, from_one, from_two)
+    raw_here = near[32:].astype(jnp.float32) + from_two[32:40].astype(jnp.float32)
+    raw_here = raw_here + from_one[32:40].astype(jnp.float32) + from_one[72:].astype(jnp.float32)
+    raw_there = trade(raw_here, "yl", 1, 2)
     rows = small(
         pack_kernel,
         jax.ShapeDtypeStruct((512, width), bf),
         [owner_slot.reshape(1, 256), jnp.transpose(decode_latent, (1, 2, 0))],
     ).reshape(64, 8, width)
 
-    keys, raw_here, rows = fence((keys, raw_here, rows))
-    raw_there = shift(raw_here, "yl", 1, 2)
+    keys, rows = fence((keys, rows))
     other_keys = shift(keys, "c", 1, 2)
     cache = lax.all_to_all(rows, CTX, 0, 0, tiled=True)
 
@@ -344,7 +352,7 @@
             kv_gain.reshape(1, KV_RANK),
         ],
         1,
-        limit=10,
+        limit=60,
     )
     own, mixed = fence((packed, mixed))
     mixed = lax.all_to_all(mixed, "x", 0, 0, tiled=True)

time: 127 us -> 131 us (1.031)
  waiting for transfers between devices: 31 us -> 39.9 us
  starting transfers between devices: 64.3 us -> 60.9 us
  local copies, waits for them, and re-layouts: 3.79 us -> 1.65 us
    ppermute x11 -> x7, starting transfers between devices: 41.5 us -> 29 us  [shift(): return lax.ppermute(v, axis, [(i, (i + k) % n) for i in range(n)])]
    all_to_all x1, waiting for transfers between devices: 13.6 us -> 26 us  [layer(): keys = lax.all_to_all(spread, 'z', 0, 0, tiled=True)]
    ppermute x0 -> x3, starting transfers between devices: none -> 9.19 us  [trade(): return lax.ppermute(v, axis, [(i, i ^ k) for i in range(n)])]
    ppermute x11 -> x7, waiting for transfers between devices: 17.4 us -> 13.9 us  [shift(): return lax.ppermute(v, axis, [(i, (i + k) % n) for i in range(n)])]
    unnamed x27 -> x29, local copies, waits for them, and re-layouts: 3.74 us -> 1.59 us
  transfers between devices with their start and end apart: 14 -> 13, of which waited for: 4 -> 4; matrix products, arithmetic and copies ran while one was open for 0% -> 0% of each run, Pallas kernels for 17% -> 18%
where the time goes in v2:
time: 131 us; the launch traced here: 130 us
  starting transfers between devices  60.9 us (46%)
  waiting for transfers between devices  39.9 us (30%)
  Pallas kernels  25.3 us (19%)
  between operations  1.68 us (1%)
  local copies, waits for them, and re-layouts  1.65 us (1%)
    ppermute x7, starting transfers between devices, shift(): return lax.ppermute(v, axis, [(i, (i + k) % n) for i in range(n)])  29 us
    all_to_all x1, waiting for transfers between devices, layer(): keys = lax.all_to_all(spread, 'z', 0, 0, tiled=True)  26 us
    pallas_call x2, Pallas kernels, flash(): pl.pallas_call(functools.partial(flash_kernel, offsets), out_shape=[jax.S...  16.6 us
    ppermute x7, waiting for transfers between devices, shift(): return lax.ppermute(v, axis, [(i, (i + k) % n) for i in range(n)])  13.9 us
    all_to_all x1, starting transfers between devices, layer(): keys = lax.all_to_all(spread, 'z', 0, 0, tiled=True)  11 us
    ppermute x3, starting transfers between devices, trade(): return lax.ppermute(v, axis, [(i, i ^ k) for i in range(n)])  9.19 us
    all_to_all x1, starting transfers between devices, layer(): cache = lax.all_to_all(rows, CTX, 0, 0, tiled=True)  8.26 us
    pallas_call x5, Pallas kernels, small(): pl.pallas_call(kernel, out_shape=outs, in_specs=[sm] * scalars + [vm] * (...  7.71 us
  transfers between devices with their start and end apart: 13, of which 4 were waited for; matrix products, arithmetic and copies ran while one was open for 0% of the time, Pallas kernels for 18%

profile of v2, /device:TPU:1, one launch (start us, length us, event | category | flops | bytes accessed | tf_op | source)
XLA Modules:
  0.0 129.6 jit_solution(1340766885770759366)
XLA Ops:
  0.6 0.9 copy-done.4
  1.5 1.0 spread.1
  2.6 0.0 copy-start
  2.6 0.0 copy-start.3
  2.6 11.0 %all-to-all-start = ((bf16[8,96,576]{2,1,0:T(8,128)(2,1)}), bf16[8,96,576]{2,1,0:T(8,128)(2,1)}, u32[]{:S(2)}, u32[]{:S(2)}) async-start(bf16[8,96,576]{2,1,0:T(8,128)(2,1)} %spread.1), calls=%async_computation | async-start | bytes 1966080 | tf_op jit(solution)/shard_map/all_to_all | solution.py:282
  13.6 0.0 copy-start.6
  13.6 0.0 copy-start.7
  13.6 1.8 %shard_map.132 = bf16[512,576]{1,0:T(8,128)(2,1)} custom-call(s32[1,256]{1,0:T(1,128)S(1)} %bitcast.12, bf16[4,576,256]{2,1,0:T(8,128)(2,1)S(1)} %bitcast.10), custom_call_target="tpu_custom_call" | custom-call | flops 134217728 | bytes 1048576 | tf_op jit(solution)/shard_map/pallas_call | solution.py:133
  15.5 26.0 %all-to-all-done.refs_1_.refs_3_ = bf16[8,96,576]{2,1,0:T(8,128)(2,1)} async-done(((bf16[8,96,576]{2,1,0:T(8,128)(2,1)}), bf16[8,96,576]{2,1,0:T(8,128)(2,1)}, u32[]{:S(2)}, u32[]{:S(2)}) %all-to-all-start) | async-done | bytes 884768 | tf_op jit(solution)/shard_map/all_to_all | solution.py:282
  41.5 2.4 %collective-permute-start.3 = (bf16[8,96,576]{2,1,0:T(8,128)(2,1)}, bf16[8,96,576]{2,1,0:T(8,128)(2,1)}, u32[]{:S(2)}, u32[]{:S(2)}) collective-permute-start(bf16[8,96,576]{2,1,0:T(8,128)(2,1)} %all-to-all-done.refs_1_.refs_3_), channel_id=1, source_target_pairs={{0,8},{8,0},{1,9},{9,1},{2,10},{10,2},{3,11},{11,3},{4,12},{12,4},... | collective-permute-start | bytes 2654216 | tf_op jit(solution)/shard_map/ppermute | solution.py:245
  43.9 0.8 shard_map.131
  44.7 4.7 %collective-permute-start = (bf16[80,576]{1,0:T(8,128)(2,1)S(1)}, bf16[80,576]{1,0:T(8,128)(2,1)S(1)}, u32[]{:S(2)}, u32[]{:S(2)}) collective-permute-start(bf16[80,576]{1,0:T(8,128)(2,1)S(1)} %get-tuple-element.16), channel_id=1, source_target_pairs={{0,4},{2,6},{4,0},{6,2},{1,5},{3,7},{5,1},{7,3},{8,12},{10,14},{12... | collective-permute-start | bytes 276488 | tf_op jit(solution)/shard_map/ppermute | solution.py:249
  49.5 8.3 %all-to-all-start.1 = ((bf16[64,8,576]{2,1,0:T(8,128)(2,1)}), bf16[64,8,576]{2,1,0:T(8,128)(2,1)}, u32[]{:S(2)}, u32[]{:S(2)}) async-start(bf16[64,8,576]{2,1,0:T(8,128)(2,1)} %bitcast.4), calls=%async_computation.1 | async-start | bytes 1310720 | tf_op jit(solution)/shard_map/all_to_all | solution.py:315
  57.9 2.2 %collective-permute-start.1 = (bf16[80,576]{1,0:T(8,128)(2,1)S(1)}, bf16[80,576]{1,0:T(8,128)(2,1)S(1)}, u32[]{:S(2)}, u32[]{:S(2)}) collective-permute-start(bf16[80,576]{1,0:T(8,128)(2,1)S(1)} %pad_maximum_fusion), channel_id=1, source_target_pairs={{0,2},{2,0},{4,6},{6,4},{1,3},{3,1},{5,7},{7,5},{8,10},{10,8},{12,... | collective-permute-start | bytes 276488 | tf_op jit(solution)/shard_map/ppermute | solution.py:249
  60.1 0.1 maximum_maximum_fusion.refs_0_
  60.2 7.2 %collective-permute-start.4 = (bf16[8,96,128]{2,1,0:T(8,128)(2,1)S(1)}, bf16[8,96,128]{2,1,0:T(8,128)(2,1)S(1)}, u32[]{:S(2)}, u32[]{:S(2)}) collective-permute-start(bf16[8,96,128]{2,1,0:T(8,128)(2,1)S(1)} %maximum_maximum_fusion.refs_0_), channel_id=1, source_target_pairs={{0,32},{16,48},{32,0},{48,16},{1,33},{17,49},{33,1},{49,17},{2,34}... | collective-permute-start | bytes 589832 | tf_op jit(solution)/shard_map/ppermute | solution.py:245
  67.4 2.2 %collective-permute-start.5 = (bf16[8,96,128]{2,1,0:T(8,128)(2,1)S(1)}, bf16[8,96,128]{2,1,0:T(8,128)(2,1)S(1)}, u32[]{:S(2)}, u32[]{:S(2)}) collective-permute-start(bf16[8,96,128]{2,1,0:T(8,128)(2,1)S(1)} %maximum_maximum_fusion.refs_0_), channel_id=1, source_target_pairs={{0,16},{16,32},{32,48},{48,0},{1,17},{17,33},{33,49},{49,1},{2,18}... | collective-permute-start | bytes 589832 | tf_op jit(solution)/shard_map/ppermute | solution.py:245
  69.6 5.2 %collective-permute-start.6 = (bf16[8,96,128]{2,1,0:T(8,128)(2,1)S(1)}, bf16[8,96,128]{2,1,0:T(8,128)(2,1)S(1)}, u32[]{:S(2)}, u32[]{:S(2)}) collective-permute-start(bf16[8,96,128]{2,1,0:T(8,128)(2,1)S(1)} %maximum_maximum_fusion.refs_0_), channel_id=1, source_target_pairs={{0,48},{16,0},{32,16},{48,32},{1,49},{17,1},{33,17},{49,33},{2,50}... | collective-permute-start | bytes 589832 | tf_op jit(solution)/shard_map/ppermute | solution.py:245
  75.5 2.3 %collective-permute-start.2 = (f32[8,576]{1,0:T(8,128)S(1)}, f32[8,576]{1,0:T(8,128)S(1)}, u32[]{:S(2)}, u32[]{:S(2)}) collective-permute-start(f32[8,576]{1,0:T(8,128)S(1)} %convert_add_fusion.raw_a), channel_id=1, source_target_pairs={{0,1},{1,0},{2,3},{3,2},{4,5},{5,4},{6,7},{7,6},{8,9},{9,8},{10,11... | collective-permute-start | bytes 55304 | tf_op jit(solution)/shard_map/ppermute | solution.py:249
  77.8 5.1 %collective-permute-done.4.refs_0_ = bf16[8,96,128]{2,1,0:T(8,128)(2,1)S(1)} collective-permute-done((bf16[8,96,128]{2,1,0:T(8,128)(2,1)S(1)}, bf16[8,96,128]{2,1,0:T(8,128)(2,1)S(1)}, u32[]{:S(2)}, u32[]{:S(2)}) %collective-permute-start.4) | collective-permute-done | bytes 196640 | tf_op jit(solution)/shard_map/ppermute | solution.py:245
  82.9 6.0 %collective-permute-done.5.refs_1_ = bf16[8,96,128]{2,1,0:T(8,128)(2,1)S(1)} collective-permute-done((bf16[8,96,128]{2,1,0:T(8,128)(2,1)S(1)}, bf16[8,96,128]{2,1,0:T(8,128)(2,1)S(1)}, u32[]{:S(2)}, u32[]{:S(2)}) %collective-permute-start.5) | collective-permute-done | bytes 196640 | tf_op jit(solution)/shard_map/ppermute | solution.py:245
  89.0 2.8 %collective-permute-done.6.refs_2_ = bf16[8,96,128]{2,1,0:T(8,128)(2,1)S(1)} collective-permute-done((bf16[8,96,128]{2,1,0:T(8,128)(2,1)S(1)}, bf16[8,96,128]{2,1,0:T(8,128)(2,1)S(1)}, u32[]{:S(2)}, u32[]{:S(2)}) %collective-permute-start.6) | collective-permute-done | bytes 196640 | tf_op jit(solution)/shard_map/ppermute | solution.py:245
  91.7 11.6 %flash.3 = (bf16[528,128]{1,0:T(8,128)(2,1)S(1)}, bf16[528,128]{1,0:T(8,128)(2,1)S(1)}, bf16[528,128]{1,0:T(8,128)(2,1)S(1)}) custom-call(s32[1]{0:T(128)S(6)} %copy.17.start, bf16[8,96,128]{2,1,0:T(8,128)(2,1)S(1)} %collective-permute-done.4.refs_0_, bf16[8,96,128]{2,1,0:T(8,128)(2,1)S(1)} %collective-permute-done.5.refs_1_, ...), custom_call_target="tpu_custom_call" | custom-call | flops 5190451200 | bytes 4194304 | tf_op jit(solution)/shard_map/flash/pallas_call | solution.py:321
  103.3 3.2 %collective-permute-start.7 = (bf16[528,128]{1,0:T(8,128)(2,1)S(1)}, bf16[528,128]{1,0:T(8,128)(2,1)S(1)}, u32[]{:S(2)}, u32[]{:S(2)}) collective-permute-start(bf16[528,128]{1,0:T(8,128)(2,1)S(1)} %get-tuple-element.22), channel_id=1, source_target_pairs={{0,48},{16,0},{32,16},{48,32},{1,49},{17,1},{33,17},{49,33},{2,50}... | collective-permute-start | bytes 405512 | tf_op jit(solution)/shard_map/ppermute | solution.py:245
  106.6 6.9 %collective-permute-start.8 = (bf16[528,128]{1,0:T(8,128)(2,1)S(1)}, bf16[528,128]{1,0:T(8,128)(2,1)S(1)}, u32[]{:S(2)}, u32[]{:S(2)}) collective-permute-start(bf16[528,128]{1,0:T(8,128)(2,1)S(1)} %get-tuple-element.23), channel_id=1, source_target_pairs={{0,32},{16,48},{32,0},{48,16},{1,33},{17,49},{33,1},{49,17},{2,34}... | collective-permute-start | bytes 405512 | tf_op jit(solution)/shard_map/ppermute | solution.py:245
  113.4 1.9 %collective-permute-start.9 = (bf16[528,128]{1,0:T(8,128)(2,1)S(1)}, bf16[528,128]{1,0:T(8,128)(2,1)S(1)}, u32[]{:S(2)}, u32[]{:S(2)}) collective-permute-start(bf16[528,128]{1,0:T(8,128)(2,1)S(1)} %get-tuple-element.24), channel_id=1, source_target_pairs={{0,16},{16,32},{32,48},{48,0},{1,17},{17,33},{33,49},{49,1},{2,18}... | collective-permute-start | bytes 405512 | tf_op jit(solution)/shard_map/ppermute | solution.py:245
  115.4 0.6 copy-done.13
  116.0 2.7 %shard_map.133 = bf16[4,32,512]{2,1,0:T(8,128)(2,1)} custom-call(s32[4]{0:T(128)} %lengths.1, bf16[40,576]{1,0:T(8,128)(2,1)} %copy-done.5, bf16[80,576]{1,0:T(8,128)(2,1)} %copy-done.11, bf16[80,576]{1,0:T(8,128)(2,1)} %copy-done.10, f32[8,576]{1,0:T(8,128)} %copy-done.12, f32[8,576]{1,0:T(8,128)} %copy-done.13, bf16[512,576]{1,0:T(8,128)(2,1)} %bitcast.5.cache_ref, ...), custom_call_target="tpu_custom_call" | custom-call | flops 134217728 | bytes 1048576 | tf_op jit(solution)/shard_map/pallas_call | solution.py:133
  118.7 3.5 %all-to-all-start.2 = ((bf16[4,32,512]{2,1,0:T(8,128)(2,1)}), bf16[4,32,512]{2,1,0:T(8,128)(2,1)S(1)}, u32[]{:S(2)}, u32[]{:S(2)}) async-start(bf16[4,32,512]{2,1,0:T(8,128)(2,1)} %shard_map.133), calls=%async_computation.2 | async-start | bytes 262144 | tf_op jit(solution)/shard_map/all_to_all | solution.py:358
  122.2 5.1 %flash.2.a_ref = bf16[528,128]{1,0:T(8,128)(2,1)S(1)} custom-call(s32[1]{0:T(128)S(6)} %copy.17.start, bf16[8,96,128]{2,1,0:T(8,128)(2,1)S(1)} %maximum_maximum_fusion.refs_0_, bf16[8,96,576]{2,1,0:T(8,128)(2,1)} %all-to-all-done.refs_1_.refs_3_, bf16[8,96,576]{2,1,0:T(8,128)(2,1)} %collective-permute-done.3.refs_2_.refs_4_, ...), custom_call_target="tpu_custom_call" | custom-call | flops 1730150400 | bytes 4194304 | tf_op jit(solution)/shard_map/flash/pallas_call | solution.py:321
  127.3 1.0 shard_map.135
  128.3 1.3 %shard_map.134 = bf16[512,128]{1,0:T(8,128)(2,1)} custom-call(bf16[528,128]{1,0:T(8,128)(2,1)S(1)} %flash.2.a_ref, bf16[528,128]{1,0:T(8,128)(2,1)S(1)} %collective-permute-done.7.b_ref, bf16[528,128]{1,0:T(8,128)(2,1)S(1)} %collective-permute-done.8.c_ref, bf16[528,128]{1,0:T(8,128)(2,1)S(1)} %collective-permute-done.9.d_ref), custom_call_target="tpu_custom_call" | custom-call | flops 134217728 | bytes 1048576 | tf_op jit(solution)/shard_map/pallas_call | solution.py:133
  (37 shorter events, 0.2 us)
Async XLA Ops:
  0.6 0.9 copy-start.4
  1.5 12.1 %copy-start.8 = (s32[256]{0:T(256)S(1)}, s32[256]{0:T(256)}, u32[]{:S(2)}) copy-start(s32[256]{0:T(256)} %param.18) | copy-start | bytes 3076
  2.6 11.1 %copy-start = (bf16[256,4,576]{0,2,1:T(8,128)(2,1)S(1)}, bf16[256,4,576]{0,2,1:T(8,128)(2,1)}, u32[]{:S(2)}) copy-start(bf16[256,4,576]{0,2,1:T(8,128)(2,1)} %param.17) | copy-start | bytes 3538948
  2.6 41.3 %copy-start.3 = (bf16[896,576]{0,1:T(8,128)(2,1)S(1)}, bf16[896,576]{0,1:T(8,128)(2,1)}, u32[]{:S(2)}) copy-start(bf16[896,576]{0,1:T(8,128)(2,1)} %param.22) | copy-start | bytes 3096580
  2.6 38.9 %all-to-all-start = ((bf16[8,96,576]{2,1,0:T(8,128)(2,1)}), bf16[8,96,576]{2,1,0:T(8,128)(2,1)}, u32[]{:S(2)}, u32[]{:S(2)}) async-start(bf16[8,96,576]{2,1,0:T(8,128)(2,1)} %spread.1), calls=%async_computation | async-start | bytes 1966080 | tf_op jit(solution)/shard_map/all_to_all | solution.py:282
  13.6 30.3 %copy-start.2 = (bf16[8,128,512]{2,1,0:T(8,128)(2,1)S(1)}, bf16[8,128,512]{2,1,0:T(8,128)(2,1)}, u32[]{:S(2)}) copy-start(bf16[8,128,512]{2,1,0:T(8,128)(2,1)} %refs_5_.1) | copy-start | bytes 3145732
  13.6 30.3 %copy-start.6 = (bf16[4,4,8,192]{3,2,1,0:T(8,128)(2,1)S(1)}, bf16[4,4,8,192]{3,2,1,0:T(8,128)(2,1)}, u32[]{:S(2)}) copy-start(bf16[4,4,8,192]{3,2,1,0:T(8,128)(2,1)} %q_ref.1) | copy-start | bytes 147460
  13.6 30.3 %copy-start.7 = (bf16[4,4,896]{2,1,0:T(4,128)(2,1)S(1)}, bf16[4,4,896]{2,1,0:T(4,128)(2,1)}, u32[]{:S(2)}) copy-start(bf16[4,4,896]{2,1,0:T(4,128)(2,1)} %hid_ref.1) | copy-start | bytes 86020
  15.5 34.0 %copy-start.9 = (bf16[64,8,192]{2,1,0:T(8,128)(2,1)S(1)}, bf16[64,8,192]{2,1,0:T(8,128)(2,1)}, u32[]{:S(2)}) copy-start(bf16[64,8,192]{2,1,0:T(8,128)(2,1)} %param.13) | copy-start | bytes 589828
  41.5 50.3 %collective-permute-start.3 = (bf16[8,96,576]{2,1,0:T(8,128)(2,1)}, bf16[8,96,576]{2,1,0:T(8,128)(2,1)}, u32[]{:S(2)}, u32[]{:S(2)}) collective-permute-start(bf16[8,96,576]{2,1,0:T(8,128)(2,1)} %all-to-all-done.refs_1_.refs_3_), channel_id=1, source_target_pairs={{0,8},{8,0},{1,9},{9,1},{2,10},{10,2},{3,11},{11,3},{4,12},{12,4},... | collective-permute-start | bytes 2654216 | tf_op jit(solution)/shard_map/ppermute | solution.py:245
  44.7 30.7 %copy-start.5 = (bf16[40,576]{1,0:T(8,128)(2,1)}, bf16[40,576]{1,0:T(8,128)(2,1)S(1)}, u32[]{:S(2)}) copy-start(bf16[40,576]{1,0:T(8,128)(2,1)S(1)} %get-tuple-element.14.p0) | copy-start | bytes 138244
  44.7 13.1 %collective-permute-start = (bf16[80,576]{1,0:T(8,128)(2,1)S(1)}, bf16[80,576]{1,0:T(8,128)(2,1)S(1)}, u32[]{:S(2)}, u32[]{:S(2)}) collective-permute-start(bf16[80,576]{1,0:T(8,128)(2,1)S(1)} %get-tuple-element.16), channel_id=1, source_target_pairs={{0,4},{2,6},{4,0},{6,2},{1,5},{3,7},{5,1},{7,3},{8,12},{10,14},{12... | collective-permute-start | bytes 276488 | tf_op jit(solution)/shard_map/ppermute | solution.py:249
  49.5 42.2 %copy-start.1 = (bf16[8,512,128]{2,1,0:T(8,128)(2,1)S(1)}, bf16[8,512,128]{2,1,0:T(8,128)(2,1)}, u32[]{:S(2)}) copy-start(bf16[8,512,128]{2,1,0:T(8,128)(2,1)} %wuv_ref.1) | copy-start | bytes 3145732
  49.5 65.9 %all-to-all-start.1 = ((bf16[64,8,576]{2,1,0:T(8,128)(2,1)}), bf16[64,8,576]{2,1,0:T(8,128)(2,1)}, u32[]{:S(2)}, u32[]{:S(2)}) async-start(bf16[64,8,576]{2,1,0:T(8,128)(2,1)} %bitcast.4), calls=%async_computation.1 | async-start | bytes 1310720 | tf_op jit(solution)/shard_map/all_to_all | solution.py:315
  57.8 45.5 %copy-start.10 = (bf16[80,576]{1,0:T(8,128)(2,1)}, bf16[80,576]{1,0:T(8,128)(2,1)S(1)}, u32[]{:S(2)}) copy-start(bf16[80,576]{1,0:T(8,128)(2,1)S(1)} %collective-permute-done.p2) | copy-start | bytes 276484
  57.9 17.6 %collective-permute-start.1 = (bf16[80,576]{1,0:T(8,128)(2,1)S(1)}, bf16[80,576]{1,0:T(8,128)(2,1)S(1)}, u32[]{:S(2)}, u32[]{:S(2)}) collective-permute-start(bf16[80,576]{1,0:T(8,128)(2,1)S(1)} %pad_maximum_fusion), channel_id=1, source_target_pairs={{0,2},{2,0},{4,6},{6,4},{1,3},{3,1},{5,7},{7,5},{8,10},{10,8},{12,... | collective-permute-start | bytes 276488 | tf_op jit(solution)/shard_map/ppermute | solution.py:249
  60.2 22.7 %collective-permute-start.4 = (bf16[8,96,128]{2,1,0:T(8,128)(2,1)S(1)}, bf16[8,96,128]{2,1,0:T(8,128)(2,1)S(1)}, u32[]{:S(2)}, u32[]{:S(2)}) collective-permute-start(bf16[8,96,128]{2,1,0:T(8,128)(2,1)S(1)} %maximum_maximum_fusion.refs_0_), channel_id=1, source_target_pairs={{0,32},{16,48},{32,0},{48,16},{1,33},{17,49},{33,1},{49,17},{2,34}... | collective-permute-start | bytes 589832 | tf_op jit(solution)/shard_map/ppermute | solution.py:245
  67.4 21.6 %collective-permute-start.5 = (bf16[8,96,128]{2,1,0:T(8,128)(2,1)S(1)}, bf16[8,96,128]{2,1,0:T(8,128)(2,1)S(1)}, u32[]{:S(2)}, u32[]{:S(2)}) collective-permute-start(bf16[8,96,128]{2,1,0:T(8,128)(2,1)S(1)} %maximum_maximum_fusion.refs_0_), channel_id=1, source_target_pairs={{0,16},{16,32},{32,48},{48,0},{1,17},{17,33},{33,49},{49,1},{2,18}... | collective-permute-start | bytes 589832 | tf_op jit(solution)/shard_map/ppermute | solution.py:245
  69.6 22.1 %collective-permute-start.6 = (bf16[8,96,128]{2,1,0:T(8,128)(2,1)S(1)}, bf16[8,96,128]{2,1,0:T(8,128)(2,1)S(1)}, u32[]{:S(2)}, u32[]{:S(2)}) collective-permute-start(bf16[8,96,128]{2,1,0:T(8,128)(2,1)S(1)} %maximum_maximum_fusion.refs_0_), channel_id=1, source_target_pairs={{0,48},{16,0},{32,16},{48,32},{1,49},{17,1},{33,17},{49,33},{2,50}... | collective-permute-start | bytes 589832 | tf_op jit(solution)/shard_map/ppermute | solution.py:245
  75.5 27.8 %copy-start.11 = (bf16[80,576]{1,0:T(8,128)(2,1)}, bf16[80,576]{1,0:T(8,128)(2,1)S(1)}, u32[]{:S(2)}) copy-start(bf16[80,576]{1,0:T(8,128)(2,1)S(1)} %collective-permute-done.1.p13) | copy-start | bytes 276484
  75.5 27.8 %copy-start.12 = (f32[8,576]{1,0:T(8,128)}, f32[8,576]{1,0:T(8,128)S(1)}, u32[]{:S(2)}) copy-start(f32[8,576]{1,0:T(8,128)S(1)} %convert_add_fusion.raw_a) | copy-start | bytes 55300
  75.5 39.9 %collective-permute-start.2 = (f32[8,576]{1,0:T(8,128)S(1)}, f32[8,576]{1,0:T(8,128)S(1)}, u32[]{:S(2)}, u32[]{:S(2)}) collective-permute-start(f32[8,576]{1,0:T(8,128)S(1)} %convert_add_fusion.raw_a), channel_id=1, source_target_pairs={{0,1},{1,0},{2,3},{3,2},{4,5},{5,4},{6,7},{7,6},{8,9},{9,8},{10,11... | collective-permute-start | bytes 55304 | tf_op jit(solution)/shard_map/ppermute | solution.py:249
  103.3 25.0 %collective-permute-start.7 = (bf16[528,128]{1,0:T(8,128)(2,1)S(1)}, bf16[528,128]{1,0:T(8,128)(2,1)S(1)}, u32[]{:S(2)}, u32[]{:S(2)}) collective-permute-start(bf16[528,128]{1,0:T(8,128)(2,1)S(1)} %get-tuple-element.22), channel_id=1, source_target_pairs={{0,48},{16,0},{32,16},{48,32},{1,49},{17,1},{33,17},{49,33},{2,50}... | collective-permute-start | bytes 405512 | tf_op jit(solution)/shard_map/ppermute | solution.py:245
  106.6 21.8 %collective-permute-start.8 = (bf16[528,128]{1,0:T(8,128)(2,1)S(1)}, bf16[528,128]{1,0:T(8,128)(2,1)S(1)}, u32[]{:S(2)}, u32[]{:S(2)}) collective-permute-start(bf16[528,128]{1,0:T(8,128)(2,1)S(1)} %get-tuple-element.23), channel_id=1, source_target_pairs={{0,32},{16,48},{32,0},{48,16},{1,33},{17,49},{33,1},{49,17},{2,34}... | collective-permute-start | bytes 405512 | tf_op jit(solution)/shard_map/ppermute | solution.py:245
  113.4 14.9 %collective-permute-start.9 = (bf16[528,128]{1,0:T(8,128)(2,1)S(1)}, bf16[528,128]{1,0:T(8,128)(2,1)S(1)}, u32[]{:S(2)}, u32[]{:S(2)}) collective-permute-start(bf16[528,128]{1,0:T(8,128)(2,1)S(1)} %get-tuple-element.24), channel_id=1, source_target_pairs={{0,16},{16,32},{32,48},{48,0},{1,17},{17,33},{33,49},{49,1},{2,18}... | collective-permute-start | bytes 405512 | tf_op jit(solution)/shard_map/ppermute | solution.py:245
  115.4 0.6 copy-start.13
  118.7 8.6 %all-to-all-start.2 = ((bf16[4,32,512]{2,1,0:T(8,128)(2,1)}), bf16[4,32,512]{2,1,0:T(8,128)(2,1)S(1)}, u32[]{:S(2)}, u32[]{:S(2)}) async-start(bf16[4,32,512]{2,1,0:T(8,128)(2,1)} %shard_map.133), calls=%async_computation.2 | async-start | bytes 262144 | tf_op jit(solution)/shard_map/all_to_all | solution.py:358

commit v3 on v2

--- a/solution.py
+++ b/solution.py
@@ -28,16 +28,16 @@
 
 def flash_kernel(offsets, start, *refs):
     count = len(offsets)
-    moved, (wuk_ref, wuv_ref), targets = refs[: count + 2], refs[count + 2 : count + 4], refs[count + 4 : 2 * count + 4]
-    held, out_held, sems = refs[2 * count + 4 : 3 * count + 6], refs[3 * count + 6 : -1], refs[-1]
+    moved, targets = refs[: count + 4], refs[count + 4 : 2 * count + 4]
+    held, out_held, sems = refs[2 * count + 4 : 3 * count + 8], refs[3 * count + 8 : -1], refs[-1]
     loads = [pltpu.make_async_copy(m, h, sems.at[i]) for i, (m, h) in enumerate(zip(moved, held))]
-    for load in (loads[0], *loads[count:], *loads[1:count]):
-        load.start()
+    for at in (0, count + 2, count, count + 1, *range(1, count), count + 3):
+        loads[at].start()
     queries, outs = dict(zip(offsets, held[:count])), dict(zip(offsets, out_held))
-    k1_ref, k2_ref = held[count:]
+    k1_ref, k2_ref, wuk_ref, wuv_ref = held[count:]
     stores = []
     z, yh, c = lax.axis_index("z"), lax.axis_index("yh"), lax.axis_index("c")
-    waits = dict(zip((*offsets, "k1", "k2"), loads))
+    waits = dict(zip((*offsets, "k1", "k2", "wuk", "wuv"), loads))
     ready = {}
 
     def key_rows(name, ref):
@@ -55,6 +55,8 @@
     def score(k):
         rows = []
         waits[k].wait()
+        if k == offsets[0]:
+            waits["wuk"].wait()
         for h in range(8):
             pair = queries[k][h, 64:, :]
             rope = jnp.concatenate([pair[:, :64], pair[:, 64:]], axis=0)
@@ -66,7 +68,7 @@
         return s1, s2
 
     def weigh(k, s):
-        source = (yh + (4 - k)) & 3
+        source = yh ^ k
         first = start[0] + ((z * 4 + source) * 2 + c) * 64
         qpos = first + (lax.broadcasted_iota(jnp.int32, (512, 1), 0) & 63)
         s1 = jnp.where(where1 <= qpos, s[0], -1e30)
@@ -79,6 +81,8 @@
         return p1.astype(jnp.bfloat16), p2.astype(jnp.bfloat16), total, lse
 
     def mix(k, p1, p2, total, lse):
+        if k == offsets[0]:
+            waits["wuv"].wait()
         acc = jnp.dot(p1, ready["k1"][:, :KV_RANK], preferred_element_type=jnp.float32)
         acc = acc + jnp.dot(p2, ready["k2"][:, :KV_RANK], preferred_element_type=jnp.float32)
         mixed = (acc * (1.0 / total)).astype(jnp.bfloat16)
@@ -95,7 +99,7 @@
     for n, k in enumerate(offsets):
         following = score(offsets[n + 1]) if n + 1 < count else None
         mix(k, *weigh(k, s))
-        store = pltpu.make_async_copy(outs[k], targets[n], sems.at[count + 2 + n])
+        store = pltpu.make_async_copy(outs[k], targets[n], sems.at[count + 4 + n])
         store.start()
         stores.append(store)
         s = following
@@ -199,18 +203,21 @@
         move.wait()
 
 
-def attend_kernel(lengths, p0, p13, p2, raw_a, raw_b, cache_ref, gain_ref, out_ref):
+def attend_kernel(p0, p13, p2, raw_a, raw_b, cache_ref, out_ref):
+    lane = lax.broadcasted_iota(jnp.int32, (1, KV_RANK + ROPE), 1)
+    length = jnp.where(lane == lax.axis_index("x"), raw_a[6:7, :], 0.0)
+    length = jnp.sum(length, axis=1, keepdims=True).astype(jnp.int32)
     raw = raw_a[...] + raw_b[...]
     front = raw[:, :KV_RANK]
     factor = lax.rsqrt(jnp.mean(front * front, axis=1, keepdims=True) + 1e-06)
-    fresh = jnp.concatenate([front * factor * gain_ref[...], raw[:, KV_RANK:]], axis=1)
+    fresh = jnp.concatenate([front * factor * raw_a[5:6, :KV_RANK], raw[:, KV_RANK:]], axis=1)
     fresh = fresh.astype(jnp.bfloat16)
     q = jnp.concatenate([p0[:32], p13[:32], p2[:32], p13[40:72]], axis=0)
     cache = cache_ref[...]
     s1 = lax.dot_general(q, cache, NT, preferred_element_type=jnp.float32)
     s2 = lax.dot_general(q, fresh, NT, preferred_element_type=jnp.float32)
     j = lax.broadcasted_iota(jnp.int32, (128, 512), 1)
-    held = ((j & 7) < 4) & ((j >> 3) * 4 + (j & 7) < lengths[lax.axis_index("x")])
+    held = ((j & 7) < 4) & ((j >> 3) * 4 + (j & 7) < length)
     s1 = jnp.where(held, s1, -1e30)
     step = (lax.broadcasted_iota(jnp.int32, (128, 8), 0) >> 3) & 3
     s2 = jnp.where(lax.broadcasted_iota(jnp.int32, (128, 8), 1) <= step, s2, -1e30)
@@ -239,10 +246,6 @@
         for s in range(4):
             at = (r * 4 + s) * 8
             out_ref[s, r] = acc[at : at + 8].astype(jnp.bfloat16)
-
-
-def shift(v, axis, k, n):
-    return lax.ppermute(v, axis, [(i, (i + k) % n) for i in range(n)])
 
 
 def trade(v, axis, k, n):
@@ -288,7 +291,7 @@
     )
     visiting = [packed] + [None] * 3
     for k in (2, 1, 3):
-        visiting[k] = shift(packed, "yh", k, 4)
+        visiting[k] = trade(packed, "yh", k, 4)
     tile = jax.ShapeDtypeStruct((40, width), bf)
     near, following, far_two = small(
         prep_kernel,
@@ -303,6 +306,8 @@
     got = (near, from_one, from_two)
     raw_here = near[32:].astype(jnp.float32) + from_two[32:40].astype(jnp.float32)
     raw_here = raw_here + from_one[32:40].astype(jnp.float32) + from_one[72:].astype(jnp.float32)
+    raw_here = raw_here + jnp.pad(kv_gain[None], ((5, 2), (0, width - KV_RANK)))
+    raw_here = raw_here + jnp.pad(lengths.astype(jnp.float32)[None], ((6, 1), (0, width - 4)))
     raw_there = trade(raw_here, "yl", 1, 2)
     rows = small(
         pack_kernel,
@@ -311,22 +316,22 @@
     ).reshape(64, 8, width)
 
     keys, rows = fence((keys, rows))
-    other_keys = shift(keys, "c", 1, 2)
+    other_keys = trade(keys, "c", 1, 2)
     cache = lax.all_to_all(rows, CTX, 0, 0, tiled=True)
 
     def flash(offsets, chunks):
         count = len(offsets)
         chunk, key = pltpu.VMEM((8, 96, 128), bf), pltpu.VMEM((8, 96, width), bf)
-        vmem = pl.BlockSpec(memory_space=pltpu.VMEM)
         return pl.pallas_call(
             functools.partial(flash_kernel, offsets),
             out_shape=[jax.ShapeDtypeStruct((512 + 16, 128), bf)] * count,
-            in_specs=[pl.BlockSpec(memory_space=pltpu.SMEM)] + [hbm] * (count + 2) + [vmem] * 2,
+            in_specs=[pl.BlockSpec(memory_space=pltpu.SMEM)] + [hbm] * (count + 4),
             out_specs=[hbm] * count,
             scratch_shapes=[chunk] * count
             + [key] * 2
+            + [pltpu.VMEM(w_uk.shape, bf), pltpu.VMEM(w_uv.shape, bf)]
             + [pltpu.VMEM((512 + 16, 128), bf)] * count
-            + [pltpu.SemaphoreType.DMA((2 * count + 2,))],
+            + [pltpu.SemaphoreType.DMA((2 * count + 4,))],
             compiler_params=pltpu.CompilerParams(vmem_limit_bytes=28 << 20),
             cost_estimate=pl.CostEstimate(
                 flops=count * 2 * 512 * 1536 * 1100, bytes_accessed=4 << 20, transcendentals=1 << 20
@@ -338,21 +343,12 @@
     sending = flash(far, [visiting[k] for k in far])
     parts = [None] * 4
     for k, piece in zip(far, sending):
-        parts[k] = shift(piece, "yh", 4 - k, 4)
+        parts[k] = trade(piece, "yh", k, 4)
 
     mixed = small(
         attend_kernel,
         jax.ShapeDtypeStruct((4, 32, KV_RANK), bf),
-        [
-            lengths,
-            *got,
-            raw_here,
-            raw_there,
-            cache.reshape(512, width),
-            kv_gain.reshape(1, KV_RANK),
-        ],
-        1,
-        limit=60,
+        [*got, raw_here, raw_there, cache.reshape(512, width)],
     )
     own, mixed = fence((packed, mixed))
     mixed = lax.all_to_all(mixed, "x", 0, 0, tiled=True)

time: 131 us -> 125 us (0.954)
  waiting for transfers between devices: 39.9 us -> 36.1 us
  starting transfers between devices: 60.9 us -> 58.8 us
    ppermute x7 -> x0, starting transfers between devices: 29 us -> none  [shift(): return lax.ppermute(v, axis, [(i, (i + k) % n) for i in range(n)])]
    ppermute x3 -> x10, starting transfers between devices: 9.19 us -> 36 us  [trade(): return lax.ppermute(v, axis, [(i, i ^ k) for i in range(n)])]
    ppermute x3 -> x10, waiting for transfers between devices: 0.01 us -> 16.4 us  [trade(): return lax.ppermute(v, axis, [(i, i ^ k) for i in range(n)])]
    ppermute x7 -> x0, waiting for transfers between devices: 13.9 us -> none  [shift(): return lax.ppermute(v, axis, [(i, (i + k) % n) for i in range(n)])]
    all_to_all x1, waiting for transfers between devices: 26 us -> 19.7 us  [layer(): keys = lax.all_to_all(spread, 'z', 0, 0, tiled=True)]
where the time goes in v3:
time: 125 us; the launch traced here: 124 us
  starting transfers between devices  58.8 us (47%)
  waiting for transfers between devices  36.1 us (29%)
  Pallas kernels  25.9 us (21%)
  between operations  1.6 us (1%)
    ppermute x10, starting transfers between devices, trade(): return lax.ppermute(v, axis, [(i, i ^ k) for i in range(n)])  36 us
    all_to_all x1, waiting for transfers between devices, layer(): keys = lax.all_to_all(spread, 'z', 0, 0, tiled=True)  19.7 us
    pallas_call x2, Pallas kernels, flash(): pl.pallas_call(functools.partial(flash_kernel, offsets), out_shape=[jax.S...  16.8 us
    ppermute x10, waiting for transfers between devices, trade(): return lax.ppermute(v, axis, [(i, i ^ k) for i in range(n)])  16.4 us
    all_to_all x1, starting transfers between devices, layer(): keys = lax.all_to_all(spread, 'z', 0, 0, tiled=True)  11 us
    pallas_call x5, Pallas kernels, small(): pl.pallas_call(kernel, out_shape=outs, in_specs=[sm] * scalars + [vm] * (...  8.09 us
    all_to_all x1, starting transfers between devices, layer(): cache = lax.all_to_all(rows, CTX, 0, 0, tiled=True)  7.78 us
    all_to_all x1, starting transfers between devices, layer(): mixed = lax.all_to_all(mixed, 'x', 0, 0, tiled=True)  4.03 us
  transfers between devices with their start and end apart: 13, of which 4 were waited for; matrix products, arithmetic and copies ran while one was open for 0% of the time, Pallas kernels for 18%

profile of v3, /device:TPU:1, one launch (start us, length us, event | category | flops | bytes accessed | tf_op | source)
XLA Modules:
  0.0 123.6 jit_solution(11460821150817584029)
XLA Ops:
  0.6 0.9 copy-done.4
  1.5 1.0 spread.1
  2.6 0.0 copy-start.2
  2.6 0.0 copy-start.5
  2.6 0.0 copy-start.6
  2.6 11.0 %all-to-all-start = ((bf16[8,96,576]{2,1,0:T(8,128)(2,1)}), bf16[8,96,576]{2,1,0:T(8,128)(2,1)}, u32[]{:S(2)}, u32[]{:S(2)}) async-start(bf16[8,96,576]{2,1,0:T(8,128)(2,1)} %spread.1), calls=%async_computation | async-start | bytes 1966080 | tf_op jit(solution)/shard_map/all_to_all | solution.py:285
  13.6 0.0 copy-start
  13.7 0.0 copy-start.7
  13.7 1.5 %shard_map.131 = (bf16[40,576]{1,0:T(8,128)(2,1)S(1)}, bf16[40,576]{1,0:T(8,128)(2,1)S(1)}, bf16[80,576]{1,0:T(8,128)(2,1)}) custom-call(bf16[4,4,8,192]{3,2,1,0:T(8,128)(2,1)S(1)} %copy-done.5, bf16[8,128,512]{2,1,0:T(8,128)(2,1)S(1)} %copy-done.2, bf16[4,4,896]{2,1,0:T(4,128)(2,1)S(1)} %copy-done.6, bf16[576,896]{1,0:T(8,128)(2,1)S(1)} %bitcast.14), custom_call_target="tpu_custom_call" | custom-call | flops 134217728 | bytes 1048576 | tf_op jit(solution)/shard_map/pallas_call | solution.py:137
  15.1 4.6 %collective-permute-start = (bf16[80,576]{1,0:T(8,128)(2,1)}, bf16[80,576]{1,0:T(8,128)(2,1)S(1)}, u32[]{:S(2)}, u32[]{:S(2)}) collective-permute-start(bf16[80,576]{1,0:T(8,128)(2,1)} %get-tuple-element.16), channel_id=1, source_target_pairs={{0,4},{2,6},{4,0},{6,2},{1,5},{3,7},{5,1},{7,3},{8,12},{10,14},{12... | collective-permute-start | bytes 276488 | tf_op jit(solution)/shard_map/ppermute | solution.py:252
  19.9 1.8 %shard_map.132 = bf16[512,576]{1,0:T(8,128)(2,1)} custom-call(s32[1,256]{1,0:T(1,128)S(1)} %bitcast.15, bf16[4,576,256]{2,1,0:T(8,128)(2,1)S(1)} %bitcast.13), custom_call_target="tpu_custom_call" | custom-call | flops 134217728 | bytes 1048576 | tf_op jit(solution)/shard_map/pallas_call | solution.py:137
  21.8 19.7 %all-to-all-done.refs_1_.refs_3_ = bf16[8,96,576]{2,1,0:T(8,128)(2,1)} async-done(((bf16[8,96,576]{2,1,0:T(8,128)(2,1)}), bf16[8,96,576]{2,1,0:T(8,128)(2,1)}, u32[]{:S(2)}, u32[]{:S(2)}) %all-to-all-start) | async-done | bytes 884768 | tf_op jit(solution)/shard_map/all_to_all | solution.py:285
  41.5 2.5 %collective-permute-start.3 = (bf16[8,96,576]{2,1,0:T(8,128)(2,1)}, bf16[8,96,576]{2,1,0:T(8,128)(2,1)}, u32[]{:S(2)}, u32[]{:S(2)}) collective-permute-start(bf16[8,96,576]{2,1,0:T(8,128)(2,1)} %all-to-all-done.refs_1_.refs_3_), channel_id=1, source_target_pairs={{0,8},{8,0},{1,9},{9,1},{2,10},{10,2},{3,11},{11,3},{4,12},{12,4},... | collective-permute-start | bytes 2654216 | tf_op jit(solution)/shard_map/ppermute | solution.py:252
  44.1 7.8 %all-to-all-start.1 = ((bf16[64,8,576]{2,1,0:T(8,128)(2,1)}), bf16[64,8,576]{2,1,0:T(8,128)(2,1)S(1)}, u32[]{:S(2)}, u32[]{:S(2)}) async-start(bf16[64,8,576]{2,1,0:T(8,128)(2,1)} %bitcast.6), calls=%async_computation.1 | async-start | bytes 1310720 | tf_op jit(solution)/shard_map/all_to_all | solution.py:320
  51.9 0.1 maximum_maximum_fusion.refs_0_
  52.0 7.2 %collective-permute-start.4 = (bf16[8,96,128]{2,1,0:T(8,128)(2,1)S(1)}, bf16[8,96,128]{2,1,0:T(8,128)(2,1)S(1)}, u32[]{:S(2)}, u32[]{:S(2)}) collective-permute-start(bf16[8,96,128]{2,1,0:T(8,128)(2,1)S(1)} %maximum_maximum_fusion.refs_0_), channel_id=1, source_target_pairs={{0,32},{16,48},{32,0},{48,16},{1,33},{17,49},{33,1},{49,17},{2,34}... | collective-permute-start | bytes 589832 | tf_op jit(solution)/shard_map/ppermute | solution.py:252
  59.1 2.2 %collective-permute-start.5 = (bf16[8,96,128]{2,1,0:T(8,128)(2,1)S(1)}, bf16[8,96,128]{2,1,0:T(8,128)(2,1)S(1)}, u32[]{:S(2)}, u32[]{:S(2)}) collective-permute-start(bf16[8,96,128]{2,1,0:T(8,128)(2,1)S(1)} %maximum_maximum_fusion.refs_0_), channel_id=1, source_target_pairs={{0,16},{16,0},{32,48},{48,32},{1,17},{17,1},{33,49},{49,33},{2,18}... | collective-permute-start | bytes 589832 | tf_op jit(solution)/shard_map/ppermute | solution.py:252
  61.3 2.0 %collective-permute-start.6 = (bf16[8,96,128]{2,1,0:T(8,128)(2,1)S(1)}, bf16[8,96,128]{2,1,0:T(8,128)(2,1)S(1)}, u32[]{:S(2)}, u32[]{:S(2)}) collective-permute-start(bf16[8,96,128]{2,1,0:T(8,128)(2,1)S(1)} %maximum_maximum_fusion.refs_0_), channel_id=1, source_target_pairs={{0,48},{16,32},{32,16},{48,0},{1,49},{17,33},{33,17},{49,1},{2,50}... | collective-permute-start | bytes 589832 | tf_op jit(solution)/shard_map/ppermute | solution.py:252
  63.4 3.1 %collective-permute-start.1 = (bf16[80,576]{1,0:T(8,128)(2,1)S(1)}, bf16[80,576]{1,0:T(8,128)(2,1)S(1)}, u32[]{:S(2)}, u32[]{:S(2)}) collective-permute-start(bf16[80,576]{1,0:T(8,128)(2,1)S(1)} %pad_maximum_fusion), channel_id=1, source_target_pairs={{0,2},{2,0},{4,6},{6,4},{1,3},{3,1},{5,7},{7,5},{8,10},{10,8},{12,... | collective-permute-start | bytes 276488 | tf_op jit(solution)/shard_map/ppermute | solution.py:252
  67.2 1.9 %collective-permute-done.1.p13 = bf16[80,576]{1,0:T(8,128)(2,1)S(1)} collective-permute-done((bf16[80,576]{1,0:T(8,128)(2,1)S(1)}, bf16[80,576]{1,0:T(8,128)(2,1)S(1)}, u32[]{:S(2)}, u32[]{:S(2)}) %collective-permute-start.1) | collective-permute-done | bytes 92192 | tf_op jit(solution)/shard_map/ppermute | solution.py:252
  69.1 2.3 %collective-permute-start.2 = (f32[8,576]{1,0:T(8,128)S(1)}, f32[8,576]{1,0:T(8,128)S(1)}, u32[]{:S(2)}, u32[]{:S(2)}) collective-permute-start(f32[8,576]{1,0:T(8,128)S(1)} %pad_add_fusion.raw_a), channel_id=1, source_target_pairs={{0,1},{1,0},{2,3},{3,2},{4,5},{5,4},{6,7},{7,6},{8,9},{9,8},{10,11... | collective-permute-start | bytes 55304 | tf_op jit(solution)/shard_map/ppermute | solution.py:252
  71.4 5.1 %collective-permute-done.4.refs_0_ = bf16[8,96,128]{2,1,0:T(8,128)(2,1)S(1)} collective-permute-done((bf16[8,96,128]{2,1,0:T(8,128)(2,1)S(1)}, bf16[8,96,128]{2,1,0:T(8,128)(2,1)S(1)}, u32[]{:S(2)}, u32[]{:S(2)}) %collective-permute-start.4) | collective-permute-done | bytes 196640 | tf_op jit(solution)/shard_map/ppermute | solution.py:252
  76.6 9.3 %collective-permute-done.5.refs_1_ = bf16[8,96,128]{2,1,0:T(8,128)(2,1)S(1)} collective-permute-done((bf16[8,96,128]{2,1,0:T(8,128)(2,1)S(1)}, bf16[8,96,128]{2,1,0:T(8,128)(2,1)S(1)}, u32[]{:S(2)}, u32[]{:S(2)}) %collective-permute-start.5) | collective-permute-done | bytes 196640 | tf_op jit(solution)/shard_map/ppermute | solution.py:252
  85.9 11.4 %flash.3 = (bf16[528,128]{1,0:T(8,128)(2,1)}, bf16[528,128]{1,0:T(8,128)(2,1)}, bf16[528,128]{1,0:T(8,128)(2,1)}) custom-call(s32[1]{0:T(128)S(6)} %copy.17.start, bf16[8,96,128]{2,1,0:T(8,128)(2,1)S(1)} %collective-permute-done.4.refs_0_, bf16[8,96,128]{2,1,0:T(8,128)(2,1)S(1)} %collective-permute-done.5.refs_1_, ...), custom_call_target="tpu_custom_call" | custom-call | flops 5190451200 | bytes 4194304 | tf_op jit(solution)/shard_map/flash/pallas_call | solution.py:325
  97.3 4.9 %collective-permute-start.7 = (bf16[528,128]{1,0:T(8,128)(2,1)}, bf16[528,128]{1,0:T(8,128)(2,1)S(1)}, u32[]{:S(2)}, u32[]{:S(2)}) collective-permute-start(bf16[528,128]{1,0:T(8,128)(2,1)} %get-tuple-element.22), channel_id=1, source_target_pairs={{0,16},{16,0},{32,48},{48,32},{1,17},{17,1},{33,49},{49,33},{2,18}... | collective-permute-start | bytes 405512 | tf_op jit(solution)/shard_map/ppermute | solution.py:252
  102.1 2.3 %collective-permute-start.8 = (bf16[528,128]{1,0:T(8,128)(2,1)}, bf16[528,128]{1,0:T(8,128)(2,1)S(1)}, u32[]{:S(2)}, u32[]{:S(2)}) collective-permute-start(bf16[528,128]{1,0:T(8,128)(2,1)} %get-tuple-element.23), channel_id=1, source_target_pairs={{0,32},{16,48},{32,0},{48,16},{1,33},{17,49},{33,1},{49,17},{2,34}... | collective-permute-start | bytes 405512 | tf_op jit(solution)/shard_map/ppermute | solution.py:252
  104.5 4.8 %collective-permute-start.9 = (bf16[528,128]{1,0:T(8,128)(2,1)}, bf16[528,128]{1,0:T(8,128)(2,1)}, u32[]{:S(2)}, u32[]{:S(2)}) collective-permute-start(bf16[528,128]{1,0:T(8,128)(2,1)} %get-tuple-element.24), channel_id=1, source_target_pairs={{0,48},{16,32},{32,16},{48,0},{1,49},{17,33},{33,17},{49,1},{2,50}... | collective-permute-start | bytes 405512 | tf_op jit(solution)/shard_map/ppermute | solution.py:252
  109.3 1.5 %shard_map.133 = bf16[4,32,512]{2,1,0:T(8,128)(2,1)} custom-call(bf16[40,576]{1,0:T(8,128)(2,1)S(1)} %get-tuple-element.14.p0, bf16[80,576]{1,0:T(8,128)(2,1)S(1)} %collective-permute-done.1.p13, bf16[80,576]{1,0:T(8,128)(2,1)S(1)} %collective-permute-done.p2, f32[8,576]{1,0:T(8,128)S(1)} %pad_add_fusion.raw_a, f32[8,576]{1,0:T(8,128)S(1)} %collective-permute-done.2.raw_b, ...), custom_call_target="tpu_custom_call" | custom-call | flops 134217728 | bytes 1048576 | tf_op jit(solution)/shard_map/pallas_call | solution.py:137
  110.8 4.0 %all-to-all-start.2 = ((bf16[4,32,512]{2,1,0:T(8,128)(2,1)}), bf16[4,32,512]{2,1,0:T(8,128)(2,1)S(1)}, u32[]{:S(2)}, u32[]{:S(2)}) async-start(bf16[4,32,512]{2,1,0:T(8,128)(2,1)} %shard_map.133), calls=%async_computation.2 | async-start | bytes 262144 | tf_op jit(solution)/shard_map/all_to_all | solution.py:354
  114.8 5.4 %flash.2.a_ref = bf16[528,128]{1,0:T(8,128)(2,1)S(1)} custom-call(s32[1]{0:T(128)S(6)} %copy.17.start, bf16[8,96,128]{2,1,0:T(8,128)(2,1)S(1)} %maximum_maximum_fusion.refs_0_, bf16[8,96,576]{2,1,0:T(8,128)(2,1)} %all-to-all-done.refs_1_.refs_3_, bf16[8,96,576]{2,1,0:T(8,128)(2,1)} %collective-permute-done.3.refs_2_.refs_4_, ...), custom_call_target="tpu_custom_call" | custom-call | flops 1730150400 | bytes 4194304 | tf_op jit(solution)/shard_map/flash/pallas_call | solution.py:325
  120.3 1.0 shard_map.135
  121.3 2.2 %shard_map.134 = bf16[512,128]{1,0:T(8,128)(2,1)} custom-call(bf16[528,128]{1,0:T(8,128)(2,1)S(1)} %flash.2.a_ref, bf16[528,128]{1,0:T(8,128)(2,1)S(1)} %collective-permute-done.7.b_ref, bf16[528,128]{1,0:T(8,128)(2,1)S(1)} %collective-permute-done.8.c_ref, bf16[528,128]{1,0:T(8,128)(2,1)} %collective-permute-done.9.d_ref), custom_call_target="tpu_custom_call" | custom-call | flops 134217728 | bytes 1048576 | tf_op jit(solution)/shard_map/pallas_call | solution.py:137
  (32 shorter events, 0.2 us)
Async XLA Ops:
  0.6 0.9 copy-start.4
  1.5 12.1 %copy-start.3 = (bf16[896,576]{0,1:T(8,128)(2,1)S(1)}, bf16[896,576]{0,1:T(8,128)(2,1)}, u32[]{:S(2)}) copy-start(bf16[896,576]{0,1:T(8,128)(2,1)} %param.22) | copy-start | bytes 3096580
  2.6 11.1 %copy-start.2 = (bf16[8,128,512]{2,1,0:T(8,128)(2,1)S(1)}, bf16[8,128,512]{2,1,0:T(8,128)(2,1)}, u32[]{:S(2)}) copy-start(bf16[8,128,512]{2,1,0:T(8,128)(2,1)} %refs_5_.1) | copy-start | bytes 3145732
  2.6 11.0 %copy-start.5 = (bf16[4,4,8,192]{3,2,1,0:T(8,128)(2,1)S(1)}, bf16[4,4,8,192]{3,2,1,0:T(8,128)(2,1)}, u32[]{:S(2)}) copy-start(bf16[4,4,8,192]{3,2,1,0:T(8,128)(2,1)} %q_ref.1) | copy-start | bytes 147460
  2.6 11.0 %copy-start.6 = (bf16[4,4,896]{2,1,0:T(4,128)(2,1)S(1)}, bf16[4,4,896]{2,1,0:T(4,128)(2,1)}, u32[]{:S(2)}) copy-start(bf16[4,4,896]{2,1,0:T(4,128)(2,1)} %hid_ref.1) | copy-start | bytes 86020
  2.6 38.9 %all-to-all-start = ((bf16[8,96,576]{2,1,0:T(8,128)(2,1)}), bf16[8,96,576]{2,1,0:T(8,128)(2,1)}, u32[]{:S(2)}, u32[]{:S(2)}) async-start(bf16[8,96,576]{2,1,0:T(8,128)(2,1)} %spread.1), calls=%async_computation | async-start | bytes 1966080 | tf_op jit(solution)/shard_map/all_to_all | solution.py:285
  13.6 6.2 %copy-start.8 = (bf16[64,8,192]{2,1,0:T(8,128)(2,1)S(1)}, bf16[64,8,192]{2,1,0:T(8,128)(2,1)}, u32[]{:S(2)}) copy-start(bf16[64,8,192]{2,1,0:T(8,128)(2,1)} %param.13) | copy-start | bytes 589828
  13.6 6.2 %copy-start = (bf16[256,4,576]{0,2,1:T(8,128)(2,1)S(1)}, bf16[256,4,576]{0,2,1:T(8,128)(2,1)}, u32[]{:S(2)}) copy-start(bf16[256,4,576]{0,2,1:T(8,128)(2,1)} %param.17) | copy-start | bytes 3538948
  13.7 6.2 %copy-start.7 = (s32[256]{0:T(256)S(1)}, s32[256]{0:T(256)}, u32[]{:S(2)}) copy-start(s32[256]{0:T(256)} %param.18) | copy-start | bytes 3076
  15.1 48.2 %collective-permute-start = (bf16[80,576]{1,0:T(8,128)(2,1)}, bf16[80,576]{1,0:T(8,128)(2,1)S(1)}, u32[]{:S(2)}, u32[]{:S(2)}) collective-permute-start(bf16[80,576]{1,0:T(8,128)(2,1)} %get-tuple-element.16), channel_id=1, source_target_pairs={{0,4},{2,6},{4,0},{6,2},{1,5},{3,7},{5,1},{7,3},{8,12},{10,14},{12... | collective-permute-start | bytes 276488 | tf_op jit(solution)/shard_map/ppermute | solution.py:252
  21.7 44.8 %copy-start.10 = (s32[4]{0:T(128)S(1)}, s32[4]{0:T(128)}, u32[]{:S(2)}) copy-start(s32[4]{0:T(128)} %param.19) | copy-start | bytes 52
  21.8 47.4 %copy-start.9 = (f32[512]{0:T(512)S(1)}, f32[512]{0:T(512)}, u32[]{:S(2)}) copy-start(f32[512]{0:T(512)} %param.23) | copy-start | bytes 6148
  41.5 44.4 %copy-start.1 = (bf16[8,512,128]{2,1,0:T(8,128)(2,1)S(1)}, bf16[8,512,128]{2,1,0:T(8,128)(2,1)}, u32[]{:S(2)}) copy-start(bf16[8,512,128]{2,1,0:T(8,128)(2,1)} %wuv_ref.1) | copy-start | bytes 3145732
  41.5 44.4 %collective-permute-start.3 = (bf16[8,96,576]{2,1,0:T(8,128)(2,1)}, bf16[8,96,576]{2,1,0:T(8,128)(2,1)}, u32[]{:S(2)}, u32[]{:S(2)}) collective-permute-start(bf16[8,96,576]{2,1,0:T(8,128)(2,1)} %all-to-all-done.refs_1_.refs_3_), channel_id=1, source_target_pairs={{0,8},{8,0},{1,9},{9,1},{2,10},{10,2},{3,11},{11,3},{4,12},{12,4},... | collective-permute-start | bytes 2654216 | tf_op jit(solution)/shard_map/ppermute | solution.py:252
  44.1 65.2 %all-to-all-start.1 = ((bf16[64,8,576]{2,1,0:T(8,128)(2,1)}), bf16[64,8,576]{2,1,0:T(8,128)(2,1)S(1)}, u32[]{:S(2)}, u32[]{:S(2)}) async-start(bf16[64,8,576]{2,1,0:T(8,128)(2,1)} %bitcast.6), calls=%async_computation.1 | async-start | bytes 1310720 | tf_op jit(solution)/shard_map/all_to_all | solution.py:320
  52.0 24.6 %collective-permute-start.4 = (bf16[8,96,128]{2,1,0:T(8,128)(2,1)S(1)}, bf16[8,96,128]{2,1,0:T(8,128)(2,1)S(1)}, u32[]{:S(2)}, u32[]{:S(2)}) collective-permute-start(bf16[8,96,128]{2,1,0:T(8,128)(2,1)S(1)} %maximum_maximum_fusion.refs_0_), channel_id=1, source_target_pairs={{0,32},{16,48},{32,0},{48,16},{1,33},{17,49},{33,1},{49,17},{2,34}... | collective-permute-start | bytes 589832 | tf_op jit(solution)/shard_map/ppermute | solution.py:252
  59.1 26.7 %collective-permute-start.5 = (bf16[8,96,128]{2,1,0:T(8,128)(2,1)S(1)}, bf16[8,96,128]{2,1,0:T(8,128)(2,1)S(1)}, u32[]{:S(2)}, u32[]{:S(2)}) collective-permute-start(bf16[8,96,128]{2,1,0:T(8,128)(2,1)S(1)} %maximum_maximum_fusion.refs_0_), channel_id=1, source_target_pairs={{0,16},{16,0},{32,48},{48,32},{1,17},{17,1},{33,49},{49,33},{2,18}... | collective-permute-start | bytes 589832 | tf_op jit(solution)/shard_map/ppermute | solution.py:252
  61.3 24.5 %collective-permute-start.6 = (bf16[8,96,128]{2,1,0:T(8,128)(2,1)S(1)}, bf16[8,96,128]{2,1,0:T(8,128)(2,1)S(1)}, u32[]{:S(2)}, u32[]{:S(2)}) collective-permute-start(bf16[8,96,128]{2,1,0:T(8,128)(2,1)S(1)} %maximum_maximum_fusion.refs_0_), channel_id=1, source_target_pairs={{0,48},{16,32},{32,16},{48,0},{1,49},{17,33},{33,17},{49,1},{2,50}... | collective-permute-start | bytes 589832 | tf_op jit(solution)/shard_map/ppermute | solution.py:252
  63.4 5.7 %collective-permute-start.1 = (bf16[80,576]{1,0:T(8,128)(2,1)S(1)}, bf16[80,576]{1,0:T(8,128)(2,1)S(1)}, u32[]{:S(2)}, u32[]{:S(2)}) collective-permute-start(bf16[80,576]{1,0:T(8,128)(2,1)S(1)} %pad_maximum_fusion), channel_id=1, source_target_pairs={{0,2},{2,0},{4,6},{6,4},{1,3},{3,1},{5,7},{7,5},{8,10},{10,8},{12,... | collective-permute-start | bytes 276488 | tf_op jit(solution)/shard_map/ppermute | solution.py:252
  69.1 40.2 %collective-permute-start.2 = (f32[8,576]{1,0:T(8,128)S(1)}, f32[8,576]{1,0:T(8,128)S(1)}, u32[]{:S(2)}, u32[]{:S(2)}) collective-permute-start(f32[8,576]{1,0:T(8,128)S(1)} %pad_add_fusion.raw_a), channel_id=1, source_target_pairs={{0,1},{1,0},{2,3},{3,2},{4,5},{5,4},{6,7},{7,6},{8,9},{9,8},{10,11... | collective-permute-start | bytes 55304 | tf_op jit(solution)/shard_map/ppermute | solution.py:252
  97.3 24.1 %collective-permute-start.7 = (bf16[528,128]{1,0:T(8,128)(2,1)}, bf16[528,128]{1,0:T(8,128)(2,1)S(1)}, u32[]{:S(2)}, u32[]{:S(2)}) collective-permute-start(bf16[528,128]{1,0:T(8,128)(2,1)} %get-tuple-element.22), channel_id=1, source_target_pairs={{0,16},{16,0},{32,48},{48,32},{1,17},{17,1},{33,49},{49,33},{2,18}... | collective-permute-start | bytes 405512 | tf_op jit(solution)/shard_map/ppermute | solution.py:252
  102.1 19.2 %collective-permute-start.8 = (bf16[528,128]{1,0:T(8,128)(2,1)}, bf16[528,128]{1,0:T(8,128)(2,1)S(1)}, u32[]{:S(2)}, u32[]{:S(2)}) collective-permute-start(bf16[528,128]{1,0:T(8,128)(2,1)} %get-tuple-element.23), channel_id=1, source_target_pairs={{0,32},{16,48},{32,0},{48,16},{1,33},{17,49},{33,1},{49,17},{2,34}... | collective-permute-start | bytes 405512 | tf_op jit(solution)/shard_map/ppermute | solution.py:252
  104.5 16.9 %collective-permute-start.9 = (bf16[528,128]{1,0:T(8,128)(2,1)}, bf16[528,128]{1,0:T(8,128)(2,1)}, u32[]{:S(2)}, u32[]{:S(2)}) collective-permute-start(bf16[528,128]{1,0:T(8,128)(2,1)} %get-tuple-element.24), channel_id=1, source_target_pairs={{0,48},{16,32},{32,16},{48,0},{1,49},{17,33},{33,17},{49,1},{2,50}... | collective-permute-start | bytes 405512 | tf_op jit(solution)/shard_map/ppermute | solution.py:252
  110.8 9.5 %all-to-all-start.2 = ((bf16[4,32,512]{2,1,0:T(8,128)(2,1)}), bf16[4,32,512]{2,1,0:T(8,128)(2,1)S(1)}, u32[]{:S(2)}, u32[]{:S(2)}) async-start(bf16[4,32,512]{2,1,0:T(8,128)(2,1)} %shard_map.133), calls=%async_computation.2 | async-start | bytes 262144 | tf_op jit(solution)/shard_map/all_to_all | solution.py:354

commit v4 on v3

--- a/solution.py
+++ b/solution.py
@@ -1,5 +1,3 @@
-import functools
-
 import jax
 import jax.numpy as jnp
 from jax import lax
@@ -26,51 +24,46 @@
     return hi, mid, low
 
 
-def flash_kernel(offsets, start, *refs):
-    count = len(offsets)
-    moved, targets = refs[: count + 4], refs[count + 4 : 2 * count + 4]
-    held, out_held, sems = refs[2 * count + 4 : 3 * count + 8], refs[3 * count + 8 : -1], refs[-1]
-    loads = [pltpu.make_async_copy(m, h, sems.at[i]) for i, (m, h) in enumerate(zip(moved, held))]
-    for at in (0, count + 2, count, count + 1, *range(1, count), count + 3):
-        loads[at].start()
-    queries, outs = dict(zip(offsets, held[:count])), dict(zip(offsets, out_held))
-    k1_ref, k2_ref, wuk_ref, wuv_ref = held[count:]
-    stores = []
+def flash_kernel(start, q0, q1, q2, q3, k1_hbm, k2_hbm, wuk_ref, wuv_ref, *refs):
+    targets, held, outs, sems = refs[:4], refs[4:10], refs[10:14], refs[14]
+    loads = [
+        pltpu.make_async_copy(m, h, sems.at[i])
+        for i, (m, h) in enumerate(zip((q0, q1, q2, q3, k1_hbm, k2_hbm), held))
+    ]
+    for load in loads:
+        load.start()
+    queries, k1_ref, k2_ref = held[:4], held[4], held[5]
     z, yh, c = lax.axis_index("z"), lax.axis_index("yh"), lax.axis_index("c")
-    waits = dict(zip((*offsets, "k1", "k2", "wuk", "wuv"), loads))
-    ready = {}
-
-    def key_rows(name, ref):
-        if name not in ready:
-            waits[name].wait()
-            ready[name] = ref[...].reshape(768, 576)
-        return ready[name]
-
     j = lax.broadcasted_iota(jnp.int32, (1, 768), 1)
     blk = (j * 683) >> 16
     kpos = blk * 768 + (j - blk * 96) + yh * 192
     where1, where2 = kpos + c * 96, kpos + (1 - c) * 96
+    row = lax.broadcasted_iota(jnp.int32, (512, 1), 0)
+    source = ((row >> 6) & 3) ^ yh
+    qpos = start[0] + ((source + z * 4) * 2 + c) * 64 + (row & 63)
     scale = SCALE * LOG2E
-
-    def score(k):
+    keys = []
+    lines = [[], [], [], []]
+
+    def score(b):
         rows = []
-        waits[k].wait()
-        if k == offsets[0]:
-            waits["wuk"].wait()
-        for h in range(8):
-            pair = queries[k][h, 64:, :]
-            rope = jnp.concatenate([pair[:, :64], pair[:, 64:]], axis=0)
-            a = jnp.dot(queries[k][h, :64, :], wuk_ref[h], preferred_element_type=jnp.float32)
+        for h in (2 * b, 2 * b + 1):
+            nope = jnp.concatenate([q[h, :64, :] for q in queries], axis=0)
+            a = jnp.dot(nope, wuk_ref[h], preferred_element_type=jnp.float32)
+            ropes = []
+            for q in queries:
+                pair = q[h, 64:, :]
+                ropes += [pair[:, :64], pair[:, 64:]]
+            rope = jnp.concatenate(ropes, axis=0)
             rows.append(jnp.concatenate([a.astype(jnp.bfloat16), rope], axis=1))
         full = jnp.concatenate(rows, axis=0)
-        s1 = lax.dot_general(full, key_rows("k1", k1_ref), NT, preferred_element_type=jnp.float32)
-        s2 = lax.dot_general(full, key_rows("k2", k2_ref), NT, preferred_element_type=jnp.float32)
-        return s1, s2
-
-    def weigh(k, s):
-        source = yh ^ k
-        first = start[0] + ((z * 4 + source) * 2 + c) * 64
-        qpos = first + (lax.broadcasted_iota(jnp.int32, (512, 1), 0) & 63)
+        if not keys:
+            for load, ref in ((loads[4], k1_ref), (loads[5], k2_ref)):
+                load.wait()
+                keys.append(ref[...].reshape(768, 576))
+        return [lax.dot_general(full, k, NT, preferred_element_type=jnp.float32) for k in keys]
+
+    def weigh(s):
         s1 = jnp.where(where1 <= qpos, s[0], -1e30)
         s2 = jnp.where(where2 <= qpos, s[1], -1e30)
         top = jnp.maximum(jnp.max(s1, axis=1, keepdims=True), jnp.max(s2, axis=1, keepdims=True))
@@ -80,29 +73,37 @@
         lse = top * scale + jnp.log2(total)
         return p1.astype(jnp.bfloat16), p2.astype(jnp.bfloat16), total, lse
 
-    def mix(k, p1, p2, total, lse):
-        if k == offsets[0]:
-            waits["wuv"].wait()
-        acc = jnp.dot(p1, ready["k1"][:, :KV_RANK], preferred_element_type=jnp.float32)
-        acc = acc + jnp.dot(p2, ready["k2"][:, :KV_RANK], preferred_element_type=jnp.float32)
+    def mix(b, p1, p2, total, lse):
+        acc = jnp.dot(p1, keys[0][:, :KV_RANK], preferred_element_type=jnp.float32)
+        acc = acc + jnp.dot(p2, keys[1][:, :KV_RANK], preferred_element_type=jnp.float32)
         mixed = (acc * (1.0 / total)).astype(jnp.bfloat16)
-        for h in range(8):
-            at = h * 64
-            o = jnp.dot(mixed[at : at + 64], wuv_ref[h], preferred_element_type=jnp.float32)
-            outs[k][at : at + 64, :] = o.astype(jnp.bfloat16)
+        for n in (0, 1):
+            h = 2 * b + n
+            o = jnp.dot(
+                mixed[n * 256 : (n + 1) * 256], wuv_ref[h], preferred_element_type=jnp.float32
+            ).astype(jnp.bfloat16)
+            for k in range(4):
+                outs[k][h * 64 : (h + 1) * 64, :] = o[k * 64 : (k + 1) * 64]
         flat = jnp.transpose(jnp.broadcast_to(lse, (512, 128)))[0:1, :]
-        lines = jnp.concatenate([flat[:, i * 128 : (i + 1) * 128] for i in range(4)], axis=0)
-        hi, mid, low = split3(lines)
+        for k in range(4):
+            at = k * 64
+            lines[k].append(
+                jnp.concatenate([flat[:, at : at + 64], flat[:, at + 256 : at + 320]], axis=1)
+            )
+
+    for load in loads[:4]:
+        load.wait()
+    s = score(0)
+    for b in range(4):
+        following = score(b + 1) if b < 3 else None
+        mix(b, *weigh(s))
+        s = following
+    stores = []
+    for k in (2, 1, 3, 0):
+        hi, mid, low = split3(jnp.concatenate(lines[k], axis=0))
         outs[k][512:, :] = jnp.concatenate([hi, mid, low, jnp.zeros_like(hi)], axis=0)
-
-    s = score(offsets[0])
-    for n, k in enumerate(offsets):
-        following = score(offsets[n + 1]) if n + 1 < count else None
-        mix(k, *weigh(k, s))
-        store = pltpu.make_async_copy(outs[k], targets[n], sems.at[count + 4 + n])
-        store.start()
-        stores.append(store)
-        s = following
+        stores.append(pltpu.make_async_copy(outs[k], targets[k], sems.at[6 + k]))
+        stores[-1].start()
     for store in stores:
         store.wait()
 
@@ -319,43 +320,36 @@
     other_keys = trade(keys, "c", 1, 2)
     cache = lax.all_to_all(rows, CTX, 0, 0, tiled=True)
 
-    def flash(offsets, chunks):
-        count = len(offsets)
-        chunk, key = pltpu.VMEM((8, 96, 128), bf), pltpu.VMEM((8, 96, width), bf)
-        return pl.pallas_call(
-            functools.partial(flash_kernel, offsets),
-            out_shape=[jax.ShapeDtypeStruct((512 + 16, 128), bf)] * count,
-            in_specs=[pl.BlockSpec(memory_space=pltpu.SMEM)] + [hbm] * (count + 4),
-            out_specs=[hbm] * count,
-            scratch_shapes=[chunk] * count
-            + [key] * 2
-            + [pltpu.VMEM(w_uk.shape, bf), pltpu.VMEM(w_uv.shape, bf)]
-            + [pltpu.VMEM((512 + 16, 128), bf)] * count
-            + [pltpu.SemaphoreType.DMA((2 * count + 4,))],
-            compiler_params=pltpu.CompilerParams(vmem_limit_bytes=28 << 20),
-            cost_estimate=pl.CostEstimate(
-                flops=count * 2 * 512 * 1536 * 1100, bytes_accessed=4 << 20, transcendentals=1 << 20
-            ),
-            name="flash",
-        )(span_start, *chunks, keys, other_keys, w_uk, w_uv)
-
-    far = (2, 1, 3)
-    sending = flash(far, [visiting[k] for k in far])
-    parts = [None] * 4
-    for k, piece in zip(far, sending):
-        parts[k] = trade(piece, "yh", k, 4)
+    chunk, key = pltpu.VMEM((8, 96, 128), bf), pltpu.VMEM((8, 96, width), bf)
+    vmem = pl.BlockSpec(memory_space=pltpu.VMEM)
+    parts = pl.pallas_call(
+        flash_kernel,
+        out_shape=[jax.ShapeDtypeStruct((512 + 16, 128), bf)] * 4,
+        in_specs=[pl.BlockSpec(memory_space=pltpu.SMEM)] + [hbm] * 6 + [vmem] * 2,
+        out_specs=[hbm] * 4,
+        scratch_shapes=[chunk] * 4
+        + [key] * 2
+        + [pltpu.VMEM((512 + 16, 128), bf)] * 4
+        + [pltpu.SemaphoreType.DMA((10,))],
+        compiler_params=pltpu.CompilerParams(vmem_limit_bytes=28 << 20),
+        cost_estimate=pl.CostEstimate(
+            flops=4 * 2 * 512 * 1536 * 1100, bytes_accessed=4 << 20, transcendentals=1 << 22
+        ),
+        name="flash",
+    )(span_start, *visiting, keys, other_keys, w_uk, w_uv)
+    parts = list(parts)
+    for k in (2, 1, 3):
+        parts[k] = trade(parts[k], "yh", k, 4)
 
     mixed = small(
         attend_kernel,
         jax.ShapeDtypeStruct((4, 32, KV_RANK), bf),
         [*got, raw_here, raw_there, cache.reshape(512, width)],
     )
-    own, mixed = fence((packed, mixed))
     mixed = lax.all_to_all(mixed, "x", 0, 0, tiled=True)
-    parts[0] = flash((0,), [own])[0]
-    mixed, parts[0] = fence((mixed, parts[0]))
+    mixed, merged = fence((mixed, merge(parts)))
     decode_out = small(finish_kernel, jax.ShapeDtypeStruct((4, 4, 8, 128), bf), [mixed, w_uv])
-    prefill_out = merge(parts).reshape(queries, heads_here, 128)
+    prefill_out = merged.reshape(queries, heads_here, 128)
     return (prefill_out, decode_out)
 
 

time: 125 us -> 128 us (1.024)
  the two profiles are of different devices: /device:TPU:1 before, /device:TPU:56 now
where the time goes in v4:
time: 128 us
  starting transfers between devices  68.7 us (54%)
  waiting for transfers between devices  33.9 us (26%)
  Pallas kernels  21 us (16%)
  local copies, waits for them, and re-layouts  2.26 us (2%)
  between operations  1.64 us (1%)
    ppermute x10, starting transfers between devices, trade(): return lax.ppermute(v, axis, [(i, i ^ k) for i in range(n)])  47.3 us
    all_to_all x1, waiting for transfers between devices, layer(): keys = lax.all_to_all(spread, 'z', 0, 0, tiled=True)  25.6 us
    pallas_call x1, Pallas kernels, layer(): pl.pallas_call(flash_kernel, out_shape=[jax.ShapeDtypeStruct((512 + 16, 1...  13.5 us
    all_to_all x1, starting transfers between devices, layer(): keys = lax.all_to_all(spread, 'z', 0, 0, tiled=True)  10.5 us
    all_to_all x1, starting transfers between devices, layer(): cache = lax.all_to_all(rows, CTX, 0, 0, tiled=True)  7.55 us
    pallas_call x5, Pallas kernels, small(): pl.pallas_call(kernel, out_shape=outs, in_specs=[sm] * scalars + [vm] * (...  6.52 us
    all_to_all x1, waiting for transfers between devices, layer(): mixed = lax.all_to_all(mixed, 'x', 0, 0, tiled=True)  4.65 us
    ppermute x10, waiting for transfers between devices, trade(): return lax.ppermute(v, axis, [(i, i ^ k) for i in range(n)])  3.69 us
  transfers between devices with their start and end apart: 13, of which 3 were waited for; matrix products, arithmetic and copies ran while one was open for 0% of the time, Pallas kernels for 15%

profile of v4, /device:TPU:56, one launch (start us, length us, event | category | flops | bytes accessed | tf_op | source)
XLA Modules:
  0.0 127.6 jit_solution(10427495119553302613)
XLA Ops:
  0.6 0.9 copy-done.4
  1.5 1.0 spread.1
  2.6 0.0 copy-start
  2.6 0.0 copy-start.7
  2.6 10.5 %all-to-all-start = ((bf16[8,96,576]{2,1,0:T(8,128)(2,1)}), bf16[8,96,576]{2,1,0:T(8,128)(2,1)}, u32[]{:S(2)}, u32[]{:S(2)}) async-start(bf16[8,96,576]{2,1,0:T(8,128)(2,1)} %spread.1), calls=%async_computation | async-start | bytes 1966080 | tf_op jit(solution)/shard_map/all_to_all | solution.py:286
  13.1 1.8 %shard_map.132 = bf16[512,576]{1,0:T(8,128)(2,1)} custom-call(s32[1,256]{1,0:T(1,128)S(1)} %bitcast.15, bf16[4,576,256]{2,1,0:T(8,128)(2,1)S(1)} %bitcast.13), custom_call_target="tpu_custom_call" | custom-call | flops 134217728 | bytes 1048576 | tf_op jit(solution)/shard_map/pallas_call | solution.py:138
  14.9 25.6 %all-to-all-done.k1_hbm = bf16[8,96,576]{2,1,0:T(8,128)(2,1)} async-done(((bf16[8,96,576]{2,1,0:T(8,128)(2,1)}), bf16[8,96,576]{2,1,0:T(8,128)(2,1)}, u32[]{:S(2)}, u32[]{:S(2)}) %all-to-all-start) | async-done | bytes 884768 | tf_op jit(solution)/shard_map/all_to_all | solution.py:286
  40.5 1.9 %collective-permute-start.6 = (bf16[8,96,576]{2,1,0:T(8,128)(2,1)}, bf16[8,96,576]{2,1,0:T(8,128)(2,1)}, u32[]{:S(2)}, u32[]{:S(2)}) collective-permute-start(bf16[8,96,576]{2,1,0:T(8,128)(2,1)} %all-to-all-done.k1_hbm), channel_id=1, source_target_pairs={{0,8},{8,0},{1,9},{9,1},{2,10},{10,2},{3,11},{11,3},{4,12},{12,4},... | collective-permute-start | bytes 2654216 | tf_op jit(solution)/shard_map/ppermute | solution.py:253
  42.5 0.1 maximum_maximum_fusion.q0
  42.6 4.0 %collective-permute-start.3 = (bf16[8,96,128]{2,1,0:T(8,128)(2,1)S(1)}, bf16[8,96,128]{2,1,0:T(8,128)(2,1)S(1)}, u32[]{:S(2)}, u32[]{:S(2)}) collective-permute-start(bf16[8,96,128]{2,1,0:T(8,128)(2,1)S(1)} %maximum_maximum_fusion.q0), channel_id=1, source_target_pairs={{0,16},{16,0},{32,48},{48,32},{1,17},{17,1},{33,49},{49,33},{2,18}... | collective-permute-start | bytes 589832 | tf_op jit(solution)/shard_map/ppermute | solution.py:253
  46.7 2.9 %collective-permute-start.4 = (bf16[8,96,128]{2,1,0:T(8,128)(2,1)S(1)}, bf16[8,96,128]{2,1,0:T(8,128)(2,1)}, u32[]{:S(2)}, u32[]{:S(2)}) collective-permute-start(bf16[8,96,128]{2,1,0:T(8,128)(2,1)S(1)} %maximum_maximum_fusion.q0), channel_id=1, source_target_pairs={{0,32},{16,48},{32,0},{48,16},{1,33},{17,49},{33,1},{49,17},{2,34}... | collective-permute-start | bytes 589832 | tf_op jit(solution)/shard_map/ppermute | solution.py:253
  49.6 5.3 %collective-permute-start.5 = (bf16[8,96,128]{2,1,0:T(8,128)(2,1)S(1)}, bf16[8,96,128]{2,1,0:T(8,128)(2,1)}, u32[]{:S(2)}, u32[]{:S(2)}) collective-permute-start(bf16[8,96,128]{2,1,0:T(8,128)(2,1)S(1)} %maximum_maximum_fusion.q0), channel_id=1, source_target_pairs={{0,48},{16,32},{32,16},{48,0},{1,49},{17,33},{33,17},{49,1},{2,50}... | collective-permute-start | bytes 589832 | tf_op jit(solution)/shard_map/ppermute | solution.py:253
  54.9 0.0 copy-start.3
  54.9 1.2 copy-done.3
  56.1 0.8 shard_map.131
  57.0 0.0 copy-start.10
  57.0 0.0 copy-start.1
  57.0 5.1 %collective-permute-start = (bf16[80,576]{1,0:T(8,128)(2,1)S(1)}, bf16[80,576]{1,0:T(8,128)(2,1)S(1)}, u32[]{:S(2)}, u32[]{:S(2)}) collective-permute-start(bf16[80,576]{1,0:T(8,128)(2,1)S(1)} %get-tuple-element.15), channel_id=1, source_target_pairs={{0,4},{2,6},{4,0},{6,2},{1,5},{3,7},{5,1},{7,3},{8,12},{10,14},{12... | collective-permute-start | bytes 276488 | tf_op jit(solution)/shard_map/ppermute | solution.py:253
  62.1 7.6 %all-to-all-start.1 = ((bf16[64,8,576]{2,1,0:T(8,128)(2,1)}), bf16[64,8,576]{2,1,0:T(8,128)(2,1)S(1)}, u32[]{:S(2)}, u32[]{:S(2)}) async-start(bf16[64,8,576]{2,1,0:T(8,128)(2,1)} %bitcast.5), calls=%async_computation.1 | async-start | bytes 1310720 | tf_op jit(solution)/shard_map/all_to_all | solution.py:321
  70.3 0.0 copy-start.9
  70.4 2.7 %collective-permute-start.1 = (bf16[80,576]{1,0:T(8,128)(2,1)S(1)}, bf16[80,576]{1,0:T(8,128)(2,1)S(1)}, u32[]{:S(2)}, u32[]{:S(2)}) collective-permute-start(bf16[80,576]{1,0:T(8,128)(2,1)S(1)} %pad_maximum_fusion), channel_id=1, source_target_pairs={{0,2},{2,0},{4,6},{6,4},{1,3},{3,1},{5,7},{7,5},{8,10},{10,8},{12,... | collective-permute-start | bytes 276488 | tf_op jit(solution)/shard_map/ppermute | solution.py:253
  73.1 13.5 %flash.1 = (bf16[528,128]{1,0:T(8,128)(2,1)S(1)}, bf16[528,128]{1,0:T(8,128)(2,1)}, bf16[528,128]{1,0:T(8,128)(2,1)}, bf16[528,128]{1,0:T(8,128)(2,1)}) custom-call(s32[1]{0:T(128)S(6)} %copy.17.start, bf16[8,96,128]{2,1,0:T(8,128)(2,1)S(1)} %maximum_maximum_fusion.q0, bf16[8,96,128]{2,1,0:T(8,128)(2,1)S(1)} %collective-permute-done.3.q1, ...), custom_call_target="tpu_custom_call" | custom-call | flops 6920601600 | bytes 4194304 | tf_op jit(solution)/shard_map/flash/pallas_call | solution.py:325
  86.6 4.3 %collective-permute-start.7 = (bf16[528,128]{1,0:T(8,128)(2,1)}, bf16[528,128]{1,0:T(8,128)(2,1)S(1)}, u32[]{:S(2)}, u32[]{:S(2)}) collective-permute-start(bf16[528,128]{1,0:T(8,128)(2,1)} %get-tuple-element.19), channel_id=1, source_target_pairs={{0,16},{16,0},{32,48},{48,32},{1,17},{17,1},{33,49},{49,33},{2,18}... | collective-permute-start | bytes 405512 | tf_op jit(solution)/shard_map/ppermute | solution.py:253
  90.8 2.4 %collective-permute-start.8 = (bf16[528,128]{1,0:T(8,128)(2,1)}, bf16[528,128]{1,0:T(8,128)(2,1)S(1)}, u32[]{:S(2)}, u32[]{:S(2)}) collective-permute-start(bf16[528,128]{1,0:T(8,128)(2,1)} %get-tuple-element.20), channel_id=1, source_target_pairs={{0,32},{16,48},{32,0},{48,16},{1,33},{17,49},{33,1},{49,17},{2,34}... | collective-permute-start | bytes 405512 | tf_op jit(solution)/shard_map/ppermute | solution.py:253
  93.2 5.6 %collective-permute-start.9 = (bf16[528,128]{1,0:T(8,128)(2,1)}, bf16[528,128]{1,0:T(8,128)(2,1)S(1)}, u32[]{:S(2)}, u32[]{:S(2)}) collective-permute-start(bf16[528,128]{1,0:T(8,128)(2,1)} %get-tuple-element.21), channel_id=1, source_target_pairs={{0,48},{16,32},{32,16},{48,0},{1,49},{17,33},{33,17},{49,1},{2,50}... | collective-permute-start | bytes 405512 | tf_op jit(solution)/shard_map/ppermute | solution.py:253
  98.9 13.2 %collective-permute-start.2 = (f32[8,576]{1,0:T(8,128)S(1)}, f32[8,576]{1,0:T(8,128)S(1)}, u32[]{:S(2)}, u32[]{:S(2)}) collective-permute-start(f32[8,576]{1,0:T(8,128)S(1)} %pad_add_fusion.raw_a), channel_id=1, source_target_pairs={{0,1},{1,0},{2,3},{3,2},{4,5},{5,4},{6,7},{7,6},{8,9},{9,8},{10,11... | collective-permute-start | bytes 55304 | tf_op jit(solution)/shard_map/ppermute | solution.py:253
  112.1 3.7 %collective-permute-done.2.raw_b = f32[8,576]{1,0:T(8,128)S(1)} collective-permute-done((f32[8,576]{1,0:T(8,128)S(1)}, f32[8,576]{1,0:T(8,128)S(1)}, u32[]{:S(2)}, u32[]{:S(2)}) %collective-permute-start.2) | collective-permute-done | bytes 18464 | tf_op jit(solution)/shard_map/ppermute | solution.py:253
  115.7 1.5 %shard_map.133 = bf16[4,32,512]{2,1,0:T(8,128)(2,1)} custom-call(bf16[40,576]{1,0:T(8,128)(2,1)S(1)} %get-tuple-element.13.p0, bf16[80,576]{1,0:T(8,128)(2,1)S(1)} %collective-permute-done.1.p13, bf16[80,576]{1,0:T(8,128)(2,1)S(1)} %collective-permute-done.p2, f32[8,576]{1,0:T(8,128)S(1)} %pad_add_fusion.raw_a, f32[8,576]{1,0:T(8,128)S(1)} %collective-permute-done.2.raw_b, ...), custom_call_target="tpu_custom_call" | custom-call | flops 134217728 | bytes 1048576 | tf_op jit(solution)/shard_map/pallas_call | solution.py:138
  117.3 3.3 %all-to-all-start.2 = ((bf16[4,32,512]{2,1,0:T(8,128)(2,1)}), bf16[4,32,512]{2,1,0:T(8,128)(2,1)S(1)}, u32[]{:S(2)}, u32[]{:S(2)}) async-start(bf16[4,32,512]{2,1,0:T(8,128)(2,1)} %shard_map.133), calls=%async_computation.2 | async-start | bytes 262144 | tf_op jit(solution)/shard_map/all_to_all | solution.py:349
  120.6 1.3 %shard_map.134 = bf16[512,128]{1,0:T(8,128)(2,1)} custom-call(bf16[528,128]{1,0:T(8,128)(2,1)S(1)} %get-tuple-element.18.a_ref, bf16[528,128]{1,0:T(8,128)(2,1)S(1)} %collective-permute-done.7.b_ref, bf16[528,128]{1,0:T(8,128)(2,1)S(1)} %collective-permute-done.8.c_ref, bf16[528,128]{1,0:T(8,128)(2,1)S(1)} %collective-permute-done.9.d_ref), custom_call_target="tpu_custom_call" | custom-call | flops 134217728 | bytes 1048576 | tf_op jit(solution)/shard_map/pallas_call | solution.py:138
  121.9 4.6 %all-to-all-done.2.m_ref = bf16[4,32,512]{2,1,0:T(8,128)(2,1)S(1)} async-done(((bf16[4,32,512]{2,1,0:T(8,128)(2,1)}), bf16[4,32,512]{2,1,0:T(8,128)(2,1)S(1)}, u32[]{:S(2)}, u32[]{:S(2)}) %all-to-all-start.2) | async-done | bytes 131104 | tf_op jit(solution)/shard_map/all_to_all | solution.py:349
  126.6 1.0 shard_map.135
  (31 shorter events, 0.2 us)
Async XLA Ops:
  0.6 0.9 copy-start.4
  2.6 10.5 %copy-start = (bf16[256,4,576]{0,2,1:T(8,128)(2,1)S(1)}, bf16[256,4,576]{0,2,1:T(8,128)(2,1)}, u32[]{:S(2)}) copy-start(bf16[256,4,576]{0,2,1:T(8,128)(2,1)} %param.17) | copy-start | bytes 3538948
  2.6 10.5 %copy-start.7 = (s32[256]{0:T(256)S(1)}, s32[256]{0:T(256)}, u32[]{:S(2)}) copy-start(s32[256]{0:T(256)} %param.18) | copy-start | bytes 3076
  2.6 37.9 %all-to-all-start = ((bf16[8,96,576]{2,1,0:T(8,128)(2,1)}), bf16[8,96,576]{2,1,0:T(8,128)(2,1)}, u32[]{:S(2)}, u32[]{:S(2)}) async-start(bf16[8,96,576]{2,1,0:T(8,128)(2,1)} %spread.1), calls=%async_computation | async-start | bytes 1966080 | tf_op jit(solution)/shard_map/all_to_all | solution.py:286
  13.0 29.4 %copy-start.8 = (bf16[64,8,192]{2,1,0:T(8,128)(2,1)S(1)}, bf16[64,8,192]{2,1,0:T(8,128)(2,1)}, u32[]{:S(2)}) copy-start(bf16[64,8,192]{2,1,0:T(8,128)(2,1)} %param.13) | copy-start | bytes 589828
  14.9 40.0 %copy-start.2 = (bf16[8,128,512]{2,1,0:T(8,128)(2,1)S(1)}, bf16[8,128,512]{2,1,0:T(8,128)(2,1)}, u32[]{:S(2)}) copy-start(bf16[8,128,512]{2,1,0:T(8,128)(2,1)} %wuk_ref.3) | copy-start | bytes 3145732
  14.9 40.0 %copy-start.5 = (bf16[4,4,8,192]{3,2,1,0:T(8,128)(2,1)S(1)}, bf16[4,4,8,192]{3,2,1,0:T(8,128)(2,1)}, u32[]{:S(2)}) copy-start(bf16[4,4,8,192]{3,2,1,0:T(8,128)(2,1)} %q_ref.1) | copy-start | bytes 147460
  14.9 40.0 %copy-start.6 = (bf16[4,4,896]{2,1,0:T(4,128)(2,1)S(1)}, bf16[4,4,896]{2,1,0:T(4,128)(2,1)}, u32[]{:S(2)}) copy-start(bf16[4,4,896]{2,1,0:T(4,128)(2,1)} %hid_ref.1) | copy-start | bytes 86020
  40.5 32.6 %collective-permute-start.6 = (bf16[8,96,576]{2,1,0:T(8,128)(2,1)}, bf16[8,96,576]{2,1,0:T(8,128)(2,1)}, u32[]{:S(2)}, u32[]{:S(2)}) collective-permute-start(bf16[8,96,576]{2,1,0:T(8,128)(2,1)} %all-to-all-done.k1_hbm), channel_id=1, source_target_pairs={{0,8},{8,0},{1,9},{9,1},{2,10},{10,2},{3,11},{11,3},{4,12},{12,4},... | collective-permute-start | bytes 2654216 | tf_op jit(solution)/shard_map/ppermute | solution.py:253
  42.6 30.4 %collective-permute-start.3 = (bf16[8,96,128]{2,1,0:T(8,128)(2,1)S(1)}, bf16[8,96,128]{2,1,0:T(8,128)(2,1)S(1)}, u32[]{:S(2)}, u32[]{:S(2)}) collective-permute-start(bf16[8,96,128]{2,1,0:T(8,128)(2,1)S(1)} %maximum_maximum_fusion.q0), channel_id=1, source_target_pairs={{0,16},{16,0},{32,48},{48,32},{1,17},{17,1},{33,49},{49,33},{2,18}... | collective-permute-start | bytes 589832 | tf_op jit(solution)/shard_map/ppermute | solution.py:253
  46.7 26.4 %collective-permute-start.4 = (bf16[8,96,128]{2,1,0:T(8,128)(2,1)S(1)}, bf16[8,96,128]{2,1,0:T(8,128)(2,1)}, u32[]{:S(2)}, u32[]{:S(2)}) collective-permute-start(bf16[8,96,128]{2,1,0:T(8,128)(2,1)S(1)} %maximum_maximum_fusion.q0), channel_id=1, source_target_pairs={{0,32},{16,48},{32,0},{48,16},{1,33},{17,49},{33,1},{49,17},{2,34}... | collective-permute-start | bytes 589832 | tf_op jit(solution)/shard_map/ppermute | solution.py:253
  49.6 23.5 %collective-permute-start.5 = (bf16[8,96,128]{2,1,0:T(8,128)(2,1)S(1)}, bf16[8,96,128]{2,1,0:T(8,128)(2,1)}, u32[]{:S(2)}, u32[]{:S(2)}) collective-permute-start(bf16[8,96,128]{2,1,0:T(8,128)(2,1)S(1)} %maximum_maximum_fusion.q0), channel_id=1, source_target_pairs={{0,48},{16,32},{32,16},{48,0},{1,49},{17,33},{33,17},{49,1},{2,50}... | collective-permute-start | bytes 589832 | tf_op jit(solution)/shard_map/ppermute | solution.py:253
  54.9 1.2 copy-start.3
  57.0 12.7 %copy-start.10 = (s32[4]{0:T(128)S(1)}, s32[4]{0:T(128)}, u32[]{:S(2)}) copy-start(s32[4]{0:T(128)} %param.19) | copy-start | bytes 52
  57.0 16.1 %copy-start.1 = (bf16[8,512,128]{2,1,0:T(8,128)(2,1)S(1)}, bf16[8,512,128]{2,1,0:T(8,128)(2,1)}, u32[]{:S(2)}) copy-start(bf16[8,512,128]{2,1,0:T(8,128)(2,1)} %wuv_ref.3) | copy-start | bytes 3145732
  57.0 13.3 %collective-permute-start = (bf16[80,576]{1,0:T(8,128)(2,1)S(1)}, bf16[80,576]{1,0:T(8,128)(2,1)S(1)}, u32[]{:S(2)}, u32[]{:S(2)}) collective-permute-start(bf16[80,576]{1,0:T(8,128)(2,1)S(1)} %get-tuple-element.15), channel_id=1, source_target_pairs={{0,4},{2,6},{4,0},{6,2},{1,5},{3,7},{5,1},{7,3},{8,12},{10,14},{12... | collective-permute-start | bytes 276488 | tf_op jit(solution)/shard_map/ppermute | solution.py:253
  62.1 53.7 %all-to-all-start.1 = ((bf16[64,8,576]{2,1,0:T(8,128)(2,1)}), bf16[64,8,576]{2,1,0:T(8,128)(2,1)S(1)}, u32[]{:S(2)}, u32[]{:S(2)}) async-start(bf16[64,8,576]{2,1,0:T(8,128)(2,1)} %bitcast.5), calls=%async_computation.1 | async-start | bytes 1310720 | tf_op jit(solution)/shard_map/all_to_all | solution.py:321
  70.3 28.5 %copy-start.9 = (f32[512]{0:T(512)S(1)}, f32[512]{0:T(512)}, u32[]{:S(2)}) copy-start(f32[512]{0:T(512)} %param.23) | copy-start | bytes 6148
  70.4 28.5 %collective-permute-start.1 = (bf16[80,576]{1,0:T(8,128)(2,1)S(1)}, bf16[80,576]{1,0:T(8,128)(2,1)S(1)}, u32[]{:S(2)}, u32[]{:S(2)}) collective-permute-start(bf16[80,576]{1,0:T(8,128)(2,1)S(1)} %pad_maximum_fusion), channel_id=1, source_target_pairs={{0,2},{2,0},{4,6},{6,4},{1,3},{3,1},{5,7},{7,5},{8,10},{10,8},{12,... | collective-permute-start | bytes 276488 | tf_op jit(solution)/shard_map/ppermute | solution.py:253
  86.6 34.0 %collective-permute-start.7 = (bf16[528,128]{1,0:T(8,128)(2,1)}, bf16[528,128]{1,0:T(8,128)(2,1)S(1)}, u32[]{:S(2)}, u32[]{:S(2)}) collective-permute-start(bf16[528,128]{1,0:T(8,128)(2,1)} %get-tuple-element.19), channel_id=1, source_target_pairs={{0,16},{16,0},{32,48},{48,32},{1,17},{17,1},{33,49},{49,33},{2,18}... | collective-permute-start | bytes 405512 | tf_op jit(solution)/shard_map/ppermute | solution.py:253
  90.8 29.8 %collective-permute-start.8 = (bf16[528,128]{1,0:T(8,128)(2,1)}, bf16[528,128]{1,0:T(8,128)(2,1)S(1)}, u32[]{:S(2)}, u32[]{:S(2)}) collective-permute-start(bf16[528,128]{1,0:T(8,128)(2,1)} %get-tuple-element.20), channel_id=1, source_target_pairs={{0,32},{16,48},{32,0},{48,16},{1,33},{17,49},{33,1},{49,17},{2,34}... | collective-permute-start | bytes 405512 | tf_op jit(solution)/shard_map/ppermute | solution.py:253
  93.2 27.4 %collective-permute-start.9 = (bf16[528,128]{1,0:T(8,128)(2,1)}, bf16[528,128]{1,0:T(8,128)(2,1)S(1)}, u32[]{:S(2)}, u32[]{:S(2)}) collective-permute-start(bf16[528,128]{1,0:T(8,128)(2,1)} %get-tuple-element.21), channel_id=1, source_target_pairs={{0,48},{16,32},{32,16},{48,0},{1,49},{17,33},{33,17},{49,1},{2,50}... | collective-permute-start | bytes 405512 | tf_op jit(solution)/shard_map/ppermute | solution.py:253
  98.9 16.9 %collective-permute-start.2 = (f32[8,576]{1,0:T(8,128)S(1)}, f32[8,576]{1,0:T(8,128)S(1)}, u32[]{:S(2)}, u32[]{:S(2)}) collective-permute-start(f32[8,576]{1,0:T(8,128)S(1)} %pad_add_fusion.raw_a), channel_id=1, source_target_pairs={{0,1},{1,0},{2,3},{3,2},{4,5},{5,4},{6,7},{7,6},{8,9},{9,8},{10,11... | collective-permute-start | bytes 55304 | tf_op jit(solution)/shard_map/ppermute | solution.py:253
  117.3 9.3 %all-to-all-start.2 = ((bf16[4,32,512]{2,1,0:T(8,128)(2,1)}), bf16[4,32,512]{2,1,0:T(8,128)(2,1)S(1)}, u32[]{:S(2)}, u32[]{:S(2)}) async-start(bf16[4,32,512]{2,1,0:T(8,128)(2,1)} %shard_map.133), calls=%async_computation.2 | async-start | bytes 262144 | tf_op jit(solution)/shard_map/all_to_all | solution.py:349

commit v5 on v4

--- a/solution.py
+++ b/solution.py
@@ -25,7 +25,7 @@
 
 
 def flash_kernel(start, q0, q1, q2, q3, k1_hbm, k2_hbm, wuk_ref, wuv_ref, *refs):
-    targets, held, outs, sems = refs[:4], refs[4:10], refs[10:14], refs[14]
+    targets, held, outs, full_keys, sems = refs[:4], refs[4:10], refs[10:14], refs[14:16], refs[16]
     loads = [
         pltpu.make_async_copy(m, h, sems.at[i])
         for i, (m, h) in enumerate(zip((q0, q1, q2, q3, k1_hbm, k2_hbm), held))
@@ -58,9 +58,16 @@
             rows.append(jnp.concatenate([a.astype(jnp.bfloat16), rope], axis=1))
         full = jnp.concatenate(rows, axis=0)
         if not keys:
-            for load, ref in ((loads[4], k1_ref), (loads[5], k2_ref)):
+            for load, ref, whole in zip(loads[4:], (k1_ref, k2_ref), full_keys):
                 load.wait()
-                keys.append(ref[...].reshape(768, 576))
+                for n in range(8):
+                    at = n * 96
+                    for t in range(4):
+                        whole[at : at + 96, t * 128 : (t + 1) * 128] = ref[n, t * 96 : (t + 1) * 96, :]
+                    pair = ref[n, 384:, :]
+                    whole[at : at + 48, KV_RANK:] = pair[:, :64]
+                    whole[at + 48 : at + 96, KV_RANK:] = pair[:, 64:]
+                keys.append(whole[...])
         return [lax.dot_general(full, k, NT, preferred_element_type=jnp.float32) for k in keys]
 
     def weigh(s):
@@ -196,8 +203,11 @@
     out_ref[...] = acc.astype(jnp.bfloat16)
 
 
-def spread_kernel(x_ref, out_ref, sems):
-    moves = [pltpu.make_async_copy(x_ref, out_ref.at[i], sems.at[i]) for i in range(8)]
+def spread_kernel(x_ref, out_ref, held, sems):
+    for t in range(4):
+        held[t * 96 : (t + 1) * 96, :] = x_ref[:, t * 128 : (t + 1) * 128]
+    held[384:, :] = jnp.concatenate([x_ref[:48, KV_RANK:], x_ref[48:, KV_RANK:]], axis=1)
+    moves = [pltpu.make_async_copy(held, out_ref.at[i], sems.at[i]) for i in range(8)]
     for move in moves:
         move.start()
     for move in moves:
@@ -275,10 +285,10 @@
     hbm = pl.BlockSpec(memory_space=pltpu.HBM)
     spread = pl.pallas_call(
         spread_kernel,
-        out_shape=jax.ShapeDtypeStruct((8, 96, width), bf),
+        out_shape=jax.ShapeDtypeStruct((8, 432, 128), bf),
         in_specs=[pl.BlockSpec(memory_space=pltpu.VMEM)],
         out_specs=hbm,
-        scratch_shapes=[pltpu.SemaphoreType.DMA((8,))],
+        scratch_shapes=[pltpu.VMEM((432, 128), bf), pltpu.SemaphoreType.DMA((8,))],
         compiler_params=pltpu.CompilerParams(vmem_limit_bytes=4 << 20),
         cost_estimate=pl.CostEstimate(flops=1 << 10, bytes_accessed=1 << 20, transcendentals=0),
         name="spread",
@@ -320,7 +330,7 @@
     other_keys = trade(keys, "c", 1, 2)
     cache = lax.all_to_all(rows, CTX, 0, 0, tiled=True)
 
-    chunk, key = pltpu.VMEM((8, 96, 128), bf), pltpu.VMEM((8, 96, width), bf)
+    chunk, key = pltpu.VMEM((8, 96, 128), bf), pltpu.VMEM((8, 432, 128), bf)
     vmem = pl.BlockSpec(memory_space=pltpu.VMEM)
     parts = pl.pallas_call(
         flash_kernel,
@@ -330,6 +340,7 @@
         scratch_shapes=[chunk] * 4
         + [key] * 2
         + [pltpu.VMEM((512 + 16, 128), bf)] * 4
+        + [pltpu.VMEM((768, width), bf)] * 2
         + [pltpu.SemaphoreType.DMA((10,))],
         compiler_params=pltpu.CompilerParams(vmem_limit_bytes=28 << 20),
         cost_estimate=pl.CostEstimate(

time: 128 us -> 126 us (0.984)
  waiting for transfers between devices: 33.9 us -> 31.8 us
    all_to_all x1, waiting for transfers between devices: 25.6 us -> 23.5 us  [layer(): keys = lax.all_to_all(spread, 'z', 0, 0, tiled=True)]
where the time goes in v5:
time: 126 us
  starting transfers between devices  68.6 us (54%)
  waiting for transfers between devices  31.8 us (25%)
  Pallas kernels  21.1 us (17%)
  local copies, waits for them, and re-layouts  2.35 us (2%)
  between operations  1.64 us (1%)
    ppermute x10, starting transfers between devices, trade(): return lax.ppermute(v, axis, [(i, i ^ k) for i in range(n)])  47.3 us
    all_to_all x1, waiting for transfers between devices, layer(): keys = lax.all_to_all(spread, 'z', 0, 0, tiled=True)  23.5 us
    pallas_call x1, Pallas kernels, layer(): pl.pallas_call(flash_kernel, out_shape=[jax.ShapeDtypeStruct((512 + 16, 1...  13.5 us
    all_to_all x1, starting transfers between devices, layer(): keys = lax.all_to_all(spread, 'z', 0, 0, tiled=True)  10.3 us
    all_to_all x1, starting transfers between devices, layer(): cache = lax.all_to_all(rows, CTX, 0, 0, tiled=True)  7.55 us
    pallas_call x5, Pallas kernels, small(): pl.pallas_call(kernel, out_shape=outs, in_specs=[sm] * scalars + [vm] * (...  6.52 us
    all_to_all x1, waiting for transfers between devices, layer(): mixed = lax.all_to_all(mixed, 'x', 0, 0, tiled=True)  4.65 us
    ppermute x10, waiting for transfers between devices, trade(): return lax.ppermute(v, axis, [(i, i ^ k) for i in range(n)])  3.67 us
  transfers between devices with their start and end apart: 13, of which 3 were waited for; matrix products, arithmetic and copies ran while one was open for 0% of the time, Pallas kernels for 15%

profile of v5, /device:TPU:56, one launch (start us, length us, event | category | flops | bytes accessed | tf_op | source)
XLA Modules:
  0.0 125.6 jit_solution(15484941218571563165)
XLA Ops:
  0.6 1.0 copy-done.4
  1.6 1.1 spread.1
  2.7 10.3 %all-to-all-start = ((bf16[8,432,128]{2,1,0:T(8,128)(2,1)}), bf16[8,432,128]{2,1,0:T(8,128)(2,1)}, u32[]{:S(2)}, u32[]{:S(2)}) async-start(bf16[8,432,128]{2,1,0:T(8,128)(2,1)} %spread.1), calls=%async_computation | async-start | bytes 1769472 | tf_op jit(solution)/shard_map/all_to_all | solution.py:296
  13.1 1.8 %shard_map.132 = bf16[512,576]{1,0:T(8,128)(2,1)} custom-call(s32[1,256]{1,0:T(1,128)S(1)} %bitcast.15, bf16[4,576,256]{2,1,0:T(8,128)(2,1)S(1)} %bitcast.13), custom_call_target="tpu_custom_call" | custom-call | flops 134217728 | bytes 1048576 | tf_op jit(solution)/shard_map/pallas_call | solution.py:145
  14.9 23.5 %all-to-all-done.k1_hbm = bf16[8,432,128]{2,1,0:T(8,128)(2,1)} async-done(((bf16[8,432,128]{2,1,0:T(8,128)(2,1)}), bf16[8,432,128]{2,1,0:T(8,128)(2,1)}, u32[]{:S(2)}, u32[]{:S(2)}) %all-to-all-start) | async-done | bytes 884768 | tf_op jit(solution)/shard_map/all_to_all | solution.py:296
  38.4 1.9 %collective-permute-start.6 = (bf16[8,432,128]{2,1,0:T(8,128)(2,1)}, bf16[8,432,128]{2,1,0:T(8,128)(2,1)}, u32[]{:S(2)}, u32[]{:S(2)}) collective-permute-start(bf16[8,432,128]{2,1,0:T(8,128)(2,1)} %all-to-all-done.k1_hbm), channel_id=1, source_target_pairs={{0,8},{8,0},{1,9},{9,1},{2,10},{10,2},{3,11},{11,3},{4,12},{12,4},... | collective-permute-start | bytes 2654216 | tf_op jit(solution)/shard_map/ppermute | solution.py:263
  40.4 0.1 maximum_maximum_fusion.q0
  40.5 4.0 %collective-permute-start.3 = (bf16[8,96,128]{2,1,0:T(8,128)(2,1)S(1)}, bf16[8,96,128]{2,1,0:T(8,128)(2,1)S(1)}, u32[]{:S(2)}, u32[]{:S(2)}) collective-permute-start(bf16[8,96,128]{2,1,0:T(8,128)(2,1)S(1)} %maximum_maximum_fusion.q0), channel_id=1, source_target_pairs={{0,16},{16,0},{32,48},{48,32},{1,17},{17,1},{33,49},{49,33},{2,18}... | collective-permute-start | bytes 589832 | tf_op jit(solution)/shard_map/ppermute | solution.py:263
  44.6 2.9 %collective-permute-start.4 = (bf16[8,96,128]{2,1,0:T(8,128)(2,1)S(1)}, bf16[8,96,128]{2,1,0:T(8,128)(2,1)}, u32[]{:S(2)}, u32[]{:S(2)}) collective-permute-start(bf16[8,96,128]{2,1,0:T(8,128)(2,1)S(1)} %maximum_maximum_fusion.q0), channel_id=1, source_target_pairs={{0,32},{16,48},{32,0},{48,16},{1,33},{17,49},{33,1},{49,17},{2,34}... | collective-permute-start | bytes 589832 | tf_op jit(solution)/shard_map/ppermute | solution.py:263
  47.5 5.3 %collective-permute-start.5 = (bf16[8,96,128]{2,1,0:T(8,128)(2,1)S(1)}, bf16[8,96,128]{2,1,0:T(8,128)(2,1)}, u32[]{:S(2)}, u32[]{:S(2)}) collective-permute-start(bf16[8,96,128]{2,1,0:T(8,128)(2,1)S(1)} %maximum_maximum_fusion.q0), channel_id=1, source_target_pairs={{0,48},{16,32},{32,16},{48,0},{1,49},{17,33},{33,17},{49,1},{2,50}... | collective-permute-start | bytes 589832 | tf_op jit(solution)/shard_map/ppermute | solution.py:263
  52.8 0.0 copy-start.3
  52.8 1.2 copy-done.3
  54.0 0.8 shard_map.131
  54.9 0.0 copy-start.10
  54.9 0.0 copy-start.1
  54.9 5.1 %collective-permute-start = (bf16[80,576]{1,0:T(8,128)(2,1)S(1)}, bf16[80,576]{1,0:T(8,128)(2,1)S(1)}, u32[]{:S(2)}, u32[]{:S(2)}) collective-permute-start(bf16[80,576]{1,0:T(8,128)(2,1)S(1)} %get-tuple-element.15), channel_id=1, source_target_pairs={{0,4},{2,6},{4,0},{6,2},{1,5},{3,7},{5,1},{7,3},{8,12},{10,14},{12... | collective-permute-start | bytes 276488 | tf_op jit(solution)/shard_map/ppermute | solution.py:263
  60.0 7.6 %all-to-all-start.1 = ((bf16[64,8,576]{2,1,0:T(8,128)(2,1)}), bf16[64,8,576]{2,1,0:T(8,128)(2,1)S(1)}, u32[]{:S(2)}, u32[]{:S(2)}) async-start(bf16[64,8,576]{2,1,0:T(8,128)(2,1)} %bitcast.5), calls=%async_computation.1 | async-start | bytes 1310720 | tf_op jit(solution)/shard_map/all_to_all | solution.py:331
  68.2 0.0 collective-permute-done.p2
  68.2 0.0 copy-start.9
  68.3 2.7 %collective-permute-start.1 = (bf16[80,576]{1,0:T(8,128)(2,1)S(1)}, bf16[80,576]{1,0:T(8,128)(2,1)S(1)}, u32[]{:S(2)}, u32[]{:S(2)}) collective-permute-start(bf16[80,576]{1,0:T(8,128)(2,1)S(1)} %pad_maximum_fusion), channel_id=1, source_target_pairs={{0,2},{2,0},{4,6},{6,4},{1,3},{3,1},{5,7},{7,5},{8,10},{10,8},{12,... | collective-permute-start | bytes 276488 | tf_op jit(solution)/shard_map/ppermute | solution.py:263
  71.0 0.0 collective-permute-done.4.q2
  71.0 13.5 %flash.1 = (bf16[528,128]{1,0:T(8,128)(2,1)S(1)}, bf16[528,128]{1,0:T(8,128)(2,1)}, bf16[528,128]{1,0:T(8,128)(2,1)}, bf16[528,128]{1,0:T(8,128)(2,1)}) custom-call(s32[1]{0:T(128)S(6)} %copy.17.start, bf16[8,96,128]{2,1,0:T(8,128)(2,1)S(1)} %maximum_maximum_fusion.q0, bf16[8,96,128]{2,1,0:T(8,128)(2,1)S(1)} %collective-permute-done.3.q1, ...), custom_call_target="tpu_custom_call" | custom-call | flops 6920601600 | bytes 4194304 | tf_op jit(solution)/shard_map/flash/pallas_call | solution.py:335
  84.5 4.3 %collective-permute-start.7 = (bf16[528,128]{1,0:T(8,128)(2,1)}, bf16[528,128]{1,0:T(8,128)(2,1)S(1)}, u32[]{:S(2)}, u32[]{:S(2)}) collective-permute-start(bf16[528,128]{1,0:T(8,128)(2,1)} %get-tuple-element.19), channel_id=1, source_target_pairs={{0,16},{16,0},{32,48},{48,32},{1,17},{17,1},{33,49},{49,33},{2,18}... | collective-permute-start | bytes 405512 | tf_op jit(solution)/shard_map/ppermute | solution.py:263
  88.8 2.4 %collective-permute-start.8 = (bf16[528,128]{1,0:T(8,128)(2,1)}, bf16[528,128]{1,0:T(8,128)(2,1)S(1)}, u32[]{:S(2)}, u32[]{:S(2)}) collective-permute-start(bf16[528,128]{1,0:T(8,128)(2,1)} %get-tuple-element.20), channel_id=1, source_target_pairs={{0,32},{16,48},{32,0},{48,16},{1,33},{17,49},{33,1},{49,17},{2,34}... | collective-permute-start | bytes 405512 | tf_op jit(solution)/shard_map/ppermute | solution.py:263
  91.2 5.6 %collective-permute-start.9 = (bf16[528,128]{1,0:T(8,128)(2,1)}, bf16[528,128]{1,0:T(8,128)(2,1)S(1)}, u32[]{:S(2)}, u32[]{:S(2)}) collective-permute-start(bf16[528,128]{1,0:T(8,128)(2,1)} %get-tuple-element.21), channel_id=1, source_target_pairs={{0,48},{16,32},{32,16},{48,0},{1,49},{17,33},{33,17},{49,1},{2,50}... | collective-permute-start | bytes 405512 | tf_op jit(solution)/shard_map/ppermute | solution.py:263
  96.8 13.2 %collective-permute-start.2 = (f32[8,576]{1,0:T(8,128)S(1)}, f32[8,576]{1,0:T(8,128)S(1)}, u32[]{:S(2)}, u32[]{:S(2)}) collective-permute-start(f32[8,576]{1,0:T(8,128)S(1)} %pad_add_fusion.raw_a), channel_id=1, source_target_pairs={{0,1},{1,0},{2,3},{3,2},{4,5},{5,4},{6,7},{7,6},{8,9},{9,8},{10,11... | collective-permute-start | bytes 55304 | tf_op jit(solution)/shard_map/ppermute | solution.py:263
  110.0 3.6 %collective-permute-done.2.raw_b = f32[8,576]{1,0:T(8,128)S(1)} collective-permute-done((f32[8,576]{1,0:T(8,128)S(1)}, f32[8,576]{1,0:T(8,128)S(1)}, u32[]{:S(2)}, u32[]{:S(2)}) %collective-permute-start.2) | collective-permute-done | bytes 18464 | tf_op jit(solution)/shard_map/ppermute | solution.py:263
  113.7 1.5 %shard_map.133 = bf16[4,32,512]{2,1,0:T(8,128)(2,1)} custom-call(bf16[40,576]{1,0:T(8,128)(2,1)S(1)} %get-tuple-element.13.p0, bf16[80,576]{1,0:T(8,128)(2,1)S(1)} %collective-permute-done.1.p13, bf16[80,576]{1,0:T(8,128)(2,1)S(1)} %collective-permute-done.p2, f32[8,576]{1,0:T(8,128)S(1)} %pad_add_fusion.raw_a, f32[8,576]{1,0:T(8,128)S(1)} %collective-permute-done.2.raw_b, ...), custom_call_target="tpu_custom_call" | custom-call | flops 134217728 | bytes 1048576 | tf_op jit(solution)/shard_map/pallas_call | solution.py:145
  115.2 3.3 %all-to-all-start.2 = ((bf16[4,32,512]{2,1,0:T(8,128)(2,1)}), bf16[4,32,512]{2,1,0:T(8,128)(2,1)S(1)}, u32[]{:S(2)}, u32[]{:S(2)}) async-start(bf16[4,32,512]{2,1,0:T(8,128)(2,1)} %shard_map.133), calls=%async_computation.2 | async-start | bytes 262144 | tf_op jit(solution)/shard_map/all_to_all | solution.py:360
  118.6 1.3 %shard_map.134 = bf16[512,128]{1,0:T(8,128)(2,1)} custom-call(bf16[528,128]{1,0:T(8,128)(2,1)S(1)} %get-tuple-element.18.a_ref, bf16[528,128]{1,0:T(8,128)(2,1)S(1)} %collective-permute-done.7.b_ref, bf16[528,128]{1,0:T(8,128)(2,1)S(1)} %collective-permute-done.8.c_ref, bf16[528,128]{1,0:T(8,128)(2,1)S(1)} %collective-permute-done.9.d_ref), custom_call_target="tpu_custom_call" | custom-call | flops 134217728 | bytes 1048576 | tf_op jit(solution)/shard_map/pallas_call | solution.py:145
  119.9 4.7 %all-to-all-done.2.m_ref = bf16[4,32,512]{2,1,0:T(8,128)(2,1)S(1)} async-done(((bf16[4,32,512]{2,1,0:T(8,128)(2,1)}), bf16[4,32,512]{2,1,0:T(8,128)(2,1)S(1)}, u32[]{:S(2)}, u32[]{:S(2)}) %all-to-all-start.2) | async-done | bytes 131104 | tf_op jit(solution)/shard_map/all_to_all | solution.py:360
  124.5 1.0 shard_map.135
  (31 shorter events, 0.2 us)
Async XLA Ops:
  0.6 12.4 %copy-start = (bf16[256,4,576]{0,2,1:T(8,128)(2,1)S(1)}, bf16[256,4,576]{0,2,1:T(8,128)(2,1)}, u32[]{:S(2)}) copy-start(bf16[256,4,576]{0,2,1:T(8,128)(2,1)} %param.17) | copy-start | bytes 3538948
  0.6 1.0 copy-start.4
  1.6 11.4 %copy-start.7 = (s32[256]{0:T(256)S(1)}, s32[256]{0:T(256)}, u32[]{:S(2)}) copy-start(s32[256]{0:T(256)} %param.18) | copy-start | bytes 3076
  2.7 35.7 %all-to-all-start = ((bf16[8,432,128]{2,1,0:T(8,128)(2,1)}), bf16[8,432,128]{2,1,0:T(8,128)(2,1)}, u32[]{:S(2)}, u32[]{:S(2)}) async-start(bf16[8,432,128]{2,1,0:T(8,128)(2,1)} %spread.1), calls=%async_computation | async-start | bytes 1769472 | tf_op jit(solution)/shard_map/all_to_all | solution.py:296
  13.1 27.2 %copy-start.8 = (bf16[64,8,192]{2,1,0:T(8,128)(2,1)S(1)}, bf16[64,8,192]{2,1,0:T(8,128)(2,1)}, u32[]{:S(2)}) copy-start(bf16[64,8,192]{2,1,0:T(8,128)(2,1)} %param.13) | copy-start | bytes 589828
  14.9 37.9 %copy-start.2 = (bf16[8,128,512]{2,1,0:T(8,128)(2,1)S(1)}, bf16[8,128,512]{2,1,0:T(8,128)(2,1)}, u32[]{:S(2)}) copy-start(bf16[8,128,512]{2,1,0:T(8,128)(2,1)} %wuk_ref.3) | copy-start | bytes 3145732
  14.9 37.9 %copy-start.5 = (bf16[4,4,8,192]{3,2,1,0:T(8,128)(2,1)S(1)}, bf16[4,4,8,192]{3,2,1,0:T(8,128)(2,1)}, u32[]{:S(2)}) copy-start(bf16[4,4,8,192]{3,2,1,0:T(8,128)(2,1)} %q_ref.1) | copy-start | bytes 147460
  14.9 37.9 %copy-start.6 = (bf16[4,4,896]{2,1,0:T(4,128)(2,1)S(1)}, bf16[4,4,896]{2,1,0:T(4,128)(2,1)}, u32[]{:S(2)}) copy-start(bf16[4,4,896]{2,1,0:T(4,128)(2,1)} %hid_ref.1) | copy-start | bytes 86020
  38.4 32.6 %collective-permute-start.6 = (bf16[8,432,128]{2,1,0:T(8,128)(2,1)}, bf16[8,432,128]{2,1,0:T(8,128)(2,1)}, u32[]{:S(2)}, u32[]{:S(2)}) collective-permute-start(bf16[8,432,128]{2,1,0:T(8,128)(2,1)} %all-to-all-done.k1_hbm), channel_id=1, source_target_pairs={{0,8},{8,0},{1,9},{9,1},{2,10},{10,2},{3,11},{11,3},{4,12},{12,4},... | collective-permute-start | bytes 2654216 | tf_op jit(solution)/shard_map/ppermute | solution.py:263
  40.5 30.4 %collective-permute-start.3 = (bf16[8,96,128]{2,1,0:T(8,128)(2,1)S(1)}, bf16[8,96,128]{2,1,0:T(8,128)(2,1)S(1)}, u32[]{:S(2)}, u32[]{:S(2)}) collective-permute-start(bf16[8,96,128]{2,1,0:T(8,128)(2,1)S(1)} %maximum_maximum_fusion.q0), channel_id=1, source_target_pairs={{0,16},{16,0},{32,48},{48,32},{1,17},{17,1},{33,49},{49,33},{2,18}... | collective-permute-start | bytes 589832 | tf_op jit(solution)/shard_map/ppermute | solution.py:263
  44.6 26.4 %collective-permute-start.4 = (bf16[8,96,128]{2,1,0:T(8,128)(2,1)S(1)}, bf16[8,96,128]{2,1,0:T(8,128)(2,1)}, u32[]{:S(2)}, u32[]{:S(2)}) collective-permute-start(bf16[8,96,128]{2,1,0:T(8,128)(2,1)S(1)} %maximum_maximum_fusion.q0), channel_id=1, source_target_pairs={{0,32},{16,48},{32,0},{48,16},{1,33},{17,49},{33,1},{49,17},{2,34}... | collective-permute-start | bytes 589832 | tf_op jit(solution)/shard_map/ppermute | solution.py:263
  47.5 23.5 %collective-permute-start.5 = (bf16[8,96,128]{2,1,0:T(8,128)(2,1)S(1)}, bf16[8,96,128]{2,1,0:T(8,128)(2,1)}, u32[]{:S(2)}, u32[]{:S(2)}) collective-permute-start(bf16[8,96,128]{2,1,0:T(8,128)(2,1)S(1)} %maximum_maximum_fusion.q0), channel_id=1, source_target_pairs={{0,48},{16,32},{32,16},{48,0},{1,49},{17,33},{33,17},{49,1},{2,50}... | collective-permute-start | bytes 589832 | tf_op jit(solution)/shard_map/ppermute | solution.py:263
  52.8 1.2 copy-start.3
  54.9 12.7 %copy-start.10 = (s32[4]{0:T(128)S(1)}, s32[4]{0:T(128)}, u32[]{:S(2)}) copy-start(s32[4]{0:T(128)} %param.19) | copy-start | bytes 52
  54.9 16.1 %copy-start.1 = (bf16[8,512,128]{2,1,0:T(8,128)(2,1)S(1)}, bf16[8,512,128]{2,1,0:T(8,128)(2,1)}, u32[]{:S(2)}) copy-start(bf16[8,512,128]{2,1,0:T(8,128)(2,1)} %wuv_ref.3) | copy-start | bytes 3145732
  54.9 13.3 %collective-permute-start = (bf16[80,576]{1,0:T(8,128)(2,1)S(1)}, bf16[80,576]{1,0:T(8,128)(2,1)S(1)}, u32[]{:S(2)}, u32[]{:S(2)}) collective-permute-start(bf16[80,576]{1,0:T(8,128)(2,1)S(1)} %get-tuple-element.15), channel_id=1, source_target_pairs={{0,4},{2,6},{4,0},{6,2},{1,5},{3,7},{5,1},{7,3},{8,12},{10,14},{12... | collective-permute-start | bytes 276488 | tf_op jit(solution)/shard_map/ppermute | solution.py:263
  60.0 53.7 %all-to-all-start.1 = ((bf16[64,8,576]{2,1,0:T(8,128)(2,1)}), bf16[64,8,576]{2,1,0:T(8,128)(2,1)S(1)}, u32[]{:S(2)}, u32[]{:S(2)}) async-start(bf16[64,8,576]{2,1,0:T(8,128)(2,1)} %bitcast.5), calls=%async_computation.1 | async-start | bytes 1310720 | tf_op jit(solution)/shard_map/all_to_all | solution.py:331
  68.2 28.5 %copy-start.9 = (f32[512]{0:T(512)S(1)}, f32[512]{0:T(512)}, u32[]{:S(2)}) copy-start(f32[512]{0:T(512)} %param.23) | copy-start | bytes 6148
  68.3 28.5 %collective-permute-start.1 = (bf16[80,576]{1,0:T(8,128)(2,1)S(1)}, bf16[80,576]{1,0:T(8,128)(2,1)S(1)}, u32[]{:S(2)}, u32[]{:S(2)}) collective-permute-start(bf16[80,576]{1,0:T(8,128)(2,1)S(1)} %pad_maximum_fusion), channel_id=1, source_target_pairs={{0,2},{2,0},{4,6},{6,4},{1,3},{3,1},{5,7},{7,5},{8,10},{10,8},{12,... | collective-permute-start | bytes 276488 | tf_op jit(solution)/shard_map/ppermute | solution.py:263
  84.5 34.0 %collective-permute-start.7 = (bf16[528,128]{1,0:T(8,128)(2,1)}, bf16[528,128]{1,0:T(8,128)(2,1)S(1)}, u32[]{:S(2)}, u32[]{:S(2)}) collective-permute-start(bf16[528,128]{1,0:T(8,128)(2,1)} %get-tuple-element.19), channel_id=1, source_target_pairs={{0,16},{16,0},{32,48},{48,32},{1,17},{17,1},{33,49},{49,33},{2,18}... | collective-permute-start | bytes 405512 | tf_op jit(solution)/shard_map/ppermute | solution.py:263
  88.8 29.8 %collective-permute-start.8 = (bf16[528,128]{1,0:T(8,128)(2,1)}, bf16[528,128]{1,0:T(8,128)(2,1)S(1)}, u32[]{:S(2)}, u32[]{:S(2)}) collective-permute-start(bf16[528,128]{1,0:T(8,128)(2,1)} %get-tuple-element.20), channel_id=1, source_target_pairs={{0,32},{16,48},{32,0},{48,16},{1,33},{17,49},{33,1},{49,17},{2,34}... | collective-permute-start | bytes 405512 | tf_op jit(solution)/shard_map/ppermute | solution.py:263
  91.2 27.4 %collective-permute-start.9 = (bf16[528,128]{1,0:T(8,128)(2,1)}, bf16[528,128]{1,0:T(8,128)(2,1)S(1)}, u32[]{:S(2)}, u32[]{:S(2)}) collective-permute-start(bf16[528,128]{1,0:T(8,128)(2,1)} %get-tuple-element.21), channel_id=1, source_target_pairs={{0,48},{16,32},{32,16},{48,0},{1,49},{17,33},{33,17},{49,1},{2,50}... | collective-permute-start | bytes 405512 | tf_op jit(solution)/shard_map/ppermute | solution.py:263
  96.8 16.9 %collective-permute-start.2 = (f32[8,576]{1,0:T(8,128)S(1)}, f32[8,576]{1,0:T(8,128)S(1)}, u32[]{:S(2)}, u32[]{:S(2)}) collective-permute-start(f32[8,576]{1,0:T(8,128)S(1)} %pad_add_fusion.raw_a), channel_id=1, source_target_pairs={{0,1},{1,0},{2,3},{3,2},{4,5},{5,4},{6,7},{7,6},{8,9},{9,8},{10,11... | collective-permute-start | bytes 55304 | tf_op jit(solution)/shard_map/ppermute | solution.py:263
  115.2 9.3 %all-to-all-start.2 = ((bf16[4,32,512]{2,1,0:T(8,128)(2,1)}), bf16[4,32,512]{2,1,0:T(8,128)(2,1)S(1)}, u32[]{:S(2)}, u32[]{:S(2)}) async-start(bf16[4,32,512]{2,1,0:T(8,128)(2,1)} %shard_map.133), calls=%async_computation.2 | async-start | bytes 262144 | tf_op jit(solution)/shard_map/all_to_all | solution.py:360

commit v6 on v5

--- a/solution.py
+++ b/solution.py
@@ -194,11 +194,11 @@
 
 
 def pack_kernel(owner_ref, x_ref, out_ref):
-    row = lax.broadcasted_iota(jnp.int32, (512, 256), 0)
-    hit = owner_ref[...] == ((row >> 3) * 4 + lax.axis_index("x"))
-    acc = jnp.zeros((512, KV_RANK + ROPE), jnp.float32)
+    row = lax.broadcasted_iota(jnp.int32, (256, 256), 0)
+    hit = owner_ref[...] == ((row >> 2) * 4 + lax.axis_index("x"))
+    acc = jnp.zeros((256, KV_RANK + ROPE), jnp.float32)
     for j in range(4):
-        pick = jnp.where(hit & ((row & 7) == j), 1.0, 0.0).astype(jnp.bfloat16)
+        pick = jnp.where(hit & ((row & 3) == j), 1.0, 0.0).astype(jnp.bfloat16)
         acc = acc + lax.dot_general(pick, x_ref[j], NT, preferred_element_type=jnp.float32)
     out_ref[...] = acc.astype(jnp.bfloat16)
 
@@ -227,9 +227,8 @@
     cache = cache_ref[...]
     s1 = lax.dot_general(q, cache, NT, preferred_element_type=jnp.float32)
     s2 = lax.dot_general(q, fresh, NT, preferred_element_type=jnp.float32)
-    j = lax.broadcasted_iota(jnp.int32, (128, 512), 1)
-    held = ((j & 7) < 4) & ((j >> 3) * 4 + (j & 7) < length)
-    s1 = jnp.where(held, s1, -1e30)
+    j = lax.broadcasted_iota(jnp.int32, (128, 256), 1)
+    s1 = jnp.where(j < length, s1, -1e30)
     step = (lax.broadcasted_iota(jnp.int32, (128, 8), 0) >> 3) & 3
     s2 = jnp.where(lax.broadcasted_iota(jnp.int32, (128, 8), 1) <= step, s2, -1e30)
     top = jnp.maximum(jnp.max(s1, axis=1, keepdims=True), jnp.max(s2, axis=1, keepdims=True))
@@ -322,9 +321,9 @@
     raw_there = trade(raw_here, "yl", 1, 2)
     rows = small(
         pack_kernel,
-        jax.ShapeDtypeStruct((512, width), bf),
+        jax.ShapeDtypeStruct((256, width), bf),
         [owner_slot.reshape(1, 256), jnp.transpose(decode_latent, (1, 2, 0))],
-    ).reshape(64, 8, width)
+    ).reshape(64, 4, width)
 
     keys, rows = fence((keys, rows))
     other_keys = trade(keys, "c", 1, 2)
@@ -355,7 +354,7 @@
     mixed = small(
         attend_kernel,
         jax.ShapeDtypeStruct((4, 32, KV_RANK), bf),
-        [*got, raw_here, raw_there, cache.reshape(512, width)],
+        [*got, raw_here, raw_there, cache.reshape(256, width)],
     )
     mixed = lax.all_to_all(mixed, "x", 0, 0, tiled=True)
     mixed, merged = fence((mixed, merge(parts)))

time: 126 us -> 121 us (0.960)
  the two profiles are of different devices: /device:TPU:56 before, /device:TPU:1 now
where the time goes in v6:
time: 121 us; the launch traced here: 120 us
  starting transfers between devices  59.5 us (49%)
  waiting for transfers between devices  34.6 us (29%)
  Pallas kernels  19.6 us (16%)
  local copies, waits for them, and re-layouts  4.03 us (3%)
  between operations  1.64 us (1%)
    ppermute x10, starting transfers between devices, trade(): return lax.ppermute(v, axis, [(i, i ^ k) for i in range(n)])  35.6 us
    all_to_all x1, waiting for transfers between devices, layer(): keys = lax.all_to_all(spread, 'z', 0, 0, tiled=True)  24.4 us
    pallas_call x1, Pallas kernels, layer(): pl.pallas_call(flash_kernel, out_shape=[jax.ShapeDtypeStruct((512 + 16, 1...  13.4 us
    all_to_all x1, starting transfers between devices, layer(): keys = lax.all_to_all(spread, 'z', 0, 0, tiled=True)  10.9 us
    all_to_all x1, starting transfers between devices, layer(): cache = lax.all_to_all(rows, CTX, 0, 0, tiled=True)  9.26 us
    ppermute x10, waiting for transfers between devices, trade(): return lax.ppermute(v, axis, [(i, i ^ k) for i in range(n)])  6.79 us
    pallas_call x5, Pallas kernels, small(): pl.pallas_call(kernel, out_shape=outs, in_specs=[sm] * scalars + [vm] * (...  5.06 us
    all_to_all x1, starting transfers between devices, layer(): mixed = lax.all_to_all(mixed, 'x', 0, 0, tiled=True)  3.74 us
  transfers between devices with their start and end apart: 13, of which 4 were waited for; matrix products, arithmetic and copies ran while one was open for 3% of the time, Pallas kernels for 15%

profile of v6, /device:TPU:1, one launch (start us, length us, event | category | flops | bytes accessed | tf_op | source)
XLA Modules:
  0.0 119.5 jit_solution(10861455327175841908)
XLA Ops:
  0.6 1.0 copy-done.4
  1.6 1.1 spread.1
  2.8 10.9 %all-to-all-start = ((bf16[8,432,128]{2,1,0:T(8,128)(2,1)}), bf16[8,432,128]{2,1,0:T(8,128)(2,1)}, u32[]{:S(2)}, u32[]{:S(2)}) async-start(bf16[8,432,128]{2,1,0:T(8,128)(2,1)} %spread.1), calls=%async_computation | async-start | bytes 1769472 | tf_op jit(solution)/shard_map/all_to_all | solution.py:295
  13.6 0.0 copy-start.6
  13.6 0.6 shard_map.132
  14.2 0.0 copy-start.3
  14.2 0.8 reshape.17
  15.1 24.4 %all-to-all-done.k1_hbm = bf16[8,432,128]{2,1,0:T(8,128)(2,1)} async-done(((bf16[8,432,128]{2,1,0:T(8,128)(2,1)}), bf16[8,432,128]{2,1,0:T(8,128)(2,1)}, u32[]{:S(2)}, u32[]{:S(2)}) %all-to-all-start) | async-done | bytes 884768 | tf_op jit(solution)/shard_map/all_to_all | solution.py:295
  39.4 2.4 %collective-permute-start.6 = (bf16[8,432,128]{2,1,0:T(8,128)(2,1)}, bf16[8,432,128]{2,1,0:T(8,128)(2,1)}, u32[]{:S(2)}, u32[]{:S(2)}) collective-permute-start(bf16[8,432,128]{2,1,0:T(8,128)(2,1)} %all-to-all-done.k1_hbm), channel_id=1, source_target_pairs={{0,8},{8,0},{1,9},{9,1},{2,10},{10,2},{3,11},{11,3},{4,12},{12,4},... | collective-permute-start | bytes 2654216 | tf_op jit(solution)/shard_map/ppermute | solution.py:262
  41.8 1.0 copy.17
  42.9 0.1 maximum_maximum_fusion.q0
  43.0 0.0 copy-start.9
  43.0 5.9 %collective-permute-start.5 = (bf16[8,96,128]{2,1,0:T(8,128)(2,1)S(1)}, bf16[8,96,128]{2,1,0:T(8,128)(2,1)}, u32[]{:S(2)}, u32[]{:S(2)}) collective-permute-start(bf16[8,96,128]{2,1,0:T(8,128)(2,1)S(1)} %maximum_maximum_fusion.q0), channel_id=1, source_target_pairs={{0,48},{16,32},{32,16},{48,0},{1,49},{17,33},{33,17},{49,1},{2,50}... | collective-permute-start | bytes 589832 | tf_op jit(solution)/shard_map/ppermute | solution.py:262
  48.9 3.5 %collective-permute-start.4 = (bf16[8,96,128]{2,1,0:T(8,128)(2,1)S(1)}, bf16[8,96,128]{2,1,0:T(8,128)(2,1)}, u32[]{:S(2)}, u32[]{:S(2)}) collective-permute-start(bf16[8,96,128]{2,1,0:T(8,128)(2,1)S(1)} %maximum_maximum_fusion.q0), channel_id=1, source_target_pairs={{0,32},{16,48},{32,0},{48,16},{1,33},{17,49},{33,1},{49,17},{2,34}... | collective-permute-start | bytes 589832 | tf_op jit(solution)/shard_map/ppermute | solution.py:262
  52.4 2.4 %collective-permute-start.3 = (bf16[8,96,128]{2,1,0:T(8,128)(2,1)S(1)}, bf16[8,96,128]{2,1,0:T(8,128)(2,1)}, u32[]{:S(2)}, u32[]{:S(2)}) collective-permute-start(bf16[8,96,128]{2,1,0:T(8,128)(2,1)S(1)} %maximum_maximum_fusion.q0), channel_id=1, source_target_pairs={{0,16},{16,0},{32,48},{48,32},{1,17},{17,1},{33,49},{49,33},{2,18}... | collective-permute-start | bytes 589832 | tf_op jit(solution)/shard_map/ppermute | solution.py:262
  54.9 0.8 shard_map.131
  55.7 4.7 %collective-permute-start = (bf16[80,576]{1,0:T(8,128)(2,1)S(1)}, bf16[80,576]{1,0:T(8,128)(2,1)S(1)}, u32[]{:S(2)}, u32[]{:S(2)}) collective-permute-start(bf16[80,576]{1,0:T(8,128)(2,1)S(1)} %get-tuple-element.15), channel_id=1, source_target_pairs={{0,4},{2,6},{4,0},{6,2},{1,5},{3,7},{5,1},{7,3},{8,12},{10,14},{12... | collective-permute-start | bytes 276488 | tf_op jit(solution)/shard_map/ppermute | solution.py:262
  61.0 2.0 %collective-permute-done.p2 = bf16[80,576]{1,0:T(8,128)(2,1)S(1)} collective-permute-done((bf16[80,576]{1,0:T(8,128)(2,1)S(1)}, bf16[80,576]{1,0:T(8,128)(2,1)S(1)}, u32[]{:S(2)}, u32[]{:S(2)}) %collective-permute-start) | collective-permute-done | bytes 92192 | tf_op jit(solution)/shard_map/ppermute | solution.py:262
  63.1 3.1 %collective-permute-start.1 = (bf16[80,576]{1,0:T(8,128)(2,1)S(1)}, bf16[80,576]{1,0:T(8,128)(2,1)S(1)}, u32[]{:S(2)}, u32[]{:S(2)}) collective-permute-start(bf16[80,576]{1,0:T(8,128)(2,1)S(1)} %pad_maximum_fusion), channel_id=1, source_target_pairs={{0,2},{2,0},{4,6},{6,4},{1,3},{3,1},{5,7},{7,5},{8,10},{10,8},{12,... | collective-permute-start | bytes 276488 | tf_op jit(solution)/shard_map/ppermute | solution.py:262
  66.2 9.3 %all-to-all-start.1 = ((bf16[64,4,576]{2,1,0:T(4,128)(2,1)}), bf16[64,4,576]{2,1,0:T(4,128)(2,1)}, u32[]{:S(2)}, u32[]{:S(2)}) async-start(bf16[64,4,576]{2,1,0:T(4,128)(2,1)} %reshape.17), calls=%async_computation.1 | async-start | bytes 655360 | tf_op jit(solution)/shard_map/all_to_all | solution.py:330
  75.5 13.4 %flash.1 = (bf16[528,128]{1,0:T(8,128)(2,1)S(1)}, bf16[528,128]{1,0:T(8,128)(2,1)S(1)}, bf16[528,128]{1,0:T(8,128)(2,1)S(1)}, bf16[528,128]{1,0:T(8,128)(2,1)S(1)}) custom-call(s32[1]{0:T(128)S(6)} %copy.18.start, bf16[8,96,128]{2,1,0:T(8,128)(2,1)S(1)} %maximum_maximum_fusion.q0, bf16[8,96,128]{2,1,0:T(8,128)(2,1)} %collective-permute-done.3.q1, ...), custom_call_target="tpu_custom_call" | custom-call | flops 6920601600 | bytes 4194304 | tf_op jit(solution)/shard_map/flash/pallas_call | solution.py:334
  89.0 4.2 %collective-permute-start.7 = (bf16[528,128]{1,0:T(8,128)(2,1)S(1)}, bf16[528,128]{1,0:T(8,128)(2,1)S(1)}, u32[]{:S(2)}, u32[]{:S(2)}) collective-permute-start(bf16[528,128]{1,0:T(8,128)(2,1)S(1)} %get-tuple-element.19), channel_id=1, source_target_pairs={{0,16},{16,0},{32,48},{48,32},{1,17},{17,1},{33,49},{49,33},{2,18}... | collective-permute-start | bytes 405512 | tf_op jit(solution)/shard_map/ppermute | solution.py:262
  93.1 5.2 %collective-permute-start.8 = (bf16[528,128]{1,0:T(8,128)(2,1)S(1)}, bf16[528,128]{1,0:T(8,128)(2,1)S(1)}, u32[]{:S(2)}, u32[]{:S(2)}) collective-permute-start(bf16[528,128]{1,0:T(8,128)(2,1)S(1)} %get-tuple-element.20), channel_id=1, source_target_pairs={{0,32},{16,48},{32,0},{48,16},{1,33},{17,49},{33,1},{49,17},{2,34}... | collective-permute-start | bytes 405512 | tf_op jit(solution)/shard_map/ppermute | solution.py:262
  98.4 2.0 %collective-permute-start.9 = (bf16[528,128]{1,0:T(8,128)(2,1)S(1)}, bf16[528,128]{1,0:T(8,128)(2,1)S(1)}, u32[]{:S(2)}, u32[]{:S(2)}) collective-permute-start(bf16[528,128]{1,0:T(8,128)(2,1)S(1)} %get-tuple-element.21), channel_id=1, source_target_pairs={{0,48},{16,32},{32,16},{48,0},{1,49},{17,33},{33,17},{49,1},{2,50}... | collective-permute-start | bytes 405512 | tf_op jit(solution)/shard_map/ppermute | solution.py:262
  100.4 2.3 %collective-permute-start.2 = (f32[8,576]{1,0:T(8,128)S(1)}, f32[8,576]{1,0:T(8,128)S(1)}, u32[]{:S(2)}, u32[]{:S(2)}) collective-permute-start(f32[8,576]{1,0:T(8,128)S(1)} %pad_add_fusion.raw_a), channel_id=1, source_target_pairs={{0,1},{1,0},{2,3},{3,2},{4,5},{5,4},{6,7},{7,6},{8,9},{9,8},{10,11... | collective-permute-start | bytes 55304 | tf_op jit(solution)/shard_map/ppermute | solution.py:262
  102.7 1.1 reshape.18.cache_ref
  103.9 4.7 %collective-permute-done.2.raw_b = f32[8,576]{1,0:T(8,128)S(1)} collective-permute-done((f32[8,576]{1,0:T(8,128)S(1)}, f32[8,576]{1,0:T(8,128)S(1)}, u32[]{:S(2)}, u32[]{:S(2)}) %collective-permute-start.2) | collective-permute-done | bytes 18464 | tf_op jit(solution)/shard_map/ppermute | solution.py:262
  108.6 1.3 %shard_map.133 = bf16[4,32,512]{2,1,0:T(8,128)(2,1)} custom-call(bf16[40,576]{1,0:T(8,128)(2,1)S(1)} %get-tuple-element.13.p0, bf16[80,576]{1,0:T(8,128)(2,1)S(1)} %collective-permute-done.1.p13, bf16[80,576]{1,0:T(8,128)(2,1)S(1)} %collective-permute-done.p2, f32[8,576]{1,0:T(8,128)S(1)} %pad_add_fusion.raw_a, f32[8,576]{1,0:T(8,128)S(1)} %collective-permute-done.2.raw_b, ...), custom_call_target="tpu_custom_call" | custom-call | flops 134217728 | bytes 1048576 | tf_op jit(solution)/shard_map/pallas_call | solution.py:145
  109.9 3.7 %all-to-all-start.2 = ((bf16[4,32,512]{2,1,0:T(8,128)(2,1)}), bf16[4,32,512]{2,1,0:T(8,128)(2,1)S(1)}, u32[]{:S(2)}, u32[]{:S(2)}) async-start(bf16[4,32,512]{2,1,0:T(8,128)(2,1)} %shard_map.133), calls=%async_computation.2 | async-start | bytes 262144 | tf_op jit(solution)/shard_map/all_to_all | solution.py:359
  113.7 1.3 %shard_map.134 = bf16[512,128]{1,0:T(8,128)(2,1)} custom-call(bf16[528,128]{1,0:T(8,128)(2,1)S(1)} %get-tuple-element.18.a_ref, bf16[528,128]{1,0:T(8,128)(2,1)S(1)} %collective-permute-done.7.b_ref, bf16[528,128]{1,0:T(8,128)(2,1)S(1)} %collective-permute-done.8.c_ref, bf16[528,128]{1,0:T(8,128)(2,1)S(1)} %collective-permute-done.9.d_ref), custom_call_target="tpu_custom_call" | custom-call | flops 134217728 | bytes 1048576 | tf_op jit(solution)/shard_map/pallas_call | solution.py:145
  115.0 3.5 %all-to-all-done.2.m_ref = bf16[4,32,512]{2,1,0:T(8,128)(2,1)S(1)} async-done(((bf16[4,32,512]{2,1,0:T(8,128)(2,1)}), bf16[4,32,512]{2,1,0:T(8,128)(2,1)S(1)}, u32[]{:S(2)}, u32[]{:S(2)}) %all-to-all-start.2) | async-done | bytes 131104 | tf_op jit(solution)/shard_map/all_to_all | solution.py:359
  118.5 1.0 shard_map.135
  (31 shorter events, 0.2 us)
Async XLA Ops:
  0.6 13.0 %copy-start = (bf16[256,4,576]{0,2,1:T(8,128)(2,1)S(1)}, bf16[256,4,576]{0,2,1:T(8,128)(2,1)}, u32[]{:S(2)}) copy-start(bf16[256,4,576]{0,2,1:T(8,128)(2,1)} %param.17) | copy-start | bytes 3538948
  0.6 1.0 copy-start.4
  1.6 12.0 %copy-start.7 = (s32[256]{0:T(256)S(1)}, s32[256]{0:T(256)}, u32[]{:S(2)}) copy-start(s32[256]{0:T(256)} %param.18) | copy-start | bytes 3076
  2.8 36.7 %all-to-all-start = ((bf16[8,432,128]{2,1,0:T(8,128)(2,1)}), bf16[8,432,128]{2,1,0:T(8,128)(2,1)}, u32[]{:S(2)}, u32[]{:S(2)}) async-start(bf16[8,432,128]{2,1,0:T(8,128)(2,1)} %spread.1), calls=%async_computation | async-start | bytes 1769472 | tf_op jit(solution)/shard_map/all_to_all | solution.py:295
  13.6 41.2 %copy-start.6 = (bf16[4,4,896]{2,1,0:T(4,128)(2,1)S(1)}, bf16[4,4,896]{2,1,0:T(4,128)(2,1)}, u32[]{:S(2)}) copy-start(bf16[4,4,896]{2,1,0:T(4,128)(2,1)} %hid_ref.1) | copy-start | bytes 86020
  14.2 40.6 %copy-start.2 = (bf16[8,128,512]{2,1,0:T(8,128)(2,1)S(1)}, bf16[8,128,512]{2,1,0:T(8,128)(2,1)}, u32[]{:S(2)}) copy-start(bf16[8,128,512]{2,1,0:T(8,128)(2,1)} %wuk_ref.3) | copy-start | bytes 3145732
  14.2 40.6 %copy-start.3 = (bf16[896,576]{0,1:T(8,128)(2,1)S(1)}, bf16[896,576]{0,1:T(8,128)(2,1)}, u32[]{:S(2)}) copy-start(bf16[896,576]{0,1:T(8,128)(2,1)} %param.22) | copy-start | bytes 3096580
  15.1 39.8 %copy-start.5 = (bf16[4,4,8,192]{3,2,1,0:T(8,128)(2,1)S(1)}, bf16[4,4,8,192]{3,2,1,0:T(8,128)(2,1)}, u32[]{:S(2)}) copy-start(bf16[4,4,8,192]{3,2,1,0:T(8,128)(2,1)} %q_ref.1) | copy-start | bytes 147460
  39.4 36.1 %collective-permute-start.6 = (bf16[8,432,128]{2,1,0:T(8,128)(2,1)}, bf16[8,432,128]{2,1,0:T(8,128)(2,1)}, u32[]{:S(2)}, u32[]{:S(2)}) collective-permute-start(bf16[8,432,128]{2,1,0:T(8,128)(2,1)} %all-to-all-done.k1_hbm), channel_id=1, source_target_pairs={{0,8},{8,0},{1,9},{9,1},{2,10},{10,2},{3,11},{11,3},{4,12},{12,4},... | collective-permute-start | bytes 2654216 | tf_op jit(solution)/shard_map/ppermute | solution.py:262
  43.0 17.4 %copy-start.9 = (s32[4]{0:T(128)S(1)}, s32[4]{0:T(128)}, u32[]{:S(2)}) copy-start(s32[4]{0:T(128)} %param.19) | copy-start | bytes 52
  43.0 32.5 %collective-permute-start.5 = (bf16[8,96,128]{2,1,0:T(8,128)(2,1)S(1)}, bf16[8,96,128]{2,1,0:T(8,128)(2,1)}, u32[]{:S(2)}, u32[]{:S(2)}) collective-permute-start(bf16[8,96,128]{2,1,0:T(8,128)(2,1)S(1)} %maximum_maximum_fusion.q0), channel_id=1, source_target_pairs={{0,48},{16,32},{32,16},{48,0},{1,49},{17,33},{33,17},{49,1},{2,50}... | collective-permute-start | bytes 589832 | tf_op jit(solution)/shard_map/ppermute | solution.py:262
  48.9 26.6 %collective-permute-start.4 = (bf16[8,96,128]{2,1,0:T(8,128)(2,1)S(1)}, bf16[8,96,128]{2,1,0:T(8,128)(2,1)}, u32[]{:S(2)}, u32[]{:S(2)}) collective-permute-start(bf16[8,96,128]{2,1,0:T(8,128)(2,1)S(1)} %maximum_maximum_fusion.q0), channel_id=1, source_target_pairs={{0,32},{16,48},{32,0},{48,16},{1,33},{17,49},{33,1},{49,17},{2,34}... | collective-permute-start | bytes 589832 | tf_op jit(solution)/shard_map/ppermute | solution.py:262
  52.4 23.1 %collective-permute-start.3 = (bf16[8,96,128]{2,1,0:T(8,128)(2,1)S(1)}, bf16[8,96,128]{2,1,0:T(8,128)(2,1)}, u32[]{:S(2)}, u32[]{:S(2)}) collective-permute-start(bf16[8,96,128]{2,1,0:T(8,128)(2,1)S(1)} %maximum_maximum_fusion.q0), channel_id=1, source_target_pairs={{0,16},{16,0},{32,48},{48,32},{1,17},{17,1},{33,49},{49,33},{2,18}... | collective-permute-start | bytes 589832 | tf_op jit(solution)/shard_map/ppermute | solution.py:262
  54.8 20.7 %copy-start.1 = (bf16[8,512,128]{2,1,0:T(8,128)(2,1)S(1)}, bf16[8,512,128]{2,1,0:T(8,128)(2,1)}, u32[]{:S(2)}) copy-start(bf16[8,512,128]{2,1,0:T(8,128)(2,1)} %wuv_ref.3) | copy-start | bytes 3145732
  55.7 7.4 %collective-permute-start = (bf16[80,576]{1,0:T(8,128)(2,1)S(1)}, bf16[80,576]{1,0:T(8,128)(2,1)S(1)}, u32[]{:S(2)}, u32[]{:S(2)}) collective-permute-start(bf16[80,576]{1,0:T(8,128)(2,1)S(1)} %get-tuple-element.15), channel_id=1, source_target_pairs={{0,4},{2,6},{4,0},{6,2},{1,5},{3,7},{5,1},{7,3},{8,12},{10,14},{12... | collective-permute-start | bytes 276488 | tf_op jit(solution)/shard_map/ppermute | solution.py:262
  63.1 37.3 %collective-permute-start.1 = (bf16[80,576]{1,0:T(8,128)(2,1)S(1)}, bf16[80,576]{1,0:T(8,128)(2,1)S(1)}, u32[]{:S(2)}, u32[]{:S(2)}) collective-permute-start(bf16[80,576]{1,0:T(8,128)(2,1)S(1)} %pad_maximum_fusion), channel_id=1, source_target_pairs={{0,2},{2,0},{4,6},{6,4},{1,3},{3,1},{5,7},{7,5},{8,10},{10,8},{12,... | collective-permute-start | bytes 276488 | tf_op jit(solution)/shard_map/ppermute | solution.py:262
  66.2 36.5 %all-to-all-start.1 = ((bf16[64,4,576]{2,1,0:T(4,128)(2,1)}), bf16[64,4,576]{2,1,0:T(4,128)(2,1)}, u32[]{:S(2)}, u32[]{:S(2)}) async-start(bf16[64,4,576]{2,1,0:T(4,128)(2,1)} %reshape.17), calls=%async_computation.1 | async-start | bytes 655360 | tf_op jit(solution)/shard_map/all_to_all | solution.py:330
  75.5 24.9 %copy-start.8 = (f32[512]{0:T(512)S(1)}, f32[512]{0:T(512)}, u32[]{:S(2)}) copy-start(f32[512]{0:T(512)} %param.23) | copy-start | bytes 6148
  89.0 24.7 %collective-permute-start.7 = (bf16[528,128]{1,0:T(8,128)(2,1)S(1)}, bf16[528,128]{1,0:T(8,128)(2,1)S(1)}, u32[]{:S(2)}, u32[]{:S(2)}) collective-permute-start(bf16[528,128]{1,0:T(8,128)(2,1)S(1)} %get-tuple-element.19), channel_id=1, source_target_pairs={{0,16},{16,0},{32,48},{48,32},{1,17},{17,1},{33,49},{49,33},{2,18}... | collective-permute-start | bytes 405512 | tf_op jit(solution)/shard_map/ppermute | solution.py:262
  93.1 20.5 %collective-permute-start.8 = (bf16[528,128]{1,0:T(8,128)(2,1)S(1)}, bf16[528,128]{1,0:T(8,128)(2,1)S(1)}, u32[]{:S(2)}, u32[]{:S(2)}) collective-permute-start(bf16[528,128]{1,0:T(8,128)(2,1)S(1)} %get-tuple-element.20), channel_id=1, source_target_pairs={{0,32},{16,48},{32,0},{48,16},{1,33},{17,49},{33,1},{49,17},{2,34}... | collective-permute-start | bytes 405512 | tf_op jit(solution)/shard_map/ppermute | solution.py:262
  98.4 15.3 %collective-permute-start.9 = (bf16[528,128]{1,0:T(8,128)(2,1)S(1)}, bf16[528,128]{1,0:T(8,128)(2,1)S(1)}, u32[]{:S(2)}, u32[]{:S(2)}) collective-permute-start(bf16[528,128]{1,0:T(8,128)(2,1)S(1)} %get-tuple-element.21), channel_id=1, source_target_pairs={{0,48},{16,32},{32,16},{48,0},{1,49},{17,33},{33,17},{49,1},{2,50}... | collective-permute-start | bytes 405512 | tf_op jit(solution)/shard_map/ppermute | solution.py:262
  100.4 8.2 %collective-permute-start.2 = (f32[8,576]{1,0:T(8,128)S(1)}, f32[8,576]{1,0:T(8,128)S(1)}, u32[]{:S(2)}, u32[]{:S(2)}) collective-permute-start(f32[8,576]{1,0:T(8,128)S(1)} %pad_add_fusion.raw_a), channel_id=1, source_target_pairs={{0,1},{1,0},{2,3},{3,2},{4,5},{5,4},{6,7},{7,6},{8,9},{9,8},{10,11... | collective-permute-start | bytes 55304 | tf_op jit(solution)/shard_map/ppermute | solution.py:262
  109.9 8.6 %all-to-all-start.2 = ((bf16[4,32,512]{2,1,0:T(8,128)(2,1)}), bf16[4,32,512]{2,1,0:T(8,128)(2,1)S(1)}, u32[]{:S(2)}, u32[]{:S(2)}) async-start(bf16[4,32,512]{2,1,0:T(8,128)(2,1)} %shard_map.133), calls=%async_computation.2 | async-start | bytes 262144 | tf_op jit(solution)/shard_map/all_to_all | solution.py:359
